TPU v7x, 256 devices: a whole 4x4x8 slice. The times are simulated.
256 devices in a mesh: dp: 8 (over x, z_lo), seq: 32 (over z_hi, y, core).
Axes of the slice: x: 4, y: 4, z: 8 (z_hi: 4, z_lo: 2; z = z_hi * 2 + z_lo), core: 2. Of those that a mesh axis runs over, the one named last changes fastest.
Arguments:
- tower_grad: bfloat16 [8192, 768], P(None, ('dp', 'seq')), may hold values from -6 to 6
- act_mid: bfloat16 [16384, 704], P('seq'), may hold values from -6 to 6
- pre_mid: bfloat16 [16384, 768], P('seq', 'dp'), may hold values from -6 to 6
- act_low: bfloat16 [32768, 640], P('seq'), may hold values from -6 to 6
- pre_low: bfloat16 [32768, 704], P('seq', 'dp'), may hold values from -6 to 6
- weight_upper: bfloat16 [5, 704, 768], P(None, 'seq', 'dp'), may hold values from -0.109375 to 0.109375
- weight_lower: bfloat16 [5, 640, 704], P(None, 'seq', 'dp'), may hold values from -0.109375 to 0.109375
Outputs:
- grad_low_act: bfloat16 [32768, 640], P('seq', 'dp')
- grad_upper: float32 [5, 704, 768], P(None, 'seq', 'dp')
- grad_lower: float32 [5, 640, 704], P(None, 'seq', 'dp')
All inputs are finite; a program needn't handle non-finite values.
Results may differ from a plain program's by a relative error of at most 0.0065.
Values may be sent and summed in bfloat16 or wider, within the bound.
No kernel may reach another device: no remote copies, remote signals or barrier semaphores. Data moves between devices by JAX's collectives and lax.ppermute only.
A program may use at most 64 MiB of HBM per device.

v0:
```python
import math

import jax
import jax.numpy as jnp
from jax import lax
from jax.sharding import PartitionSpec as P

KWIDTH = 5


def with_halo(block, sides, width):
    for axis, dim in sides:
        count = lax.axis_size(axis)
        forward = [(i, i + 1) for i in range(count - 1)]
        backward = [(target, source) for source, target in forward]
        low = lax.ppermute(
            lax.slice_in_dim(block, block.shape[dim] - width, None, axis=dim), axis, forward
        )
        high = lax.ppermute(lax.slice_in_dim(block, 0, width, axis=dim), axis, backward)
        block = jnp.concatenate([low, block, high], axis=dim)
    return block


def gelu_slope(pre_act):
    values = pre_act.astype(jnp.float32)
    cumulative = 0.5 * (1.0 + lax.erf(values * (1.0 / math.sqrt(2.0))))
    density = jnp.exp(-0.5 * values * values) * (1.0 / math.sqrt(2.0 * math.pi))
    return cumulative + values * density


def level_back(upper_grad, act, pre_act, weight):
    rows = act.shape[0]
    half = KWIDTH // 2
    spread = jnp.repeat(upper_grad.astype(jnp.float32), 2, axis=0) * 0.5
    pre_grad = (spread * gelu_slope(pre_act)).astype(jnp.bfloat16)
    padded = with_halo(pre_grad, (("seq", 0),), half)
    act_grad = jnp.zeros((rows, weight.shape[1]), jnp.float32)
    pieces = []
    for offset in range(KWIDTH):
        begin = 2 * half - offset
        shifted = padded[begin : begin + rows]
        pieces.append(jnp.einsum("si,so->io", act, shifted, preferred_element_type=jnp.float32))
        act_grad = act_grad + jnp.einsum(
            "so,io->si", shifted, weight[offset], preferred_element_type=jnp.float32
        )
    return (act_grad, jnp.stack(pieces))


def local(tower_grad, act_mid, pre_mid, act_low, pre_low, weight_upper, weight_lower):
    upper_full, lower_full = (
        lax.all_gather(weight_upper, "seq", axis=1, tiled=True),
        lax.all_gather(weight_lower, "seq", axis=1, tiled=True),
    )
    slab_grad = lax.all_to_all(tower_grad, "seq", split_axis=0, concat_axis=1, tiled=True)
    mid_part, upper_part = level_back(slab_grad, act_mid, pre_mid, upper_full)
    mid_total = act_mid.shape[0] * lax.axis_size("seq")
    low_total = act_low.shape[0] * lax.axis_size("seq")
    upper_term = upper_part * (1.0 / math.sqrt(mid_total))
    mid_summed = lax.psum(mid_part, "dp")
    share_width = pre_low.shape[1]
    mid_own = lax.dynamic_slice_in_dim(
        mid_summed, lax.axis_index("dp") * share_width, share_width, 1
    )
    low_part, lower_part = level_back(mid_own.astype(jnp.bfloat16), act_low, pre_low, lower_full)
    lower_term = lower_part * (1.0 / math.sqrt(low_total))
    grad_upper, grad_lower = (
        lax.psum_scatter(upper_term, "seq", scatter_dimension=1, tiled=True),
        lax.psum_scatter(lower_term, "seq", scatter_dimension=1, tiled=True),
    )
    low_grad = lax.psum_scatter(low_part, "dp", scatter_dimension=1, tiled=True)
    return (low_grad.astype(jnp.bfloat16), grad_upper, grad_lower)


def solution(mesh):
    in_specs = (
        P(None, ("dp", "seq")),
        P("seq", None),
        P("seq", "dp"),
        P("seq", None),
        P("seq", "dp"),
        P(None, "seq", "dp"),
        P(None, "seq", "dp"),
    )
    out_specs = (P("seq", "dp"), P(None, "seq", "dp"), P(None, "seq", "dp"))
    return jax.shard_map(local, mesh=mesh, in_specs=in_specs, out_specs=out_specs, check_vma=False)
```

profile of v0, /device:TPU:8, one launch (start us, length us, event | category | flops | bytes accessed | tf_op | source)
XLA Modules:
  0.0 442.3 jit_solution(7031288359553033006)
XLA Ops:
  7.2 11.9 %all-to-all-start = ((bf16[32,256,3]{1,2,0:T(4,128)(2,1)}), bf16[32,256,3]{1,2,0:T(4,128)(2,1)}, u32[]{:S(2)}, u32[]{:S(2)}) async-start(bf16[32,256,3]{1,2,0:T(4,128)(2,1)} %bitcast.113), calls=%async_computation | async-start | bytes 131072 | tf_op jit(solution)/shard_map/all_to_all | solution.py:54
  19.1 0.8 copy.33
  19.9 46.2 %all_gather.6 = bf16[5,704,96]{2,0,1:T(8,128)(2,1)S(1)} all-gather(bf16[5,22,96]{2,0,1:T(8,128)(2,1)S(1)} %copy.33), channel_id=1, replica_groups=mesh['dp'=8,'seq'=32] {'seq'}, dimensions={1}, use_global_device_ids=true | all-gather | bytes 696960 | tf_op jit(solution)/shard_map/all_gather | solution.py:51
  66.1 1.3 fusion.66
  67.4 0.8 copy.32
  68.2 1.1 copy.40
  69.3 0.8 copy.54
  70.1 0.8 copy.53
  70.9 0.8 copy.52
  71.7 0.8 copy.51
  72.5 0.8 copy.55
  73.3 0.9 multiply_bitcast_fusion
  74.6 6.6 %collective-permute-start = (bf16[2,96]{1,0:T(2,128)(2,1)S(1)}, bf16[2,96]{1,0:T(2,128)(2,1)S(1)}, u32[]{:S(2)}, u32[]{:S(2)}) collective-permute-start(bf16[2,96]{1,0:T(2,128)(2,1)S(1)} %get-tuple-element.27), channel_id=1, source_target_pairs={{1,0},{2,1},{3,2},{4,3},{5,4},{6,5},{7,6},{8,7},{9,8},{10,9},{11,1... | collective-permute-start | bytes 1160 | tf_op jit(solution)/shard_map/ppermute | solution.py:19
  81.2 1.9 collective-permute-start.1
  83.1 0.4 fusion.35
  83.5 2.5 collective-permute-done.1
  86.1 0.4 fusion.32
  86.5 0.4 fusion.37
  87.0 0.4 fusion.1
  87.4 0.4 fusion
  87.8 77.5 %all-reduce.1 = bf16[512,704]{0,1:T(8,128)(2,1)} all-reduce(f32[512,704]{0,1:T(8,128)S(1)} %fusion), channel_id=1, replica_groups=mesh['dp'=8,'seq'=32] {'dp'}, use_global_device_ids=true, to_apply=%region_0.0 | all-reduce | flops 360448 | bytes 2162688 | tf_op jit(solution)/shard_map/psum | solution.py:59
  165.3 0.9 convert_multiply_fusion.8
  166.8 1.9 collective-permute-start.2
  168.8 2.4 collective-permute-start.3
  171.2 0.4 fusion.11
  171.6 0.4 fusion.10
  172.3 1.3 collective-permute-done.3
  173.6 0.4 fusion.8
  174.0 0.4 fusion.7
  174.5 2.2 copy.48
  176.8 44.6 %all_gather.7 = bf16[5,640,88]{2,0,1:T(8,128)(2,1)} all-gather(bf16[5,20,88]{2,0,1:T(8,128)(2,1)S(1)} %copy.41), channel_id=1, replica_groups=mesh['dp'=8,'seq'=32] {'seq'}, dimensions={1}, use_global_device_ids=true | all-gather | bytes 580800 | tf_op jit(solution)/shard_map/all_gather | solution.py:52
  223.3 2.2 copy.47
  225.8 1.1 copy-done.2
  226.8 2.1 fusion.67
  228.9 1.1 copy.60
  230.1 1.1 copy.59
  231.2 1.1 copy.58
  232.7 0.6 fusion.45
  233.3 0.5 fusion.43
  233.8 0.5 fusion.30
  234.4 0.5 fusion.48
  234.9 2.2 add_add_fusion
  237.2 34.6 %reduce-scatter.8.cloned.1.call-done = f32[5,20,88]{2,0,1:T(8,128)} async-done(((f32[5,640,88]{2,0,1:T(8,128)}), f32[5,20,88]{2,0,1:T(8,128)}) %reduce-scatter.8.cloned.1.call-update) | async-done | bytes 35216 | tf_op jit(solution)/shard_map/reduce_scatter | solution.py:68
  271.7 1.5 copy.50
  273.3 95.0 %reduce-scatter.6.cloned.1.call-done = f32[5,22,96]{2,0,1:T(8,128)} async-done(((f32[5,704,96]{2,0,1:T(8,128)}), f32[5,22,96]{2,0,1:T(8,128)}) %reduce-scatter.6.cloned.1.call-update) | async-done | bytes 42256 | tf_op jit(solution)/shard_map/reduce_scatter | solution.py:67
  368.3 1.5 copy.49
  369.8 64.3 %reduce-scatter.4.cloned.1.call-done = f32[1024,80]{0,1:T(8,128)} async-done(((f32[1024,640]{0,1:T(8,128)}), f32[1024,80]{0,1:T(8,128)}) %reduce-scatter.4.cloned.1.call-update) | async-done | bytes 327696 | tf_op jit(solution)/shard_map/reduce_scatter | solution.py:70
  434.1 1.7 convert_element_type.33
  (48 shorter events, 4.2 us)
Async XLA Ops:
  7.2 164.0 %copy-start = (bf16[1024,640]{1,0:T(8,128)(2,1)S(1)}, bf16[1024,640]{1,0:T(8,128)(2,1)}, u32[]{:S(2)}) copy-start(bf16[1024,640]{1,0:T(8,128)(2,1)} %param.10) | copy-start | bytes 3932164
  7.2 66.2 %all-to-all-start = ((bf16[32,256,3]{1,2,0:T(4,128)(2,1)}), bf16[32,256,3]{1,2,0:T(4,128)(2,1)}, u32[]{:S(2)}, u32[]{:S(2)}) async-start(bf16[32,256,3]{1,2,0:T(4,128)(2,1)} %bitcast.113), calls=%async_computation | async-start | bytes 131072 | tf_op jit(solution)/shard_map/all_to_all | solution.py:54
  19.1 252.7 %reduce-scatter.8.cloned.1.call-start = ((), (), s32[]{:S(2)}) async-start(), calls=%async_computation.6 | async-start | bytes 2703360 | tf_op jit(solution)/shard_map/reduce_scatter | solution.py:68
  66.1 1.3 copy-start.4
  70.1 4.4 copy-start.3
  74.6 11.8 %collective-permute-start = (bf16[2,96]{1,0:T(2,128)(2,1)S(1)}, bf16[2,96]{1,0:T(2,128)(2,1)S(1)}, u32[]{:S(2)}, u32[]{:S(2)}) collective-permute-start(bf16[2,96]{1,0:T(2,128)(2,1)S(1)} %get-tuple-element.27), channel_id=1, source_target_pairs={{1,0},{2,1},{3,2},{4,3},{5,4},{6,5},{7,6},{8,7},{9,8},{10,9},{11,1... | collective-permute-start | bytes 1160 | tf_op jit(solution)/shard_map/ppermute | solution.py:19
  81.2 4.9 %collective-permute-start.1 = (bf16[2,96]{1,0:T(2,128)(2,1)S(1)}, bf16[2,96]{1,0:T(2,128)(2,1)S(1)}, u32[]{:S(2)}, u32[]{:S(2)}) collective-permute-start(bf16[2,96]{1,0:T(2,128)(2,1)S(1)} %get-tuple-element.28), channel_id=1, source_target_pairs={{0,1},{1,2},{2,3},{3,4},{4,5},{5,6},{6,7},{7,8},{8,9},{9,10},{10,1... | collective-permute-start | bytes 1160 | tf_op jit(solution)/shard_map/ppermute | solution.py:16
  86.1 1.3 copy-start.6
  86.5 0.5 copy-start.8
  165.3 3.4 copy-start.5
  166.8 4.4 collective-permute-start.2
  168.8 4.9 %collective-permute-start.3 = (bf16[2,88]{1,0:T(2,128)(2,1)S(1)}, bf16[2,88]{1,0:T(2,128)(2,1)S(1)}, u32[]{:S(2)}, u32[]{:S(2)}) collective-permute-start(bf16[2,88]{1,0:T(2,128)(2,1)S(1)} %get-tuple-element.26), channel_id=1, source_target_pairs={{0,1},{1,2},{2,3},{3,4},{4,5},{5,6},{6,7},{7,8},{8,9},{9,10},{10,1... | collective-permute-start | bytes 1064 | tf_op jit(solution)/shard_map/ppermute | solution.py:16
  176.7 44.6 %copy-start.1 = (bf16[512,704]{0,1:T(8,128)(2,1)S(1)}, bf16[512,704]{0,1:T(8,128)(2,1)}, u32[]{:S(2)}) copy-start(bf16[512,704]{0,1:T(8,128)(2,1)} %param.8) | copy-start | bytes 2162692
  176.7 44.6 %copy-start.9 = (bf16[2,96]{1,0:T(2,128)(2,1)S(1)}, bf16[2,96]{1,0:T(2,128)(2,1)}, u32[]{:S(2)}) copy-start(bf16[2,96]{1,0:T(2,128)(2,1)} %copy-done.8) | copy-start | bytes 1156
  176.7 191.6 %reduce-scatter.6.cloned.1.call-start = ((), (), s32[]{:S(2)}) async-start(), calls=%async_computation.5 | async-start | bytes 2973696 | tf_op jit(solution)/shard_map/reduce_scatter | solution.py:67
  221.3 1.1 copy-start.7
  225.5 1.3 copy-start.2
  225.5 208.6 %reduce-scatter.4.cloned.1.call-start = ((), (), s32[]{:S(2)}) async-start(), calls=%async_computation.4 | async-start | bytes 2949120 | tf_op jit(solution)/shard_map/reduce_scatter | solution.py:70
Sparse Core Ops, SparseCore 0:
  176.8 94.8 reduce-scatter.7
  276.1 92.0 reduce-scatter.5
  370.8 63.2 reduce-scatter.3
where the time goes:
time: 444 us; the launch traced here: 442 us
  waiting for transfers between devices  198 us (45%)
  blocking collectives  168 us (38%)
  starting transfers between devices  25 us (6%)
  local copies, waits for them, and re-layouts  23 us (5%)
  between operations  14.1 us (3%)
  matrix products  10 us (2%)
    reduce_scatter x1, waiting for transfers between devices, local(): lax.psum_scatter(upper_term, 'seq', scatter_dimension=1, tiled=True)  95 us
    psum x1, blocking collectives, local(): mid_summed = lax.psum(mid_part, 'dp')  77.5 us
    reduce_scatter x1, waiting for transfers between devices, local(): low_grad = lax.psum_scatter(low_part, 'dp', scatter_dimension=1, tiled=True)  64.3 us
    all_gather x1, blocking collectives, local(): lax.all_gather(weight_upper, 'seq', axis=1, tiled=True)  46.2 us
    all_gather x1, blocking collectives, local(): lax.all_gather(weight_lower, 'seq', axis=1, tiled=True)  44.6 us
    reduce_scatter x1, waiting for transfers between devices, local(): lax.psum_scatter(lower_term, 'seq', scatter_dimension=1, tiled=True)  34.6 us
    unnamed x36, local copies, waits for them, and re-layouts  14.7 us
    all_to_all x1, starting transfers between devices, local(): lax.all_to_all(tower_grad, 'seq', split_axis=0, concat_axis=1, tiled=True)  11.9 us
  transfers between devices with their start and end apart: 8, of which 5 were waited for; matrix products, arithmetic and copies ran while one was open for 6% of the time, Pallas kernels for 0%

commit v1 on v0

v1 whole, which is shorter than its diff:
```python
import math

import jax
import jax.numpy as jnp
from jax import lax
from jax.experimental import pallas as pl
from jax.experimental.pallas import tpu as pltpu
from jax.sharding import Mesh, PartitionSpec as P

KWIDTH = 5
HALF = 2
DP = ("x", "zl")
SEQ = ("zh", "y", "c")
NZ, NY, NC = 4, 4, 2
BF = jnp.bfloat16
F32 = jnp.float32
PARAMS = pltpu.CompilerParams(vmem_limit_bytes=40 * 1024 * 1024)
VMEM = pl.BlockSpec(memory_space=pltpu.VMEM)
SMEM = pl.BlockSpec(memory_space=pltpu.SMEM)


def half_slope(pre_act):
    values = pre_act.astype(F32)
    cumulative = 0.5 * (1.0 + lax.erf(values * (1.0 / math.sqrt(2.0))))
    density = jnp.exp(-0.5 * values * values) * (1.0 / math.sqrt(2.0 * math.pi))
    return 0.5 * (cumulative + values * density)


def shifted(block, axis, count, step):
    return lax.ppermute(block, axis, [(i, (i + step) % count) for i in range(count)])


def gather_rows(block):
    level = jnp.stack([block] + [shifted(block, "zh", NZ, s) for s in range(1, NZ)])
    level = jnp.concatenate([level] + [shifted(level, "y", NY, s) for s in range(1, NY)])
    return level, shifted(level, "c", NC, 1)


def scatter_rows(keep, send):
    total = keep + shifted(send, "c", NC, 1).astype(F32)
    parts = [shifted(total[s].astype(BF), "y", NY, s) for s in range(1, NY)]
    total = total[0] + sum(p.astype(F32) for p in parts)
    parts = [shifted(total[s].astype(BF), "zh", NZ, s) for s in range(1, NZ)]
    return total[0] + sum(p.astype(F32) for p in parts)


def source_slot(q, pos):
    zh, y = q // (NY * NC), (q // NC) % NY
    return lax.rem(pos[1] - y + NY, NY) * NZ + lax.rem(pos[0] - zh + NZ, NZ)


def block_of(q, pos, own_ref, other_ref):
    slot = source_slot(q, pos)
    mine = own_ref[slot].astype(F32)
    theirs = other_ref[slot].astype(F32)
    return jnp.where(pos[2] == q % NC, mine, theirs)


def doubling():
    row = lax.broadcasted_iota(jnp.int32, (128, 256), 0)
    col = lax.broadcasted_iota(jnp.int32, (128, 256), 1)
    return (row == lax.shift_right_logical(col, 1)).astype(F32).astype(BF)


def mm(a, b):
    return jnp.dot(a, b, preferred_element_type=F32)


def upper_kernel(pos_ref, tower_ref, slope_ref, own_ref, other_ref, mid_ref, taps_ref, main_ref, edge_ref, w_ref):
    pos = (pos_ref[0], pos_ref[1], pos_ref[2])
    for q in range(32):
        rows = tower_ref[q].astype(F32)
        main_ref[3 * q : 3 * q + 3, :] = rows[0:3]
        edge_ref[3 * q : 3 * q + 3, :] = rows[3:6]
    for pair in range(16):
        both = [block_of(2 * pair + j, pos, own_ref, other_ref) for j in range(2)]
        w_ref[48 * pair : 48 * pair + 48, :] = jnp.concatenate(both, axis=0).astype(BF)
    spread = doubling()
    main = main_ref[...].astype(BF)
    edge = edge_ref[...].astype(BF)
    grad = jnp.concatenate(
        [
            mm(edge[:, :128], spread)[:, 128:],
            mm(main[:, :128], spread),
            mm(main[:, 128:], spread),
            mm(edge[:, 128:], spread)[:, :128],
        ],
        axis=1,
    )
    grad = grad * slope_ref[...]
    lane = lax.broadcasted_iota(jnp.int32, (96, 128), 1)
    for k in range(KWIDTH):
        moved = pltpu.roll(grad, 768 - (130 - k), 1)
        outer = jnp.where(lane == 127, moved[:, 640:768], moved[:, 512:640])
        taps_ref[96 * k : 96 * k + 96, 0:512] = moved[:, 0:512].astype(BF)
        taps_ref[96 * k : 96 * k + 96, 512:640] = outer.astype(BF)
    taps = taps_ref[...]
    for d in range(8):
        mid_ref[d] = mm(w_ref[96 * d : 96 * d + 96, :], taps).astype(BF)


def lower_weight_kernel(pos_ref, own_ref, other_ref, out_ref, rows_ref):
    pos = (pos_ref[0], pos_ref[1], pos_ref[2])
    for q in range(32):
        rows_ref[20 * q : 20 * q + 24, :] = block_of(q, pos, own_ref, other_ref)
    out_ref[...] = rows_ref[0:640, :].astype(BF)


def lower_kernel(pos_ref, mid_ref, slope_ref, w_ref, low_ref, taps_ref):
    place = pos_ref[0] * (NY * NC) + pos_ref[1] * NC + pos_ref[2]
    total = mid_ref[0].astype(F32)
    for d in range(1, 8):
        total = total + mid_ref[d].astype(F32)
    mid = total.astype(BF)
    ends = mid[:, 512:640].astype(F32)
    left = jnp.broadcast_to(jnp.where(place == 0, 0.0, ends[:, 127:128]), (96, 128))
    right = jnp.broadcast_to(jnp.where(place == 31, 0.0, ends[:, 0:1]), (96, 128))
    spread = doubling()
    grad = jnp.concatenate(
        [left] + [mm(mid[:, 128 * j : 128 * j + 128], spread) for j in range(4)] + [right], axis=1
    )
    grad = grad * slope_ref[...]
    for k in range(KWIDTH):
        moved = pltpu.roll(grad, 1280 - (130 - k), 1)
        taps_ref[96 * k : 96 * k + 96, :] = moved[:, 0:1024].astype(BF)
    taps = taps_ref[...]
    for d in range(8):
        low_ref[d] = mm(w_ref[80 * d : 80 * d + 80, :], taps).astype(BF)


def weight_grad_kernel(pos_ref, act_ref, taps_ref, keep_ref, send_ref, rows_ref, block_ref):
    channels, count = act_ref.shape
    width = channels // 32
    rows_ref[channels:, :] = jnp.zeros((8, rows_ref.shape[1]), F32)
    rows_ref[0:channels, :] = lax.dot_general(
        act_ref[...], taps_ref[:, 0:count], (((1,), (1,)), ((), ())), preferred_element_type=F32
    )
    for q in range(32):
        block_ref[q] = rows_ref[width * q : width * q + 24, :]
    for ry in range(NY):
        for rz in range(NZ):
            zh = lax.rem(pos_ref[0] + rz, NZ)
            y = lax.rem(pos_ref[1] + ry, NY)
            base = (zh * NY + y) * NC
            keep_ref[ry, rz] = block_ref[base + pos_ref[2]]
            send_ref[ry, rz] = block_ref[base + 1 - pos_ref[2]].astype(BF)


def weight_grad(pos, act, taps):
    block = (NY, NZ, 24, taps.shape[0])
    return pl.pallas_call(
        weight_grad_kernel,
        out_shape=(jax.ShapeDtypeStruct(block, F32), jax.ShapeDtypeStruct(block, BF)),
        in_specs=[SMEM, VMEM, VMEM],
        out_specs=(VMEM, VMEM),
        scratch_shapes=[pltpu.VMEM((act.shape[0] + 8, taps.shape[0]), F32), pltpu.VMEM((32, 24, taps.shape[0]), F32)],
        compiler_params=PARAMS,
        name="weight_grad",
    )(pos, act, taps)


def neighbours(block):
    count = NZ * NY * NC
    forward = [(i, i + 1) for i in range(count - 1)]
    backward = [(i + 1, i) for i in range(count - 1)]
    low = lax.ppermute(block[:, :, -128:], SEQ, forward)
    high = lax.ppermute(block[:, :, :128], SEQ, backward)
    return low, high


def local(tower_grad, act_mid, pre_mid, act_low, pre_low, weight_upper, weight_lower):
    pos = jnp.stack([lax.axis_index("zh"), lax.axis_index("y"), lax.axis_index("c")]).astype(jnp.int32)
    tower = tower_grad.T.reshape(3, 32, 256)
    blank = jnp.zeros((3, 1, 128), BF)
    before = jnp.concatenate([blank, tower[:, :-1, 128:]], axis=1)
    after = jnp.concatenate([tower[:, 1:, :128], blank], axis=1)
    windows = jnp.concatenate([tower, jnp.concatenate([before, after], axis=2)], axis=0)
    tower_rows = lax.all_to_all(windows.transpose(1, 0, 2), SEQ, split_axis=0, concat_axis=0, tiled=True)

    upper = jnp.pad(weight_upper.transpose(1, 0, 2).reshape(22, 480), ((0, 2), (0, 0)))
    lower = jnp.pad(weight_lower.reshape(5, 20, 4, 22), ((0, 0), (0, 4), (0, 0), (0, 2)))
    lower = lower.transpose(1, 0, 2, 3).reshape(24, 480)
    upper_own, upper_other = gather_rows(upper)
    lower_own, lower_other = gather_rows(lower)

    pre_upper = pre_mid.T
    pre_lower = jnp.pad(pre_low.T.reshape(4, 22, 1024), ((0, 0), (0, 2), (0, 0))).reshape(96, 1024)
    edges = jnp.stack(
        [
            jnp.concatenate([pre_upper[:, :128], pre_upper[:, -128:]], axis=1),
            jnp.concatenate([pre_lower[:, :128], pre_lower[:, -128:]], axis=1),
        ]
    )
    low_side, high_side = neighbours(edges)
    slope_upper = half_slope(jnp.concatenate([low_side[0], pre_upper, high_side[0]], axis=1))
    slope_lower = half_slope(jnp.concatenate([low_side[1], pre_lower, high_side[1]], axis=1))

    mid_part, upper_taps = pl.pallas_call(
        upper_kernel,
        out_shape=(jax.ShapeDtypeStruct((8, 96, 640), BF), jax.ShapeDtypeStruct((480, 640), BF)),
        in_specs=[SMEM] + [VMEM] * 4,
        out_specs=(VMEM, VMEM),
        scratch_shapes=[pltpu.VMEM((96, 256), F32), pltpu.VMEM((96, 256), F32), pltpu.VMEM((768, 480), BF)],
        compiler_params=PARAMS,
        name="upper",
    )(pos, tower_rows, slope_upper, upper_own.reshape(16, 24, 480), upper_other.reshape(16, 24, 480))
    mid_parts = lax.all_to_all(mid_part, DP, split_axis=0, concat_axis=0, tiled=True)

    upper_sum = scatter_rows(*weight_grad(pos, act_mid.T, upper_taps))
    lower_full = pl.pallas_call(
        lower_weight_kernel,
        out_shape=jax.ShapeDtypeStruct((640, 480), BF),
        in_specs=[SMEM] + [VMEM] * 2,
        out_specs=VMEM,
        scratch_shapes=[pltpu.VMEM((648, 480), F32)],
        compiler_params=PARAMS,
        name="lower_weight",
    )(pos, lower_own.reshape(16, 24, 480), lower_other.reshape(16, 24, 480))

    low_part, lower_taps = pl.pallas_call(
        lower_kernel,
        out_shape=(jax.ShapeDtypeStruct((8, 80, 1024), BF), jax.ShapeDtypeStruct((480, 1024), BF)),
        in_specs=[SMEM] + [VMEM] * 3,
        out_specs=(VMEM, VMEM),
        compiler_params=PARAMS,
        name="lower",
    )(pos, mid_parts, slope_lower, lower_full)
    low_parts = lax.all_to_all(low_part, DP, split_axis=0, concat_axis=0, tiled=True)
    lower_sum = scatter_rows(*weight_grad(pos, act_low.T, lower_taps))

    low_grad = jnp.sum(low_parts.astype(F32), axis=0).astype(BF).T
    mid_total = act_mid.shape[0] * NZ * NY * NC
    low_total = act_low.shape[0] * NZ * NY * NC
    grad_upper = upper_sum[:22].reshape(22, 5, 96).transpose(1, 0, 2) * (1.0 / math.sqrt(mid_total))
    grad_lower = lower_sum[:20].reshape(20, 5, 4, 24)[:, :, :, :22].reshape(20, 5, 88)
    grad_lower = grad_lower.transpose(1, 0, 2) * (1.0 / math.sqrt(low_total))
    return low_grad, grad_upper, grad_lower


def solution(mesh):
    fine = Mesh(mesh.devices.reshape(4, 2, NZ, NY, NC), DP + SEQ)
    in_specs = (
        P(None, DP + SEQ),
        P(SEQ, None),
        P(SEQ, DP),
        P(SEQ, None),
        P(SEQ, DP),
        P(None, SEQ, DP),
        P(None, SEQ, DP),
    )
    out_specs = (P(SEQ, DP), P(None, SEQ, DP), P(None, SEQ, DP))
    return jax.shard_map(local, mesh=fine, in_specs=in_specs, out_specs=out_specs, check_vma=False)
```

time: 444 us -> 141 us (0.32)
  blocking collectives: 168 us -> 0 us
  waiting for transfers between devices: 198 us -> 31.8 us
  starting transfers between devices: 25 us -> 76.2 us
  between operations: 14.1 us -> 1.15 us
  matrix products: 10 us -> 0 us
  Pallas kernels: 0 us -> 8.72 us
  local copies, waits for them, and re-layouts: 23 us -> 15.4 us
    reduce_scatter x3 -> x0, waiting for transfers between devices: 194 us -> none  [the longest x1 95 us: local(): lax.psum_scatter(upper_term, 'seq', scatter_dimension=1, tiled=True)]
    all_gather x2 -> x0, blocking collectives: 90.7 us -> none  [the longest x1 46.2 us: local(): lax.all_gather(weight_upper, 'seq', axis=1, tiled=True)]
    psum x1 -> x0, blocking collectives: 77.5 us -> none  [local(): mid_summed = lax.psum(mid_part, 'dp')]
    ppermute x4 -> x30, starting transfers between devices: 12.8 us -> 57 us  [the longest x28 51.4 us: shifted(): lax.ppermute(block, axis, [(i, (i + step) % count) for i in range(count)])]
    ppermute x4 -> x30, waiting for transfers between devices: 3.84 us -> 31.8 us  [the longest x28 31.8 us: shifted(): lax.ppermute(block, axis, [(i, (i + step) % count) for i in range(count)])]
    dot_general x20 -> x0, matrix products: 10 us -> none  [the longest x10 6.33 us: level_back(): jnp.einsum('so,io->si', shifted, weight[offset], preferred_element_type=j...]
    pallas_call x0 -> x5, Pallas kernels: none -> 8.72 us  [the longest x2 2.85 us: weight_grad(): pl.pallas_call(weight_grad_kernel, out_shape=(jax.ShapeDtypeStruct(block,...]
    all_to_all x1 -> x3, starting transfers between devices: 11.9 us -> 19.3 us  [the longest x1 8.55 us: local(): lax.all_to_all(windows.transpose(1, 0, 2), SEQ, split_axis=0, concat_axis...]
  transfers between devices with their start and end apart: 8 -> 33, of which waited for: 5 -> 9; matrix products, arithmetic and copies ran while one was open for 6% -> 9% of each run, Pallas kernels for 0% -> 5%
where the time goes in v1:
time: 141 us; the launch traced here: 139 us
  starting transfers between devices  76.2 us (54%)
  waiting for transfers between devices  31.8 us (23%)
  local copies, waits for them, and re-layouts  15.4 us (11%)
  Pallas kernels  8.72 us (6%)
  other arithmetic  6.13 us (4%)
    ppermute x28, starting transfers between devices, shifted(): lax.ppermute(block, axis, [(i, (i + step) % count) for i in range(count)])  51.4 us
    ppermute x28, waiting for transfers between devices, shifted(): lax.ppermute(block, axis, [(i, (i + step) % count) for i in range(count)])  31.8 us
    unnamed x38, local copies, waits for them, and re-layouts  9.63 us
    all_to_all x1, starting transfers between devices, local(): lax.all_to_all(windows.transpose(1, 0, 2), SEQ, split_axis=0, concat_axis...  8.55 us
    all_to_all x1, starting transfers between devices, local(): lax.all_to_all(low_part, DP, split_axis=0, concat_axis=0, tiled=True)  5.83 us
    all_to_all x1, starting transfers between devices, local(): lax.all_to_all(mid_part, DP, split_axis=0, concat_axis=0, tiled=True)  4.88 us
    ppermute x1, starting transfers between devices, neighbours(): high = lax.ppermute(block[:, :, :128], SEQ, backward)  3.64 us
    pallas_call x2, Pallas kernels, weight_grad(): pl.pallas_call(weight_grad_kernel, out_shape=(jax.ShapeDtypeStruct(block,...  2.85 us
  transfers between devices with their start and end apart: 33, of which 9 were waited for; matrix products, arithmetic and copies ran while one was open for 9% of the time, Pallas kernels for 5%

profile of v1, /device:TPU:8, one launch (start us, length us, event | category | flops | bytes accessed | tf_op | source)
XLA Modules:
  0.0 139.4 jit_solution(10581811336881758367)
XLA Ops:
  1.6 7.3 %collective-permute-start.3 = (bf16[24,480]{1,0:T(8,128)(2,1)S(1)}, bf16[24,480]{1,0:T(8,128)(2,1)S(1)}, u32[]{:S(2)}, u32[]{:S(2)}) collective-permute-start(bf16[24,480]{1,0:T(8,128)(2,1)S(1)} %get-tuple-element.55), channel_id=1, source_target_pairs={{0,16},{8,24},{16,0},{24,8},{1,17},{9,25},{17,1},{25,9},{2,18},{10... | collective-permute-start | bytes 69128 | tf_op jit(solution)/shard_map/ppermute | solution.py:30
  8.8 1.5 %collective-permute-start.2 = (bf16[24,480]{1,0:T(8,128)(2,1)S(1)}, bf16[24,480]{1,0:T(8,128)(2,1)S(1)}, u32[]{:S(2)}, u32[]{:S(2)}) collective-permute-start(bf16[24,480]{1,0:T(8,128)(2,1)S(1)} %get-tuple-element.55), channel_id=1, source_target_pairs={{0,8},{8,16},{16,24},{24,0},{1,9},{9,17},{17,25},{25,1},{2,10},{10... | collective-permute-start | bytes 69128 | tf_op jit(solution)/shard_map/ppermute | solution.py:30
  10.3 0.9 reshape.49
  11.4 2.7 %collective-permute-start.11 = (bf16[24,480]{1,0:T(8,128)(2,1)S(1)}, bf16[24,480]{1,0:T(8,128)(2,1)S(1)}, u32[]{:S(2)}, u32[]{:S(2)}) collective-permute-start(bf16[24,480]{1,0:T(8,128)(2,1)S(1)} %reshape.50), channel_id=1, source_target_pairs={{0,24},{8,0},{16,8},{24,16},{1,25},{9,1},{17,9},{25,17},{2,26},{10... | collective-permute-start | bytes 69128 | tf_op jit(solution)/shard_map/ppermute | solution.py:30
  14.2 0.9 collective-permute-start.10
  15.1 1.5 %collective-permute-start.9 = (bf16[24,480]{1,0:T(8,128)(2,1)S(1)}, bf16[24,480]{1,0:T(8,128)(2,1)S(1)}, u32[]{:S(2)}, u32[]{:S(2)}) collective-permute-start(bf16[24,480]{1,0:T(8,128)(2,1)S(1)} %reshape.50), channel_id=1, source_target_pairs={{0,8},{8,16},{16,24},{24,0},{1,9},{9,17},{17,25},{25,1},{2,10},{10... | collective-permute-start | bytes 69128 | tf_op jit(solution)/shard_map/ppermute | solution.py:30
  17.4 1.6 %fusion.24 = bf16[32,6,256]{2,1,0:T(8,128)(2,1)} fusion(bf16[3,31,128]{2,0,1:T(4,128)(2,1)S(1)} %get-tuple-element.49, bf16[3,31,128]{2,0,1:T(4,128)(2,1)S(1)} %get-tuple-element.48, bf16[3,32,256]{2,0,1:T(4,128)(2,1)} %bitcast.92), kind=kLoop, calls=%fused_computation.40 | loop fusion | flops 737280 | bytes 195072 | tf_op jit(solution)/shard_map/transpose | solution.py:178
  19.0 8.5 %all-to-all-start = ((bf16[32,6,256]{2,1,0:T(8,128)(2,1)}), bf16[32,6,256]{2,1,0:T(8,128)(2,1)S(1)}, u32[]{:S(2)}, u32[]{:S(2)}) async-start(bf16[32,6,256]{2,1,0:T(8,128)(2,1)} %fusion.24), calls=%async_computation | async-start | bytes 262144 | tf_op jit(solution)/shard_map/all_to_all | solution.py:178
  28.6 1.6 %copy.17 = bf16[1024,640]{0,1:T(8,128)(2,1)S(1)} copy(bf16[1024,640]{1,0:T(8,128)(2,1)} %param.10) | data formatting | bytes 2621440 | tf_op args[3]
  30.2 3.7 %collective-permute-start.4 = (bf16[24,480]{1,0:T(8,128)(2,1)S(1)}, bf16[24,480]{1,0:T(8,128)(2,1)S(1)}, u32[]{:S(2)}, u32[]{:S(2)}) collective-permute-start(bf16[24,480]{1,0:T(8,128)(2,1)S(1)} %get-tuple-element.55), channel_id=1, source_target_pairs={{0,24},{8,0},{16,8},{24,16},{1,25},{9,1},{17,9},{25,17},{2,26},{10... | collective-permute-start | bytes 69128 | tf_op jit(solution)/shard_map/ppermute | solution.py:30
  33.9 1.9 %collective-permute-start = (bf16[2,96,128]{2,1,0:T(8,128)(2,1)S(1)}, bf16[2,96,128]{2,1,0:T(8,128)(2,1)S(1)}, u32[]{:S(2)}, u32[]{:S(2)}) collective-permute-start(bf16[2,96,128]{2,1,0:T(8,128)(2,1)S(1)} %get-tuple-element.44), channel_id=1, source_target_pairs={{0,1},{1,2},{2,3},{3,4},{4,5},{5,6},{6,7},{7,8},{8,9},{9,10},{10,1... | collective-permute-start | bytes 147464 | tf_op jit(solution)/shard_map/ppermute | solution.py:166
  35.8 3.6 %collective-permute-start.1 = (bf16[2,96,128]{2,1,0:T(8,128)(2,1)S(1)}, bf16[2,96,128]{2,1,0:T(8,128)(2,1)S(1)}, u32[]{:S(2)}, u32[]{:S(2)}) collective-permute-start(bf16[2,96,128]{2,1,0:T(8,128)(2,1)S(1)} %get-tuple-element.45), channel_id=1, source_target_pairs={{1,0},{2,1},{3,2},{4,3},{5,4},{6,5},{7,6},{8,7},{9,8},{10,9},{11,1... | collective-permute-start | bytes 147464 | tf_op jit(solution)/shard_map/ppermute | solution.py:167
  40.2 2.9 %collective-permute-start.13 = (bf16[4,24,480]{2,1,0:T(8,128)(2,1)}, bf16[4,24,480]{2,1,0:T(8,128)(2,1)}, u32[]{:S(2)}, u32[]{:S(2)}) collective-permute-start(bf16[4,24,480]{2,1,0:T(8,128)(2,1)} %pad_maximum_fusion.1), channel_id=1, source_target_pairs={{0,4},{2,6},{4,0},{6,2},{1,5},{3,7},{5,1},{7,3},{8,12},{10,14},{12... | collective-permute-start | bytes 276488 | tf_op jit(solution)/shard_map/ppermute | solution.py:30
  43.1 1.9 %collective-permute-start.5 = (bf16[4,24,480]{2,1,0:T(8,128)(2,1)S(1)}, bf16[4,24,480]{2,1,0:T(8,128)(2,1)S(1)}, u32[]{:S(2)}, u32[]{:S(2)}) collective-permute-start(bf16[4,24,480]{2,1,0:T(8,128)(2,1)S(1)} %pad_maximum_fusion), channel_id=1, source_target_pairs={{0,2},{2,4},{4,6},{6,0},{1,3},{3,5},{5,7},{7,1},{8,10},{10,12},{12... | collective-permute-start | bytes 276488 | tf_op jit(solution)/shard_map/ppermute | solution.py:30
  45.0 3.9 %collective-permute-done.5 = bf16[4,24,480]{2,1,0:T(8,128)(2,1)S(1)} collective-permute-done((bf16[4,24,480]{2,1,0:T(8,128)(2,1)S(1)}, bf16[4,24,480]{2,1,0:T(8,128)(2,1)S(1)}, u32[]{:S(2)}, u32[]{:S(2)}) %collective-permute-start.5) | collective-permute-done | bytes 92192 | tf_op jit(solution)/shard_map/ppermute | solution.py:30
  48.9 1.3 collective-permute-start.6
  50.2 4.8 %collective-permute-done.6 = bf16[4,24,480]{2,1,0:T(8,128)(2,1)S(1)} collective-permute-done((bf16[4,24,480]{2,1,0:T(8,128)(2,1)S(1)}, bf16[4,24,480]{2,1,0:T(8,128)(2,1)S(1)}, u32[]{:S(2)}, u32[]{:S(2)}) %collective-permute-start.6) | collective-permute-done | bytes 92192 | tf_op jit(solution)/shard_map/ppermute | solution.py:30
  55.0 1.9 %collective-permute-start.7 = (bf16[4,24,480]{2,1,0:T(8,128)(2,1)S(1)}, bf16[4,24,480]{2,1,0:T(8,128)(2,1)S(1)}, u32[]{:S(2)}, u32[]{:S(2)}) collective-permute-start(bf16[4,24,480]{2,1,0:T(8,128)(2,1)S(1)} %pad_maximum_fusion), channel_id=1, source_target_pairs={{0,6},{2,0},{4,2},{6,4},{1,7},{3,1},{5,3},{7,5},{8,14},{10,8},{12,... | collective-permute-start | bytes 276488 | tf_op jit(solution)/shard_map/ppermute | solution.py:30
  56.9 2.7 %collective-permute-done.7 = bf16[4,24,480]{2,1,0:T(8,128)(2,1)S(1)} collective-permute-done((bf16[4,24,480]{2,1,0:T(8,128)(2,1)S(1)}, bf16[4,24,480]{2,1,0:T(8,128)(2,1)S(1)}, u32[]{:S(2)}, u32[]{:S(2)}) %collective-permute-start.7) | collective-permute-done | bytes 92192 | tf_op jit(solution)/shard_map/ppermute | solution.py:30
  59.6 1.3 collective-permute-start.12
  61.2 1.5 %collective-permute-done.8.other_ref = bf16[16,24,480]{2,1,0:T(8,128)(2,1)S(1)} collective-permute-done((bf16[16,24,480]{2,1,0:T(8,128)(2,1)S(1)}, bf16[16,24,480]{2,1,0:T(8,128)(2,1)S(1)}, u32[]{:S(2)}, u32[]{:S(2)}) %collective-permute-start.8) | collective-permute-done | bytes 368672 | tf_op jit(solution)/shard_map/ppermute | solution.py:30
  62.7 2.8 %upper.1 = (bf16[8,96,640]{2,1,0:T(8,128)(2,1)}, bf16[480,640]{1,0:T(8,128)(2,1)S(1)}) custom-call(s32[3]{0:T(128)S(1)} %pad_add_fusion.pos_ref, bf16[32,6,256]{2,1,0:T(8,128)(2,1)S(1)} %all-to-all-done.tower_ref, f32[96,768]{1,0:T(8,128)S(1)} %fusion.13.slope_ref, bf16[16,24,480]{2,1,0:T(8,128)(2,1)S(1)} %constant_dynamic-update-slice_fusion.own_ref, ...), custom_call_target="tpu_custom_call" | custom-call | tf_op jit(solution)/shard_map/upper/pallas_call | solution.py:198
  66.4 4.9 %all-to-all-start.1 = ((bf16[8,96,640]{2,1,0:T(8,128)(2,1)}), bf16[8,96,640]{2,1,0:T(8,128)(2,1)S(1)}, u32[]{:S(2)}, u32[]{:S(2)}) async-start(bf16[8,96,640]{2,1,0:T(8,128)(2,1)} %get-tuple-element.11), calls=%async_computation.1 | async-start | bytes 1966080 | tf_op jit(solution)/shard_map/all_to_all | solution.py:207
  71.3 1.1 copy-done.5
  72.3 1.3 weight_grad.2
  73.7 0.9 constant_dynamic-update-slice_fusion.9
  74.6 0.9 constant_dynamic-update-slice_fusion.8
  75.5 0.9 constant_dynamic-update-slice_fusion.7.own_ref
  77.2 1.9 %collective-permute-start.17 = (bf16[4,24,480]{2,1,0:T(8,128)(2,1)S(1)}, bf16[4,24,480]{2,1,0:T(8,128)(2,1)S(1)}, u32[]{:S(2)}, u32[]{:S(2)}) collective-permute-start(bf16[4,24,480]{2,1,0:T(8,128)(2,1)S(1)} %get-tuple-element.33), channel_id=1, source_target_pairs={{0,2},{2,4},{4,6},{6,0},{1,3},{3,5},{5,7},{7,1},{8,10},{10,12},{12... | collective-permute-start | bytes 276488 | tf_op jit(solution)/shard_map/ppermute | solution.py:30
  79.3 2.7 %collective-permute-start.18 = (bf16[4,24,480]{2,1,0:T(8,128)(2,1)S(1)}, bf16[4,24,480]{2,1,0:T(8,128)(2,1)S(1)}, u32[]{:S(2)}, u32[]{:S(2)}) collective-permute-start(bf16[4,24,480]{2,1,0:T(8,128)(2,1)S(1)} %get-tuple-element.35), channel_id=1, source_target_pairs={{0,4},{2,6},{4,0},{6,2},{1,5},{3,7},{5,1},{7,3},{8,12},{10,14},{12... | collective-permute-start | bytes 276488 | tf_op jit(solution)/shard_map/ppermute | solution.py:30
  82.3 1.0 copy-done.7
  84.1 2.9 %collective-permute-done.18 = bf16[4,24,480]{2,1,0:T(8,128)(2,1)S(1)} collective-permute-done((bf16[4,24,480]{2,1,0:T(8,128)(2,1)S(1)}, bf16[4,24,480]{2,1,0:T(8,128)(2,1)S(1)}, u32[]{:S(2)}, u32[]{:S(2)}) %collective-permute-start.18) | collective-permute-done | bytes 92192 | tf_op jit(solution)/shard_map/ppermute | solution.py:30
  87.7 2.3 %lower.1 = (bf16[8,80,1024]{2,1,0:T(8,128)(2,1)S(1)}, bf16[480,1024]{1,0:T(8,128)(2,1)S(1)}) custom-call(s32[3]{0:T(128)S(1)} %pad_add_fusion.pos_ref, bf16[8,96,640]{2,1,0:T(8,128)(2,1)S(1)} %all-to-all-done.1.mid_ref, f32[96,1280]{1,0:T(8,128)S(1)} %fusion.6.slope_ref, bf16[640,480]{1,0:T(8,128)(2,1)S(1)} %lower_weight.1.w_ref), custom_call_target="tpu_custom_call" | custom-call | tf_op jit(solution)/shard_map/lower/pallas_call | solution.py:220
  90.0 1.1 copy-done
  91.1 0.9 copy-done.1
  92.0 5.8 %all-to-all-start.2 = ((bf16[8,80,1024]{2,1,0:T(8,128)(2,1)}), bf16[8,80,1024]{2,1,0:T(8,128)(2,1)}, u32[]{:S(2)}, u32[]{:S(2)}) async-start(bf16[8,80,1024]{2,1,0:T(8,128)(2,1)} %copy-done), calls=%async_computation.2 | async-start | bytes 2621440 | tf_op jit(solution)/shard_map/all_to_all | solution.py:228
  97.9 1.6 %weight_grad.3 = (f32[4,4,24,480]{3,2,1,0:T(8,128)S(1)}, bf16[4,4,24,480]{3,2,1,0:T(8,128)(2,1)S(1)}) custom-call(s32[3]{0:T(128)S(1)} %pad_add_fusion.pos_ref, bf16[640,1024]{1,0:T(8,128)(2,1)S(1)} %bitcast.86, bf16[480,1024]{1,0:T(8,128)(2,1)S(1)} %copy-done.2), custom_call_target="tpu_custom_call" | custom-call | tf_op jit(solution)/shard_map/weight_grad/pallas_call | solution.py:151
  99.6 1.8 %collective-permute-start.20 = (bf16[24,480]{1,0:T(8,128)(2,1)S(1)}, bf16[24,480]{1,0:T(8,128)(2,1)S(1)}, u32[]{:S(2)}, u32[]{:S(2)}) collective-permute-start(bf16[24,480]{1,0:T(8,128)(2,1)S(1)} %get-tuple-element.41), channel_id=1, source_target_pairs={{0,8},{8,16},{16,24},{24,0},{1,9},{9,17},{17,25},{25,1},{2,10},{10... | collective-permute-start | bytes 69128 | tf_op jit(solution)/shard_map/ppermute | solution.py:30
  101.3 2.5 %collective-permute-start.22 = (bf16[24,480]{1,0:T(8,128)(2,1)S(1)}, bf16[24,480]{1,0:T(8,128)(2,1)S(1)}, u32[]{:S(2)}, u32[]{:S(2)}) collective-permute-start(bf16[24,480]{1,0:T(8,128)(2,1)S(1)} %get-tuple-element.42), channel_id=1, source_target_pairs={{0,24},{8,0},{16,8},{24,16},{1,25},{9,1},{17,9},{25,17},{2,26},{10... | collective-permute-start | bytes 69128 | tf_op jit(solution)/shard_map/ppermute | solution.py:30
  103.8 5.0 %collective-permute-start.21 = (bf16[24,480]{1,0:T(8,128)(2,1)S(1)}, bf16[24,480]{1,0:T(8,128)(2,1)S(1)}, u32[]{:S(2)}, u32[]{:S(2)}) collective-permute-start(bf16[24,480]{1,0:T(8,128)(2,1)S(1)} %get-tuple-element.43), channel_id=1, source_target_pairs={{0,16},{8,24},{16,0},{24,8},{1,17},{9,25},{17,1},{25,9},{2,18},{10... | collective-permute-start | bytes 69128 | tf_op jit(solution)/shard_map/ppermute | solution.py:30
  109.8 1.3 collective-permute-start.24
  111.9 5.8 %collective-permute-done.20 = bf16[24,480]{1,0:T(8,128)(2,1)S(1)} collective-permute-done((bf16[24,480]{1,0:T(8,128)(2,1)S(1)}, bf16[24,480]{1,0:T(8,128)(2,1)S(1)}, u32[]{:S(2)}, u32[]{:S(2)}) %collective-permute-start.20) | collective-permute-done | bytes 23072 | tf_op jit(solution)/shard_map/ppermute | solution.py:30
  117.7 2.1 %collective-permute-start.25 = (bf16[4,24,480]{2,1,0:T(8,128)(2,1)S(1)}, bf16[4,24,480]{2,1,0:T(8,128)(2,1)S(1)}, u32[]{:S(2)}, u32[]{:S(2)}) collective-permute-start(bf16[4,24,480]{2,1,0:T(8,128)(2,1)S(1)} %get-tuple-element.32), channel_id=1, source_target_pairs={{0,4},{2,6},{4,0},{6,2},{1,5},{3,7},{5,1},{7,3},{8,12},{10,14},{12... | collective-permute-start | bytes 276488 | tf_op jit(solution)/shard_map/ppermute | solution.py:30
  120.6 3.3 %collective-permute-done.25 = bf16[4,24,480]{2,1,0:T(8,128)(2,1)S(1)} collective-permute-done((bf16[4,24,480]{2,1,0:T(8,128)(2,1)S(1)}, bf16[4,24,480]{2,1,0:T(8,128)(2,1)S(1)}, u32[]{:S(2)}, u32[]{:S(2)}) %collective-permute-start.25) | collective-permute-done | bytes 92192 | tf_op jit(solution)/shard_map/ppermute | solution.py:30
  124.0 4.1 %collective-permute-start.29 = (bf16[24,480]{1,0:T(8,128)(2,1)S(1)}, bf16[24,480]{1,0:T(8,128)(2,1)S(1)}, u32[]{:S(2)}, u32[]{:S(2)}) collective-permute-start(bf16[24,480]{1,0:T(8,128)(2,1)S(1)} %get-tuple-element.39), channel_id=1, source_target_pairs={{0,24},{8,0},{16,8},{24,16},{1,25},{9,1},{17,9},{25,17},{2,26},{10... | collective-permute-start | bytes 69128 | tf_op jit(solution)/shard_map/ppermute | solution.py:30
  128.1 1.1 collective-permute-start.28
  129.9 6.2 %collective-permute-done.28 = bf16[24,480]{1,0:T(8,128)(2,1)S(1)} collective-permute-done((bf16[24,480]{1,0:T(8,128)(2,1)S(1)}, bf16[24,480]{1,0:T(8,128)(2,1)S(1)}, u32[]{:S(2)}, u32[]{:S(2)}) %collective-permute-start.28) | collective-permute-done | bytes 23072 | tf_op jit(solution)/shard_map/ppermute | solution.py:30
  137.2 2.3 %reduce_sum.12 = bf16[80,1024]{1,0:T(8,128)(2,1)} reduce(bf16[8,80,1024]{2,1,0:T(8,128)(2,1)} %all-to-all-done.2, bf16[]{:T(256)} %constant.12.clone.1), dimensions={0}, to_apply=%region_0.1 | reduce | flops 573440 | bytes 1474562 | tf_op jit(solution)/shard_map/reduce_sum | solution.py:231
  (103 shorter events, 11.9 us)
Async XLA Ops:
  0.6 27.1 %copy-start.10 = (bf16[512,96]{0,1:T(8,128)(2,1)S(1)}, bf16[512,96]{0,1:T(8,128)(2,1)}, u32[]{:S(2)}) copy-start(bf16[512,96]{0,1:T(8,128)(2,1)} %param.9) | copy-start | bytes 294916
  0.6 27.1 %copy-start.11 = (bf16[1024,88]{0,1:T(8,128)(2,1)S(1)}, bf16[1024,88]{0,1:T(8,128)(2,1)}, u32[]{:S(2)}) copy-start(bf16[1024,88]{0,1:T(8,128)(2,1)} %param.11) | copy-start | bytes 540676
  1.6 38.6 %collective-permute-start.3 = (bf16[24,480]{1,0:T(8,128)(2,1)S(1)}, bf16[24,480]{1,0:T(8,128)(2,1)S(1)}, u32[]{:S(2)}, u32[]{:S(2)}) collective-permute-start(bf16[24,480]{1,0:T(8,128)(2,1)S(1)} %get-tuple-element.55), channel_id=1, source_target_pairs={{0,16},{8,24},{16,0},{24,8},{1,17},{9,25},{17,1},{25,9},{2,18},{10... | collective-permute-start | bytes 69128 | tf_op jit(solution)/shard_map/ppermute | solution.py:30
  8.8 31.3 %collective-permute-start.2 = (bf16[24,480]{1,0:T(8,128)(2,1)S(1)}, bf16[24,480]{1,0:T(8,128)(2,1)S(1)}, u32[]{:S(2)}, u32[]{:S(2)}) collective-permute-start(bf16[24,480]{1,0:T(8,128)(2,1)S(1)} %get-tuple-element.55), channel_id=1, source_target_pairs={{0,8},{8,16},{16,24},{24,0},{1,9},{9,17},{17,25},{25,1},{2,10},{10... | collective-permute-start | bytes 69128 | tf_op jit(solution)/shard_map/ppermute | solution.py:30
  11.4 18.8 %collective-permute-start.11 = (bf16[24,480]{1,0:T(8,128)(2,1)S(1)}, bf16[24,480]{1,0:T(8,128)(2,1)S(1)}, u32[]{:S(2)}, u32[]{:S(2)}) collective-permute-start(bf16[24,480]{1,0:T(8,128)(2,1)S(1)} %reshape.50), channel_id=1, source_target_pairs={{0,24},{8,0},{16,8},{24,16},{1,25},{9,1},{17,9},{25,17},{2,26},{10... | collective-permute-start | bytes 69128 | tf_op jit(solution)/shard_map/ppermute | solution.py:30
  14.2 19.8 %collective-permute-start.10 = (bf16[24,480]{1,0:T(8,128)(2,1)S(1)}, bf16[24,480]{1,0:T(8,128)(2,1)S(1)}, u32[]{:S(2)}, u32[]{:S(2)}) collective-permute-start(bf16[24,480]{1,0:T(8,128)(2,1)S(1)} %reshape.50), channel_id=1, source_target_pairs={{0,16},{8,24},{16,0},{24,8},{1,17},{9,25},{17,1},{25,9},{2,18},{10... | collective-permute-start | bytes 69128 | tf_op jit(solution)/shard_map/ppermute | solution.py:30
  15.1 20.8 %collective-permute-start.9 = (bf16[24,480]{1,0:T(8,128)(2,1)S(1)}, bf16[24,480]{1,0:T(8,128)(2,1)S(1)}, u32[]{:S(2)}, u32[]{:S(2)}) collective-permute-start(bf16[24,480]{1,0:T(8,128)(2,1)S(1)} %reshape.50), channel_id=1, source_target_pairs={{0,8},{8,16},{16,24},{24,0},{1,9},{9,17},{17,25},{25,1},{2,10},{10... | collective-permute-start | bytes 69128 | tf_op jit(solution)/shard_map/ppermute | solution.py:30
  19.0 42.2 %all-to-all-start = ((bf16[32,6,256]{2,1,0:T(8,128)(2,1)}), bf16[32,6,256]{2,1,0:T(8,128)(2,1)S(1)}, u32[]{:S(2)}, u32[]{:S(2)}) async-start(bf16[32,6,256]{2,1,0:T(8,128)(2,1)} %fusion.24), calls=%async_computation | async-start | bytes 262144 | tf_op jit(solution)/shard_map/all_to_all | solution.py:178
  27.8 0.7 copy-start.8
  30.2 12.9 %collective-permute-start.4 = (bf16[24,480]{1,0:T(8,128)(2,1)S(1)}, bf16[24,480]{1,0:T(8,128)(2,1)S(1)}, u32[]{:S(2)}, u32[]{:S(2)}) collective-permute-start(bf16[24,480]{1,0:T(8,128)(2,1)S(1)} %get-tuple-element.55), channel_id=1, source_target_pairs={{0,24},{8,0},{16,8},{24,16},{1,25},{9,1},{17,9},{25,17},{2,26},{10... | collective-permute-start | bytes 69128 | tf_op jit(solution)/shard_map/ppermute | solution.py:30
  33.9 27.0 %collective-permute-start = (bf16[2,96,128]{2,1,0:T(8,128)(2,1)S(1)}, bf16[2,96,128]{2,1,0:T(8,128)(2,1)S(1)}, u32[]{:S(2)}, u32[]{:S(2)}) collective-permute-start(bf16[2,96,128]{2,1,0:T(8,128)(2,1)S(1)} %get-tuple-element.44), channel_id=1, source_target_pairs={{0,1},{1,2},{2,3},{3,4},{4,5},{5,6},{6,7},{7,8},{8,9},{9,10},{10,1... | collective-permute-start | bytes 147464 | tf_op jit(solution)/shard_map/ppermute | solution.py:166
  35.8 25.2 %collective-permute-start.1 = (bf16[2,96,128]{2,1,0:T(8,128)(2,1)S(1)}, bf16[2,96,128]{2,1,0:T(8,128)(2,1)S(1)}, u32[]{:S(2)}, u32[]{:S(2)}) collective-permute-start(bf16[2,96,128]{2,1,0:T(8,128)(2,1)S(1)} %get-tuple-element.45), channel_id=1, source_target_pairs={{1,0},{2,1},{3,2},{4,3},{5,4},{6,5},{7,6},{8,7},{9,8},{10,9},{11,1... | collective-permute-start | bytes 147464 | tf_op jit(solution)/shard_map/ppermute | solution.py:167
  40.1 35.4 %collective-permute-start.14 = (bf16[4,24,480]{2,1,0:T(8,128)(2,1)}, bf16[4,24,480]{2,1,0:T(8,128)(2,1)}, u32[]{:S(2)}, u32[]{:S(2)}) collective-permute-start(bf16[4,24,480]{2,1,0:T(8,128)(2,1)} %pad_maximum_fusion.1), channel_id=1, source_target_pairs={{0,6},{2,0},{4,2},{6,4},{1,7},{3,1},{5,3},{7,5},{8,14},{10,8},{12,... | collective-permute-start | bytes 276488 | tf_op jit(solution)/shard_map/ppermute | solution.py:30
  40.2 34.5 %collective-permute-start.13 = (bf16[4,24,480]{2,1,0:T(8,128)(2,1)}, bf16[4,24,480]{2,1,0:T(8,128)(2,1)}, u32[]{:S(2)}, u32[]{:S(2)}) collective-permute-start(bf16[4,24,480]{2,1,0:T(8,128)(2,1)} %pad_maximum_fusion.1), channel_id=1, source_target_pairs={{0,4},{2,6},{4,0},{6,2},{1,5},{3,7},{5,1},{7,3},{8,12},{10,14},{12... | collective-permute-start | bytes 276488 | tf_op jit(solution)/shard_map/ppermute | solution.py:30
  43.1 5.7 %collective-permute-start.5 = (bf16[4,24,480]{2,1,0:T(8,128)(2,1)S(1)}, bf16[4,24,480]{2,1,0:T(8,128)(2,1)S(1)}, u32[]{:S(2)}, u32[]{:S(2)}) collective-permute-start(bf16[4,24,480]{2,1,0:T(8,128)(2,1)S(1)} %pad_maximum_fusion), channel_id=1, source_target_pairs={{0,2},{2,4},{4,6},{6,0},{1,3},{3,5},{5,7},{7,1},{8,10},{10,12},{12... | collective-permute-start | bytes 276488 | tf_op jit(solution)/shard_map/ppermute | solution.py:30
  48.9 6.1 %collective-permute-start.6 = (bf16[4,24,480]{2,1,0:T(8,128)(2,1)S(1)}, bf16[4,24,480]{2,1,0:T(8,128)(2,1)S(1)}, u32[]{:S(2)}, u32[]{:S(2)}) collective-permute-start(bf16[4,24,480]{2,1,0:T(8,128)(2,1)S(1)} %pad_maximum_fusion), channel_id=1, source_target_pairs={{0,4},{2,6},{4,0},{6,2},{1,5},{3,7},{5,1},{7,3},{8,12},{10,14},{12... | collective-permute-start | bytes 276488 | tf_op jit(solution)/shard_map/ppermute | solution.py:30
  55.0 4.6 %collective-permute-start.7 = (bf16[4,24,480]{2,1,0:T(8,128)(2,1)S(1)}, bf16[4,24,480]{2,1,0:T(8,128)(2,1)S(1)}, u32[]{:S(2)}, u32[]{:S(2)}) collective-permute-start(bf16[4,24,480]{2,1,0:T(8,128)(2,1)S(1)} %pad_maximum_fusion), channel_id=1, source_target_pairs={{0,6},{2,0},{4,2},{6,4},{1,7},{3,1},{5,3},{7,5},{8,14},{10,8},{12,... | collective-permute-start | bytes 276488 | tf_op jit(solution)/shard_map/ppermute | solution.py:30
  59.6 14.1 %collective-permute-start.12 = (bf16[4,24,480]{2,1,0:T(8,128)(2,1)}, bf16[4,24,480]{2,1,0:T(8,128)(2,1)}, u32[]{:S(2)}, u32[]{:S(2)}) collective-permute-start(bf16[4,24,480]{2,1,0:T(8,128)(2,1)} %pad_maximum_fusion.1), channel_id=1, source_target_pairs={{0,2},{2,4},{4,6},{6,0},{1,3},{3,5},{5,7},{7,1},{8,10},{10,12},{12... | collective-permute-start | bytes 276488 | tf_op jit(solution)/shard_map/ppermute | solution.py:30
  60.9 1.8 %collective-permute-start.8 = (bf16[16,24,480]{2,1,0:T(8,128)(2,1)S(1)}, bf16[16,24,480]{2,1,0:T(8,128)(2,1)S(1)}, u32[]{:S(2)}, u32[]{:S(2)}) collective-permute-start(bf16[16,24,480]{2,1,0:T(8,128)(2,1)S(1)} %constant_dynamic-update-slice_fusion.own_ref), channel_id=1, source_target_pairs={{0,1},{1,0},{2,3},{3,2},{4,5},{5,4},{6,7},{7,6},{8,9},{9,8},{10,11... | collective-permute-start | bytes 1105928 | tf_op jit(solution)/shard_map/ppermute | solution.py:30
  65.5 0.8 copy-start.4
  66.4 4.9 %copy-start.3 = (bf16[512,704]{0,1:T(8,128)(2,1)S(1)}, bf16[512,704]{0,1:T(8,128)(2,1)}, u32[]{:S(2)}) copy-start(bf16[512,704]{0,1:T(8,128)(2,1)} %param.8) | copy-start | bytes 2162692
  66.4 21.4 %all-to-all-start.1 = ((bf16[8,96,640]{2,1,0:T(8,128)(2,1)}), bf16[8,96,640]{2,1,0:T(8,128)(2,1)S(1)}, u32[]{:S(2)}, u32[]{:S(2)}) async-start(bf16[8,96,640]{2,1,0:T(8,128)(2,1)} %get-tuple-element.11), calls=%async_computation.1 | async-start | bytes 1966080 | tf_op jit(solution)/shard_map/all_to_all | solution.py:207
  71.3 1.1 copy-start.5
  73.6 3.4 %collective-permute-start.16 = (bf16[4,4,24,480]{3,2,1,0:T(8,128)(2,1)S(1)}, bf16[4,4,24,480]{3,2,1,0:T(8,128)(2,1)S(1)}, u32[]{:S(2)}, u32[]{:S(2)}) collective-permute-start(bf16[4,4,24,480]{3,2,1,0:T(8,128)(2,1)S(1)} %get-tuple-element.15), channel_id=1, source_target_pairs={{0,1},{1,0},{2,3},{3,2},{4,5},{5,4},{6,7},{7,6},{8,9},{9,8},{10,11... | collective-permute-start | bytes 1105928 | tf_op jit(solution)/shard_map/ppermute | solution.py:30
  76.4 0.8 copy-start.6
  76.5 5.8 %collective-permute-start.15 = (bf16[16,24,480]{2,1,0:T(8,128)(2,1)S(1)}, bf16[16,24,480]{2,1,0:T(8,128)(2,1)S(1)}, u32[]{:S(2)}, u32[]{:S(2)}) collective-permute-start(bf16[16,24,480]{2,1,0:T(8,128)(2,1)S(1)} %constant_dynamic-update-slice_fusion.7.own_ref), channel_id=1, source_target_pairs={{0,1},{1,0},{2,3},{3,2},{4,5},{5,4},{6,7},{7,6},{8,9},{9,8},{10,11... | collective-permute-start | bytes 1105928 | tf_op jit(solution)/shard_map/ppermute | solution.py:30
  77.0 5.0 %copy-start.9 = (bf16[4,24,1024]{2,1,0:T(8,128)(2,1)S(1)}, bf16[4,24,1024]{2,1,0:T(8,128)(2,1)}, u32[]{:S(2)}) copy-start(bf16[4,24,1024]{2,1,0:T(8,128)(2,1)} %copy-done.8) | copy-start | bytes 589828
  77.2 6.8 %collective-permute-start.17 = (bf16[4,24,480]{2,1,0:T(8,128)(2,1)S(1)}, bf16[4,24,480]{2,1,0:T(8,128)(2,1)S(1)}, u32[]{:S(2)}, u32[]{:S(2)}) collective-permute-start(bf16[4,24,480]{2,1,0:T(8,128)(2,1)S(1)} %get-tuple-element.33), channel_id=1, source_target_pairs={{0,2},{2,4},{4,6},{6,0},{1,3},{3,5},{5,7},{7,1},{8,10},{10,12},{12... | collective-permute-start | bytes 276488 | tf_op jit(solution)/shard_map/ppermute | solution.py:30
  79.1 4.9 %collective-permute-start.19 = (bf16[4,24,480]{2,1,0:T(8,128)(2,1)S(1)}, bf16[4,24,480]{2,1,0:T(8,128)(2,1)S(1)}, u32[]{:S(2)}, u32[]{:S(2)}) collective-permute-start(bf16[4,24,480]{2,1,0:T(8,128)(2,1)S(1)} %get-tuple-element.34), channel_id=1, source_target_pairs={{0,6},{2,0},{4,2},{6,4},{1,7},{3,1},{5,3},{7,5},{8,14},{10,8},{12,... | collective-permute-start | bytes 276488 | tf_op jit(solution)/shard_map/ppermute | solution.py:30
  79.3 7.7 %collective-permute-start.18 = (bf16[4,24,480]{2,1,0:T(8,128)(2,1)S(1)}, bf16[4,24,480]{2,1,0:T(8,128)(2,1)S(1)}, u32[]{:S(2)}, u32[]{:S(2)}) collective-permute-start(bf16[4,24,480]{2,1,0:T(8,128)(2,1)S(1)} %get-tuple-element.35), channel_id=1, source_target_pairs={{0,4},{2,6},{4,0},{6,2},{1,5},{3,7},{5,1},{7,3},{8,12},{10,14},{12... | collective-permute-start | bytes 276488 | tf_op jit(solution)/shard_map/ppermute | solution.py:30
  82.3 1.0 copy-start.7
  90.0 1.1 copy-start
  91.1 0.9 copy-start.1
  92.0 5.8 %copy-start.2 = (bf16[480,1024]{1,0:T(8,128)(2,1)S(1)}, bf16[480,1024]{1,0:T(8,128)(2,1)}, u32[]{:S(2)}) copy-start(bf16[480,1024]{1,0:T(8,128)(2,1)} %copy-done.1) | copy-start | bytes 2949124
  92.0 45.1 %all-to-all-start.2 = ((bf16[8,80,1024]{2,1,0:T(8,128)(2,1)}), bf16[8,80,1024]{2,1,0:T(8,128)(2,1)}, u32[]{:S(2)}, u32[]{:S(2)}) async-start(bf16[8,80,1024]{2,1,0:T(8,128)(2,1)} %copy-done), calls=%async_computation.2 | async-start | bytes 2621440 | tf_op jit(solution)/shard_map/all_to_all | solution.py:228
  99.5 10.1 %collective-permute-start.23 = (bf16[4,4,24,480]{3,2,1,0:T(8,128)(2,1)S(1)}, bf16[4,4,24,480]{3,2,1,0:T(8,128)(2,1)S(1)}, u32[]{:S(2)}, u32[]{:S(2)}) collective-permute-start(bf16[4,4,24,480]{3,2,1,0:T(8,128)(2,1)S(1)} %get-tuple-element.18), channel_id=1, source_target_pairs={{0,1},{1,0},{2,3},{3,2},{4,5},{5,4},{6,7},{7,6},{8,9},{9,8},{10,11... | collective-permute-start | bytes 1105928 | tf_op jit(solution)/shard_map/ppermute | solution.py:30
  99.6 18.2 %collective-permute-start.20 = (bf16[24,480]{1,0:T(8,128)(2,1)S(1)}, bf16[24,480]{1,0:T(8,128)(2,1)S(1)}, u32[]{:S(2)}, u32[]{:S(2)}) collective-permute-start(bf16[24,480]{1,0:T(8,128)(2,1)S(1)} %get-tuple-element.41), channel_id=1, source_target_pairs={{0,8},{8,16},{16,24},{24,0},{1,9},{9,17},{17,25},{25,1},{2,10},{10... | collective-permute-start | bytes 69128 | tf_op jit(solution)/shard_map/ppermute | solution.py:30
  101.3 18.5 %collective-permute-start.22 = (bf16[24,480]{1,0:T(8,128)(2,1)S(1)}, bf16[24,480]{1,0:T(8,128)(2,1)S(1)}, u32[]{:S(2)}, u32[]{:S(2)}) collective-permute-start(bf16[24,480]{1,0:T(8,128)(2,1)S(1)} %get-tuple-element.42), channel_id=1, source_target_pairs={{0,24},{8,0},{16,8},{24,16},{1,25},{9,1},{17,9},{25,17},{2,26},{10... | collective-permute-start | bytes 69128 | tf_op jit(solution)/shard_map/ppermute | solution.py:30
  103.8 16.0 %collective-permute-start.21 = (bf16[24,480]{1,0:T(8,128)(2,1)S(1)}, bf16[24,480]{1,0:T(8,128)(2,1)S(1)}, u32[]{:S(2)}, u32[]{:S(2)}) collective-permute-start(bf16[24,480]{1,0:T(8,128)(2,1)S(1)} %get-tuple-element.43), channel_id=1, source_target_pairs={{0,16},{8,24},{16,0},{24,8},{1,17},{9,25},{17,1},{25,9},{2,18},{10... | collective-permute-start | bytes 69128 | tf_op jit(solution)/shard_map/ppermute | solution.py:30
  109.8 10.8 %collective-permute-start.24 = (bf16[4,24,480]{2,1,0:T(8,128)(2,1)S(1)}, bf16[4,24,480]{2,1,0:T(8,128)(2,1)S(1)}, u32[]{:S(2)}, u32[]{:S(2)}) collective-permute-start(bf16[4,24,480]{2,1,0:T(8,128)(2,1)S(1)} %get-tuple-element.30), channel_id=1, source_target_pairs={{0,2},{2,4},{4,6},{6,0},{1,3},{3,5},{5,7},{7,1},{8,10},{10,12},{12... | collective-permute-start | bytes 276488 | tf_op jit(solution)/shard_map/ppermute | solution.py:30
  111.1 9.5 %collective-permute-start.26 = (bf16[4,24,480]{2,1,0:T(8,128)(2,1)S(1)}, bf16[4,24,480]{2,1,0:T(8,128)(2,1)S(1)}, u32[]{:S(2)}, u32[]{:S(2)}) collective-permute-start(bf16[4,24,480]{2,1,0:T(8,128)(2,1)S(1)} %get-tuple-element.31), channel_id=1, source_target_pairs={{0,6},{2,0},{4,2},{6,4},{1,7},{3,1},{5,3},{7,5},{8,14},{10,8},{12,... | collective-permute-start | bytes 276488 | tf_op jit(solution)/shard_map/ppermute | solution.py:30
  117.7 6.1 %collective-permute-start.25 = (bf16[4,24,480]{2,1,0:T(8,128)(2,1)S(1)}, bf16[4,24,480]{2,1,0:T(8,128)(2,1)S(1)}, u32[]{:S(2)}, u32[]{:S(2)}) collective-permute-start(bf16[4,24,480]{2,1,0:T(8,128)(2,1)S(1)} %get-tuple-element.32), channel_id=1, source_target_pairs={{0,4},{2,6},{4,0},{6,2},{1,5},{3,7},{5,1},{7,3},{8,12},{10,14},{12... | collective-permute-start | bytes 276488 | tf_op jit(solution)/shard_map/ppermute | solution.py:30
  123.9 6.0 %collective-permute-start.27 = (bf16[24,480]{1,0:T(8,128)(2,1)S(1)}, bf16[24,480]{1,0:T(8,128)(2,1)S(1)}, u32[]{:S(2)}, u32[]{:S(2)}) collective-permute-start(bf16[24,480]{1,0:T(8,128)(2,1)S(1)} %get-tuple-element.38), channel_id=1, source_target_pairs={{0,8},{8,16},{16,24},{24,0},{1,9},{9,17},{17,25},{25,1},{2,10},{10... | collective-permute-start | bytes 69128 | tf_op jit(solution)/shard_map/ppermute | solution.py:30
  124.0 5.9 %collective-permute-start.29 = (bf16[24,480]{1,0:T(8,128)(2,1)S(1)}, bf16[24,480]{1,0:T(8,128)(2,1)S(1)}, u32[]{:S(2)}, u32[]{:S(2)}) collective-permute-start(bf16[24,480]{1,0:T(8,128)(2,1)S(1)} %get-tuple-element.39), channel_id=1, source_target_pairs={{0,24},{8,0},{16,8},{24,16},{1,25},{9,1},{17,9},{25,17},{2,26},{10... | collective-permute-start | bytes 69128 | tf_op jit(solution)/shard_map/ppermute | solution.py:30
  128.1 8.0 %collective-permute-start.28 = (bf16[24,480]{1,0:T(8,128)(2,1)S(1)}, bf16[24,480]{1,0:T(8,128)(2,1)S(1)}, u32[]{:S(2)}, u32[]{:S(2)}) collective-permute-start(bf16[24,480]{1,0:T(8,128)(2,1)S(1)} %get-tuple-element.40), channel_id=1, source_target_pairs={{0,16},{8,24},{16,0},{24,8},{1,17},{9,25},{17,1},{25,9},{2,18},{10... | collective-permute-start | bytes 69128 | tf_op jit(solution)/shard_map/ppermute | solution.py:30

commit v2 on v1

v2 whole, which is shorter than its diff:
```python
import math

import jax
import jax.numpy as jnp
from jax import lax
from jax.experimental import pallas as pl
from jax.experimental.pallas import tpu as pltpu
from jax.sharding import Mesh, PartitionSpec as P

KWIDTH = 5
HALF = 2
DP = ("x", "zl")
SEQ = ("zh", "y", "c")
NZ, NY, NC = 4, 4, 2
BF = jnp.bfloat16
F32 = jnp.float32
PARAMS = pltpu.CompilerParams(vmem_limit_bytes=40 * 1024 * 1024)
VMEM = pl.BlockSpec(memory_space=pltpu.VMEM)
SMEM = pl.BlockSpec(memory_space=pltpu.SMEM)
HBM = pl.BlockSpec(memory_space=pltpu.HBM)


def half_slope(pre_act):
    values = pre_act.astype(F32)
    cumulative = 0.5 * (1.0 + lax.erf(values * (1.0 / math.sqrt(2.0))))
    density = jnp.exp(-0.5 * values * values) * (1.0 / math.sqrt(2.0 * math.pi))
    return 0.5 * (cumulative + values * density)


def shifted(block, axis, count, step):
    return lax.ppermute(block, axis, [(i, (i + step) % count) for i in range(count)])


def scatter_rows(keep, send):
    total = keep + shifted(send, "c", NC, 1).astype(F32)
    parts = [shifted(total[s].astype(BF), "y", NY, s) for s in range(1, NY)]
    total = total[0] + sum(p.astype(F32) for p in parts)
    parts = [shifted(total[s].astype(BF), "zh", NZ, s) for s in range(1, NZ)]
    return total[0] + sum(p.astype(F32) for p in parts)


def doubling():
    row = lax.broadcasted_iota(jnp.int32, (128, 256), 0)
    col = lax.broadcasted_iota(jnp.int32, (128, 256), 1)
    return (row == lax.shift_right_logical(col, 1)).astype(F32).astype(BF)


def mm(a, b):
    return jnp.dot(a, b, preferred_element_type=F32)


def one_hot(rows, start, pads):
    row = lax.broadcasted_iota(jnp.int32, (rows, 512), 0)
    col = lax.broadcasted_iota(jnp.int32, (rows, 512), 1)
    place = row + start
    if pads:
        for edge in (22, 44, 66):
            place = place + jnp.where(row >= edge, 2, 0)
    return (place == col).astype(F32).astype(BF)


def pack_kernel(tower_ref, upper_ref, lower_ref, out_ref, weight_ref, tower_rows_ref, buf_ref, sem):
    weight_ref[...] = jnp.zeros((48, 512), F32)
    weight_ref[0:22, :] = sum(mm(upper_ref[k], one_hot(96, 96 * k, False)) for k in range(KWIDTH))
    weight_ref[24:44, :] = sum(mm(lower_ref[k], one_hot(88, 96 * k, True)) for k in range(KWIDTH))
    weight = weight_ref[...].astype(BF)
    tower = tower_ref[...].astype(F32)
    tower_rows_ref[...] = jnp.zeros((128, 512), F32)
    for p in range(16):
        at, row = 512 * p, 8 * p
        tower_rows_ref[row : row + 3, :] = tower[:, at : at + 512]
        if p > 0:
            tower_rows_ref[row + 3 : row + 6, 0:128] = tower[:, at - 128 : at]
        tower_rows_ref[row + 3 : row + 6, 128:256] = tower[:, at + 256 : at + 384]
        tower_rows_ref[row + 3 : row + 6, 256:384] = tower[:, at + 128 : at + 256]
        if p < 15:
            tower_rows_ref[row + 3 : row + 6, 384:512] = tower[:, at + 512 : at + 640]
        buf_ref[p, 0:48, :] = weight
        buf_ref[p, 48:56, :] = tower_rows_ref[row : row + 8, :].astype(BF)
        pltpu.make_async_copy(buf_ref.at[p], out_ref.at[p], sem.at[p]).start()
    for p in range(16):
        pltpu.make_async_copy(buf_ref.at[p], out_ref.at[p], sem.at[p]).wait()


def upper_kernel(
    pos_ref, slope_ref, own_ref, other_ref, mid_ref, taps_ref, main_ref, edge_ref, w_ref, halo_ref, buf_ref, sem
):
    first = pos_ref[2] == 0
    for p in range(16):
        own, other = own_ref[p, 48:56, :].astype(F32), other_ref[p, 48:56, :].astype(F32)
        for j in range(2):
            rows = jnp.where(first, own, other) if j == 0 else jnp.where(first, other, own)
            rows = jnp.where(first, rows[:, 0:256], rows[:, 256:512])
            at = 3 * (2 * p + j)
            main_ref[at : at + 3, :] = rows[0:3]
            edge_ref[at : at + 3, :] = rows[3:6]
        own, other = own_ref[p, 0:24, :].astype(F32), other_ref[p, 0:24, :].astype(F32)
        both = [jnp.where(first, own, other), jnp.where(first, other, own)]
        w_ref[48 * p : 48 * p + 48, :] = jnp.concatenate(both, axis=0).astype(BF)
    spread = doubling()
    main = main_ref[...].astype(BF)
    edge = edge_ref[...].astype(BF)
    grad = jnp.concatenate(
        [
            mm(edge[:, :128], spread)[:, 128:],
            mm(main[:, :128], spread),
            mm(main[:, 128:], spread),
            mm(edge[:, 128:], spread)[:, :128],
        ],
        axis=1,
    )
    grad = grad * slope_ref[...]
    lane = lax.broadcasted_iota(jnp.int32, (96, 128), 1)
    taps_ref[480:512, :] = jnp.zeros((32, 512), BF)
    halo_ref[480:512, :] = jnp.zeros((32, 128), F32)
    for k in range(KWIDTH):
        moved = pltpu.roll(grad, 768 - (130 - k), 1)
        after = pltpu.roll(moved[:, 512:640], 126, 1)
        taps_ref[96 * k : 96 * k + 96, :] = moved[:, 0:512].astype(BF)
        halo_ref[96 * k : 96 * k + 96, :] = jnp.where(lane == 127, moved[:, 640:768], after)
    outside = lax.dot_general(
        halo_ref[...].T.astype(BF), w_ref[...], (((1,), (1,)), ((), ())), preferred_element_type=F32
    )[120:128]
    row = lax.broadcasted_iota(jnp.int32, (8, 512), 0)
    taps = taps_ref[...]
    for d in range(8):
        mid = mm(w_ref[96 * d : 96 * d + 96, :], taps)
        moved = pltpu.roll(outside, (768 - 96 * d) % 768, 1)[:, 0:512]
        buf_ref[d] = jnp.concatenate([mid[0:16], jnp.where(row >= 6, moved, mid[16:24]), mid[24:]], axis=0).astype(BF)
        pltpu.make_async_copy(buf_ref.at[d], mid_ref.at[d], sem.at[d]).start()
    for d in range(8):
        pltpu.make_async_copy(buf_ref.at[d], mid_ref.at[d], sem.at[d]).wait()


def lower_weight_kernel(pos_ref, own_ref, other_ref, out_ref, rows_ref):
    first = pos_ref[2] == 0
    for p in range(16):
        own, other = own_ref[p, 24:48, :].astype(F32), other_ref[p, 24:48, :].astype(F32)
        rows_ref[40 * p : 40 * p + 24, :] = jnp.where(first, own, other)
        rows_ref[40 * p + 20 : 40 * p + 44, :] = jnp.where(first, other, own)
    out_ref[...] = rows_ref[0:640, :].astype(BF)


def lower_kernel(pos_ref, mid_ref, slope_ref, w_ref, low_ref, taps_ref, buf_ref, sem):
    place = pos_ref[0] * (NY * NC) + pos_ref[1] * NC + pos_ref[2]
    total = mid_ref[0].astype(F32)
    for d in range(1, 8):
        total = total + mid_ref[d].astype(F32)
    mid = total.astype(BF)
    ends = mid[:, 0:128].astype(F32).T
    left = jnp.broadcast_to(jnp.where(place == 0, 0.0, ends[0:96, 23:24]), (96, 128))
    right = jnp.broadcast_to(jnp.where(place == 31, 0.0, ends[0:96, 22:23]), (96, 128))
    spread = doubling()
    grad = jnp.concatenate(
        [left] + [mm(mid[:, 128 * j : 128 * j + 128], spread) for j in range(4)] + [right], axis=1
    )
    grad = grad * slope_ref[...]
    taps_ref[480:512, :] = jnp.zeros((32, 1024), BF)
    for k in range(KWIDTH):
        moved = pltpu.roll(grad, 1280 - (130 - k), 1)
        taps_ref[96 * k : 96 * k + 96, :] = moved[:, 0:1024].astype(BF)
    taps = taps_ref[...]
    for d in range(8):
        buf_ref[d] = mm(w_ref[80 * d : 80 * d + 80, :], taps).astype(BF)
        pltpu.make_async_copy(buf_ref.at[d], low_ref.at[d], sem.at[d]).start()
    for d in range(8):
        pltpu.make_async_copy(buf_ref.at[d], low_ref.at[d], sem.at[d]).wait()


def total_kernel(low_ref, out_ref):
    total = low_ref[0].astype(F32)
    for d in range(1, 8):
        total = total + low_ref[d].astype(F32)
    out_ref[...] = total.astype(BF)


def weight_grad_kernel(pos_ref, act_ref, taps_ref, keep_ref, send_ref, rows_ref, block_ref):
    channels, count = act_ref.shape
    width = channels // 32
    rows_ref[channels:, :] = jnp.zeros((8, rows_ref.shape[1]), F32)
    rows_ref[0:channels, :] = lax.dot_general(
        act_ref[...], taps_ref[:, 0:count], (((1,), (1,)), ((), ())), preferred_element_type=F32
    )
    for q in range(32):
        block_ref[q] = rows_ref[width * q : width * q + 24, :]
    for ry in range(NY):
        for rz in range(NZ):
            zh = lax.rem(pos_ref[0] + rz, NZ)
            y = lax.rem(pos_ref[1] + ry, NY)
            base = (zh * NY + y) * NC
            keep_ref[ry, rz] = block_ref[base + pos_ref[2]]
            send_ref[ry, rz] = block_ref[base + 1 - pos_ref[2]].astype(BF)


def weight_grad(pos, act, taps):
    block = (NY, NZ, 24, taps.shape[0])
    return pl.pallas_call(
        weight_grad_kernel,
        out_shape=(jax.ShapeDtypeStruct(block, F32), jax.ShapeDtypeStruct(block, BF)),
        in_specs=[SMEM, VMEM, VMEM],
        out_specs=(VMEM, VMEM),
        scratch_shapes=[pltpu.VMEM((act.shape[0] + 8, taps.shape[0]), F32), pltpu.VMEM((32, 24, taps.shape[0]), F32)],
        compiler_params=PARAMS,
        name="weight_grad",
    )(pos, act, taps)


def neighbours(block):
    count = NZ * NY * NC
    forward = [(i, i + 1) for i in range(count - 1)]
    backward = [(i + 1, i) for i in range(count - 1)]
    low = lax.ppermute(block[:, :, -128:], SEQ, forward)
    high = lax.ppermute(block[:, :, :128], SEQ, backward)
    return low, high


def local(tower_grad, act_mid, pre_mid, act_low, pre_low, weight_upper, weight_lower):
    pos = jnp.stack([lax.axis_index("zh"), lax.axis_index("y"), lax.axis_index("c")]).astype(jnp.int32)
    packed = pl.pallas_call(
        pack_kernel,
        out_shape=jax.ShapeDtypeStruct((16, 56, 512), BF),
        in_specs=[VMEM] * 3,
        out_specs=HBM,
        scratch_shapes=[
            pltpu.VMEM((48, 512), F32),
            pltpu.VMEM((128, 512), F32),
            pltpu.VMEM((16, 56, 512), BF),
            pltpu.SemaphoreType.DMA((16,)),
        ],
        compiler_params=PARAMS,
        name="pack",
    )(tower_grad.T, weight_upper, weight_lower)
    own = lax.all_to_all(packed, ("zh", "y"), split_axis=0, concat_axis=0, tiled=True)
    other = shifted(own, "c", NC, 1)

    pre_upper = pre_mid.T
    pre_lower = jnp.pad(pre_low.T.reshape(4, 22, 1024), ((0, 0), (0, 2), (0, 0))).reshape(96, 1024)
    edges = jnp.stack(
        [
            jnp.concatenate([pre_upper[:, :128], pre_upper[:, -128:]], axis=1),
            jnp.concatenate([pre_lower[:, :128], pre_lower[:, -128:]], axis=1),
        ]
    )
    low_side, high_side = neighbours(edges)
    slope_upper = half_slope(jnp.concatenate([low_side[0], pre_upper, high_side[0]], axis=1))
    slope_lower = half_slope(jnp.concatenate([low_side[1], pre_lower, high_side[1]], axis=1))

    mid_part, upper_taps = pl.pallas_call(
        upper_kernel,
        out_shape=(jax.ShapeDtypeStruct((8, 96, 512), BF), jax.ShapeDtypeStruct((512, 512), BF)),
        in_specs=[SMEM] + [VMEM] * 3,
        out_specs=(HBM, VMEM),
        scratch_shapes=[
            pltpu.VMEM((96, 256), F32),
            pltpu.VMEM((96, 256), F32),
            pltpu.VMEM((768, 512), BF),
            pltpu.VMEM((512, 128), F32),
            pltpu.VMEM((8, 96, 512), BF),
            pltpu.SemaphoreType.DMA((8,)),
        ],
        compiler_params=PARAMS,
        name="upper",
    )(pos, slope_upper, own, other)
    mid_parts = lax.all_to_all(mid_part, DP, split_axis=0, concat_axis=0, tiled=True)

    upper_sum = scatter_rows(*weight_grad(pos, act_mid.T, upper_taps))
    lower_full = pl.pallas_call(
        lower_weight_kernel,
        out_shape=jax.ShapeDtypeStruct((640, 512), BF),
        in_specs=[SMEM] + [VMEM] * 2,
        out_specs=VMEM,
        scratch_shapes=[pltpu.VMEM((648, 512), F32)],
        compiler_params=PARAMS,
        name="lower_weight",
    )(pos, own, other)

    low_part, lower_taps = pl.pallas_call(
        lower_kernel,
        out_shape=(jax.ShapeDtypeStruct((8, 80, 1024), BF), jax.ShapeDtypeStruct((512, 1024), BF)),
        in_specs=[SMEM] + [VMEM] * 3,
        out_specs=(HBM, VMEM),
        scratch_shapes=[pltpu.VMEM((8, 80, 1024), BF), pltpu.SemaphoreType.DMA((8,))],
        compiler_params=PARAMS,
        name="lower",
    )(pos, mid_parts, slope_lower, lower_full)
    low_parts = lax.all_to_all(low_part, DP, split_axis=0, concat_axis=0, tiled=True)
    lower_sum = scatter_rows(*weight_grad(pos, act_low.T, lower_taps))

    low_grad = pl.pallas_call(
        total_kernel,
        out_shape=jax.ShapeDtypeStruct((80, 1024), BF),
        in_specs=[VMEM],
        out_specs=VMEM,
        compiler_params=PARAMS,
        name="low_total",
    )(low_parts).T
    mid_total = act_mid.shape[0] * NZ * NY * NC
    low_total = act_low.shape[0] * NZ * NY * NC
    grad_upper = upper_sum[:22, :480].reshape(22, 5, 96).transpose(1, 0, 2) * (1.0 / math.sqrt(mid_total))
    grad_lower = lower_sum[:20, :480].reshape(20, 5, 4, 24)[:, :, :, :22].reshape(20, 5, 88)
    grad_lower = grad_lower.transpose(1, 0, 2) * (1.0 / math.sqrt(low_total))
    return low_grad, grad_upper, grad_lower


def solution(mesh):
    fine = Mesh(mesh.devices.reshape(4, 2, NZ, NY, NC), DP + SEQ)
    in_specs = (
        P(None, DP + SEQ),
        P(SEQ, None),
        P(SEQ, DP),
        P(SEQ, None),
        P(SEQ, DP),
        P(None, SEQ, DP),
        P(None, SEQ, DP),
    )
    out_specs = (P(SEQ, DP), P(None, SEQ, DP), P(None, SEQ, DP))
    return jax.shard_map(local, mesh=fine, in_specs=in_specs, out_specs=out_specs, check_vma=False)
```

time: 141 us -> 130 us (0.922)
  the two profiles are of different devices: /device:TPU:8 before, /device:TPU:2 now
where the time goes in v2:
time: 130 us; the launch traced here: 129 us
  starting transfers between devices  59.3 us (46%)
  waiting for transfers between devices  37.1 us (29%)
  Pallas kernels  14.2 us (11%)
  local copies, waits for them, and re-layouts  14.1 us (11%)
  other arithmetic  3 us (2%)
    ppermute x15, starting transfers between devices, shifted(): lax.ppermute(block, axis, [(i, (i + step) % count) for i in range(count)])  32 us
    all_to_all x1, waiting for transfers between devices, local(): lax.all_to_all(packed, ('zh', 'y'), split_axis=0, concat_axis=0, tiled=True)  24.9 us
    unnamed x36, local copies, waits for them, and re-layouts  11.7 us
    all_to_all x1, starting transfers between devices, local(): lax.all_to_all(packed, ('zh', 'y'), split_axis=0, concat_axis=0, tiled=True)  11.3 us
    ppermute x15, waiting for transfers between devices, shifted(): lax.ppermute(block, axis, [(i, (i + step) % count) for i in range(count)])  11.1 us
    all_to_all x1, starting transfers between devices, local(): lax.all_to_all(mid_part, DP, split_axis=0, concat_axis=0, tiled=True)  6.57 us
    all_to_all x1, starting transfers between devices, local(): lax.all_to_all(low_part, DP, split_axis=0, concat_axis=0, tiled=True)  5.7 us
    pallas_call x1, Pallas kernels, local(): pl.pallas_call(lower_kernel, out_shape=(jax.ShapeDtypeStruct((8, 80, 1024...  5.62 us
  transfers between devices with their start and end apart: 20, of which 7 were waited for; matrix products, arithmetic and copies ran while one was open for 6% of the time, Pallas kernels for 2%

profile of v2, /device:TPU:2, one launch (start us, length us, event | category | flops | bytes accessed | tf_op | source)
XLA Modules:
  0.0 128.8 jit_solution(6263744408711299513)
XLA Ops:
  0.6 0.8 copy-done.8
  1.5 0.8 copy-done.9
  2.2 0.8 copy-done.10
  3.0 1.4 %pack.1 = bf16[16,56,512]{2,1,0:T(8,128)(2,1)} custom-call(bf16[3,8192]{1,0:T(4,128)(2,1)S(1)} %bitcast.66, bf16[5,22,96]{2,1,0:T(8,128)(2,1)S(1)} %copy-done.9, bf16[5,20,88]{2,1,0:T(8,128)(2,1)S(1)} %copy-done.10), custom_call_target="tpu_custom_call" | custom-call | tf_op jit(solution)/shard_map/pack/pallas_call | solution.py:219
  4.4 11.3 %all-to-all-start = ((bf16[16,56,512]{2,1,0:T(8,128)(2,1)}), bf16[16,56,512]{2,1,0:T(8,128)(2,1)S(1)}, u32[]{:S(2)}, u32[]{:S(2)}) async-start(bf16[16,56,512]{2,1,0:T(8,128)(2,1)} %pack.1), calls=%async_computation | async-start | bytes 1835008 | tf_op jit(solution)/shard_map/all_to_all | solution.py:233
  15.9 24.9 %all-to-all-done.own_ref = bf16[16,56,512]{2,1,0:T(8,128)(2,1)S(1)} async-done(((bf16[16,56,512]{2,1,0:T(8,128)(2,1)}), bf16[16,56,512]{2,1,0:T(8,128)(2,1)S(1)}, u32[]{:S(2)}, u32[]{:S(2)}) %all-to-all-start) | async-done | bytes 917536 | tf_op jit(solution)/shard_map/all_to_all | solution.py:233
  40.8 2.4 %collective-permute-start = (bf16[2,96,128]{2,1,0:T(8,128)(2,1)S(1)}, bf16[2,96,128]{2,1,0:T(8,128)(2,1)S(1)}, u32[]{:S(2)}, u32[]{:S(2)}) collective-permute-start(bf16[2,96,128]{2,1,0:T(8,128)(2,1)S(1)} %get-tuple-element.44), channel_id=1, source_target_pairs={{0,1},{1,2},{2,3},{3,4},{4,5},{5,6},{6,7},{7,8},{8,9},{9,10},{10,1... | collective-permute-start | bytes 147464 | tf_op jit(solution)/shard_map/ppermute | solution.py:212
  43.3 1.3 %collective-permute-start.1 = (bf16[2,96,128]{2,1,0:T(8,128)(2,1)S(1)}, bf16[2,96,128]{2,1,0:T(8,128)(2,1)S(1)}, u32[]{:S(2)}, u32[]{:S(2)}) collective-permute-start(bf16[2,96,128]{2,1,0:T(8,128)(2,1)S(1)} %get-tuple-element.45), channel_id=1, source_target_pairs={{1,0},{2,1},{3,2},{4,3},{5,4},{6,5},{7,6},{8,7},{9,8},{10,9},{11,1... | collective-permute-start | bytes 147464 | tf_op jit(solution)/shard_map/ppermute | solution.py:213
  44.6 0.6 slice_bitcast_fusion.17
  45.3 1.1 collective-permute-done.1
  46.4 0.6 slice_bitcast_fusion.16
  47.1 2.8 %upper.1 = (bf16[8,96,512]{2,1,0:T(8,128)(2,1)}, bf16[512,512]{1,0:T(8,128)(2,1)S(1)}) custom-call(s32[3]{0:T(128)S(1)} %pad_add_fusion.pos_ref, f32[96,768]{1,0:T(8,128)S(1)} %fusion.13.slope_ref, bf16[16,56,512]{2,1,0:T(8,128)(2,1)S(1)} %all-to-all-done.own_ref, bf16[16,56,512]{2,1,0:T(8,128)(2,1)S(1)} %collective-permute-done.2.other_ref), custom_call_target="tpu_custom_call" | custom-call | tf_op jit(solution)/shard_map/upper/pallas_call | solution.py:248
  49.9 1.3 weight_grad.2
  51.2 0.9 copy-done.6
  52.0 2.5 %collective-permute-start.3 = (bf16[4,4,24,512]{3,2,1,0:T(8,128)(2,1)S(1)}, bf16[4,4,24,512]{3,2,1,0:T(8,128)(2,1)}, u32[]{:S(2)}, u32[]{:S(2)}) collective-permute-start(bf16[4,4,24,512]{3,2,1,0:T(8,128)(2,1)S(1)} %get-tuple-element.15), channel_id=1, source_target_pairs={{0,1},{1,0},{2,3},{3,2},{4,5},{5,4},{6,7},{7,6},{8,9},{9,8},{10,11... | collective-permute-start | bytes 1179656 | tf_op jit(solution)/shard_map/ppermute | solution.py:31
  54.5 6.6 %all-to-all-start.1 = ((bf16[8,96,512]{2,1,0:T(8,128)(2,1)}), bf16[8,96,512]{2,1,0:T(8,128)(2,1)}, u32[]{:S(2)}, u32[]{:S(2)}) async-start(bf16[8,96,512]{2,1,0:T(8,128)(2,1)} %get-tuple-element.11), calls=%async_computation.1 | async-start | bytes 1572864 | tf_op jit(solution)/shard_map/all_to_all | solution.py:264
  61.1 1.6 %copy.13 = bf16[1024,640]{0,1:T(8,128)(2,1)S(1)} copy(bf16[1024,640]{1,0:T(8,128)(2,1)} %param.10) | data formatting | bytes 2621440 | tf_op args[3]
  62.7 1.4 %fusion.23 = (bf16[4,4,24,512]{3,2,1,0:T(8,128)(2,1)S(1)}, f32[4,4,24,512]{3,2,1,0:T(8,128)S(1)}) fusion(f32[4,4,24,512]{3,2,1,0:T(8,128)} %copy-done.6, bf16[4,4,24,512]{3,2,1,0:T(8,128)(2,1)} %collective-permute-done.3), kind=kLoop, calls=%fused_computation.61 | loop fusion | flops 589824 | bytes 2359296 | tf_op jit(solution)/shard_map/convert.11
  64.2 0.9 collective-permute-start.4
  65.1 5.5 %collective-permute-start.6 = (bf16[4,24,512]{2,1,0:T(8,128)(2,1)S(1)}, bf16[4,24,512]{2,1,0:T(8,128)(2,1)S(1)}, u32[]{:S(2)}, u32[]{:S(2)}) collective-permute-start(bf16[4,24,512]{2,1,0:T(8,128)(2,1)S(1)} %get-tuple-element.34), channel_id=1, source_target_pairs={{0,6},{2,0},{4,2},{6,4},{1,7},{3,1},{5,3},{7,5},{8,14},{10,8},{12,... | collective-permute-start | bytes 294920 | tf_op jit(solution)/shard_map/ppermute | solution.py:31
  70.6 1.4 %collective-permute-start.5 = (bf16[4,24,512]{2,1,0:T(8,128)(2,1)S(1)}, bf16[4,24,512]{2,1,0:T(8,128)(2,1)S(1)}, u32[]{:S(2)}, u32[]{:S(2)}) collective-permute-start(bf16[4,24,512]{2,1,0:T(8,128)(2,1)S(1)} %get-tuple-element.35), channel_id=1, source_target_pairs={{0,4},{2,6},{4,0},{6,2},{1,5},{3,7},{5,1},{7,3},{8,12},{10,14},{12... | collective-permute-start | bytes 294920 | tf_op jit(solution)/shard_map/ppermute | solution.py:31
  72.0 1.0 fusion.6.slope_ref
  73.0 0.8 lower_weight.1.w_ref
  73.8 0.8 copy-done
  74.6 2.1 %collective-permute-done.5 = bf16[4,24,512]{2,1,0:T(8,128)(2,1)S(1)} collective-permute-done((bf16[4,24,512]{2,1,0:T(8,128)(2,1)S(1)}, bf16[4,24,512]{2,1,0:T(8,128)(2,1)S(1)}, u32[]{:S(2)}, u32[]{:S(2)}) %collective-permute-start.5) | collective-permute-done | bytes 98336 | tf_op jit(solution)/shard_map/ppermute | solution.py:31
  76.8 1.1 copy-done.1
  77.9 1.0 copy-done.2
  78.9 5.6 %lower.1 = (bf16[8,80,1024]{2,1,0:T(8,128)(2,1)S(1)}, bf16[512,1024]{1,0:T(8,128)(2,1)S(1)}) custom-call(s32[3]{0:T(128)S(1)} %pad_add_fusion.pos_ref, bf16[8,96,512]{2,1,0:T(8,128)(2,1)} %all-to-all-done.1.mid_ref, f32[96,1280]{1,0:T(8,128)S(1)} %copy-done.2, bf16[640,512]{1,0:T(8,128)(2,1)S(1)} %copy-done.1), custom_call_target="tpu_custom_call" | custom-call | tf_op jit(solution)/shard_map/lower/pallas_call | solution.py:277
  84.6 1.1 copy-done.3
  85.7 1.0 copy-done.4
  86.6 5.7 %all-to-all-start.2 = ((bf16[8,80,1024]{2,1,0:T(8,128)(2,1)}), bf16[8,80,1024]{2,1,0:T(8,128)(2,1)S(1)}, u32[]{:S(2)}, u32[]{:S(2)}) async-start(bf16[8,80,1024]{2,1,0:T(8,128)(2,1)} %copy-done.3), calls=%async_computation.2 | async-start | bytes 2621440 | tf_op jit(solution)/shard_map/all_to_all | solution.py:286
  92.3 1.2 copy-done.5
  93.6 1.6 %weight_grad.3 = (f32[4,4,24,512]{3,2,1,0:T(8,128)S(1)}, bf16[4,4,24,512]{3,2,1,0:T(8,128)(2,1)S(1)}) custom-call(s32[3]{0:T(128)S(1)} %pad_add_fusion.pos_ref, bf16[640,1024]{1,0:T(8,128)(2,1)S(1)} %bitcast.64, bf16[512,1024]{1,0:T(8,128)(2,1)S(1)} %copy-done.5), custom_call_target="tpu_custom_call" | custom-call | tf_op jit(solution)/shard_map/weight_grad/pallas_call | solution.py:197
  95.2 3.7 %collective-permute-start.7 = (bf16[24,512]{1,0:T(8,128)(2,1)S(1)}, bf16[24,512]{1,0:T(8,128)(2,1)S(1)}, u32[]{:S(2)}, u32[]{:S(2)}) collective-permute-start(bf16[24,512]{1,0:T(8,128)(2,1)S(1)} %get-tuple-element.41), channel_id=1, source_target_pairs={{0,8},{8,16},{16,24},{24,0},{1,9},{9,17},{17,25},{25,1},{2,10},{10... | collective-permute-start | bytes 73736 | tf_op jit(solution)/shard_map/ppermute | solution.py:31
  98.9 0.6 collective-permute-start.9
  99.5 3.4 %collective-permute-start.8 = (bf16[24,512]{1,0:T(8,128)(2,1)S(1)}, bf16[24,512]{1,0:T(8,128)(2,1)S(1)}, u32[]{:S(2)}, u32[]{:S(2)}) collective-permute-start(bf16[24,512]{1,0:T(8,128)(2,1)S(1)} %get-tuple-element.43), channel_id=1, source_target_pairs={{0,16},{8,24},{16,0},{24,8},{1,17},{9,25},{17,1},{25,9},{2,18},{10... | collective-permute-start | bytes 73736 | tf_op jit(solution)/shard_map/ppermute | solution.py:31
  103.1 0.8 collective-permute-start.11
  103.9 2.5 %collective-permute-start.13 = (bf16[4,24,512]{2,1,0:T(8,128)(2,1)S(1)}, bf16[4,24,512]{2,1,0:T(8,128)(2,1)S(1)}, u32[]{:S(2)}, u32[]{:S(2)}) collective-permute-start(bf16[4,24,512]{2,1,0:T(8,128)(2,1)S(1)} %get-tuple-element.31), channel_id=1, source_target_pairs={{0,6},{2,0},{4,2},{6,4},{1,7},{3,1},{5,3},{7,5},{8,14},{10,8},{12,... | collective-permute-start | bytes 294920 | tf_op jit(solution)/shard_map/ppermute | solution.py:31
  106.4 2.1 %collective-permute-done.7 = bf16[24,512]{1,0:T(8,128)(2,1)S(1)} collective-permute-done((bf16[24,512]{1,0:T(8,128)(2,1)S(1)}, bf16[24,512]{1,0:T(8,128)(2,1)S(1)}, u32[]{:S(2)}, u32[]{:S(2)}) %collective-permute-start.7) | collective-permute-done | bytes 24608 | tf_op jit(solution)/shard_map/ppermute | solution.py:31
  108.9 1.7 %collective-permute-done.8 = bf16[24,512]{1,0:T(8,128)(2,1)S(1)} collective-permute-done((bf16[24,512]{1,0:T(8,128)(2,1)S(1)}, bf16[24,512]{1,0:T(8,128)(2,1)S(1)}, u32[]{:S(2)}, u32[]{:S(2)}) %collective-permute-start.8) | collective-permute-done | bytes 24608 | tf_op jit(solution)/shard_map/ppermute | solution.py:31
  110.8 0.6 copy.15
  111.4 3.3 %collective-permute-done.12 = bf16[4,24,512]{2,1,0:T(8,128)(2,1)S(1)} collective-permute-done((bf16[4,24,512]{2,1,0:T(8,128)(2,1)S(1)}, bf16[4,24,512]{2,1,0:T(8,128)(2,1)S(1)}, u32[]{:S(2)}, u32[]{:S(2)}) %collective-permute-start.12) | collective-permute-done | bytes 98336 | tf_op jit(solution)/shard_map/ppermute | solution.py:31
  114.7 2.2 %collective-permute-start.14 = (bf16[24,512]{1,0:T(8,128)(2,1)S(1)}, bf16[24,512]{1,0:T(8,128)(2,1)S(1)}, u32[]{:S(2)}, u32[]{:S(2)}) collective-permute-start(bf16[24,512]{1,0:T(8,128)(2,1)S(1)} %get-tuple-element.38), channel_id=1, source_target_pairs={{0,8},{8,16},{16,24},{24,0},{1,9},{9,17},{17,25},{25,1},{2,10},{10... | collective-permute-start | bytes 73736 | tf_op jit(solution)/shard_map/ppermute | solution.py:31
  116.9 2.1 %collective-permute-start.16 = (bf16[24,512]{1,0:T(8,128)(2,1)S(1)}, bf16[24,512]{1,0:T(8,128)(2,1)S(1)}, u32[]{:S(2)}, u32[]{:S(2)}) collective-permute-start(bf16[24,512]{1,0:T(8,128)(2,1)S(1)} %get-tuple-element.39), channel_id=1, source_target_pairs={{0,24},{8,0},{16,8},{24,16},{1,25},{9,1},{17,9},{25,17},{2,26},{10... | collective-permute-start | bytes 73736 | tf_op jit(solution)/shard_map/ppermute | solution.py:31
  119.0 6.1 %collective-permute-start.15 = (bf16[24,512]{1,0:T(8,128)(2,1)S(1)}, bf16[24,512]{1,0:T(8,128)(2,1)S(1)}, u32[]{:S(2)}, u32[]{:S(2)}) collective-permute-start(bf16[24,512]{1,0:T(8,128)(2,1)S(1)} %get-tuple-element.40), channel_id=1, source_target_pairs={{0,16},{8,24},{16,0},{24,8},{1,17},{9,25},{17,1},{25,9},{2,18},{10... | collective-permute-start | bytes 73736 | tf_op jit(solution)/shard_map/ppermute | solution.py:31
  125.1 1.8 %collective-permute-done.15 = bf16[24,512]{1,0:T(8,128)(2,1)S(1)} collective-permute-done((bf16[24,512]{1,0:T(8,128)(2,1)S(1)}, bf16[24,512]{1,0:T(8,128)(2,1)S(1)}, u32[]{:S(2)}, u32[]{:S(2)}) %collective-permute-start.15) | collective-permute-done | bytes 24608 | tf_op jit(solution)/shard_map/ppermute | solution.py:31
  127.3 0.6 copy.18
  127.9 0.8 low_total.1
  (63 shorter events, 1.7 us)
Async XLA Ops:
  0.6 0.8 copy-start.8
  1.5 0.8 copy-start.9
  2.2 0.8 copy-start.10
  3.0 12.8 %copy-start.14 = (bf16[1024,88]{0,1:T(8,128)(2,1)S(1)}, bf16[1024,88]{0,1:T(8,128)(2,1)}, u32[]{:S(2)}) copy-start(bf16[1024,88]{0,1:T(8,128)(2,1)} %param.11) | copy-start | bytes 540676
  4.4 11.5 %copy-start.13 = (bf16[512,96]{0,1:T(8,128)(2,1)S(1)}, bf16[512,96]{0,1:T(8,128)(2,1)}, u32[]{:S(2)}) copy-start(bf16[512,96]{0,1:T(8,128)(2,1)} %param.9) | copy-start | bytes 294916
  4.4 36.4 %all-to-all-start = ((bf16[16,56,512]{2,1,0:T(8,128)(2,1)}), bf16[16,56,512]{2,1,0:T(8,128)(2,1)S(1)}, u32[]{:S(2)}, u32[]{:S(2)}) async-start(bf16[16,56,512]{2,1,0:T(8,128)(2,1)} %pack.1), calls=%async_computation | async-start | bytes 1835008 | tf_op jit(solution)/shard_map/all_to_all | solution.py:233
  15.9 28.7 %copy-start.11 = (bf16[4,24,1024]{2,1,0:T(8,128)(2,1)}, bf16[4,24,1024]{2,1,0:T(8,128)(2,1)S(1)}, u32[]{:S(2)}) copy-start(bf16[4,24,1024]{2,1,0:T(8,128)(2,1)S(1)} %pad.4) | copy-start | bytes 589828
  40.8 6.4 %collective-permute-start.2 = (bf16[16,56,512]{2,1,0:T(8,128)(2,1)S(1)}, bf16[16,56,512]{2,1,0:T(8,128)(2,1)S(1)}, u32[]{:S(2)}, u32[]{:S(2)}) collective-permute-start(bf16[16,56,512]{2,1,0:T(8,128)(2,1)S(1)} %all-to-all-done.own_ref), channel_id=1, source_target_pairs={{0,1},{1,0},{2,3},{3,2},{4,5},{5,4},{6,7},{7,6},{8,9},{9,8},{10,11... | collective-permute-start | bytes 2752520 | tf_op jit(solution)/shard_map/ppermute | solution.py:31
  40.8 3.8 %collective-permute-start = (bf16[2,96,128]{2,1,0:T(8,128)(2,1)S(1)}, bf16[2,96,128]{2,1,0:T(8,128)(2,1)S(1)}, u32[]{:S(2)}, u32[]{:S(2)}) collective-permute-start(bf16[2,96,128]{2,1,0:T(8,128)(2,1)S(1)} %get-tuple-element.44), channel_id=1, source_target_pairs={{0,1},{1,2},{2,3},{3,4},{4,5},{5,6},{6,7},{7,8},{8,9},{9,10},{10,1... | collective-permute-start | bytes 147464 | tf_op jit(solution)/shard_map/ppermute | solution.py:212
  43.3 3.1 %collective-permute-start.1 = (bf16[2,96,128]{2,1,0:T(8,128)(2,1)S(1)}, bf16[2,96,128]{2,1,0:T(8,128)(2,1)S(1)}, u32[]{:S(2)}, u32[]{:S(2)}) collective-permute-start(bf16[2,96,128]{2,1,0:T(8,128)(2,1)S(1)} %get-tuple-element.45), channel_id=1, source_target_pairs={{1,0},{2,1},{3,2},{4,3},{5,4},{6,5},{7,6},{8,7},{9,8},{10,9},{11,1... | collective-permute-start | bytes 147464 | tf_op jit(solution)/shard_map/ppermute | solution.py:213
  47.0 2.9 %copy-start.7 = (bf16[512,704]{0,1:T(8,128)(2,1)S(1)}, bf16[512,704]{0,1:T(8,128)(2,1)}, u32[]{:S(2)}) copy-start(bf16[512,704]{0,1:T(8,128)(2,1)} %param.8) | copy-start | bytes 2162692
  51.2 0.9 copy-start.6
  52.0 10.7 %collective-permute-start.3 = (bf16[4,4,24,512]{3,2,1,0:T(8,128)(2,1)S(1)}, bf16[4,4,24,512]{3,2,1,0:T(8,128)(2,1)}, u32[]{:S(2)}, u32[]{:S(2)}) collective-permute-start(bf16[4,4,24,512]{3,2,1,0:T(8,128)(2,1)S(1)} %get-tuple-element.15), channel_id=1, source_target_pairs={{0,1},{1,0},{2,3},{3,2},{4,5},{5,4},{6,7},{7,6},{8,9},{9,8},{10,11... | collective-permute-start | bytes 1179656 | tf_op jit(solution)/shard_map/ppermute | solution.py:31
  54.5 22.3 %all-to-all-start.1 = ((bf16[8,96,512]{2,1,0:T(8,128)(2,1)}), bf16[8,96,512]{2,1,0:T(8,128)(2,1)}, u32[]{:S(2)}, u32[]{:S(2)}) async-start(bf16[8,96,512]{2,1,0:T(8,128)(2,1)} %get-tuple-element.11), calls=%async_computation.1 | async-start | bytes 1572864 | tf_op jit(solution)/shard_map/all_to_all | solution.py:264
  62.7 9.3 %copy-start.12 = (bf16[4,24,1024]{2,1,0:T(8,128)(2,1)S(1)}, bf16[4,24,1024]{2,1,0:T(8,128)(2,1)}, u32[]{:S(2)}) copy-start(bf16[4,24,1024]{2,1,0:T(8,128)(2,1)} %copy-done.11) | copy-start | bytes 589828
  62.7 9.3 %copy-start.15 = (bf16[96,128]{1,0:T(8,128)(2,1)S(1)}, bf16[96,128]{1,0:T(8,128)(2,1)}, u32[]{:S(2)}) copy-start(bf16[96,128]{1,0:T(8,128)(2,1)} %get-tuple-element.48) | copy-start | bytes 73732
  62.7 9.3 %copy-start.16 = (bf16[96,128]{1,0:T(8,128)(2,1)S(1)}, bf16[96,128]{1,0:T(8,128)(2,1)}, u32[]{:S(2)}) copy-start(bf16[96,128]{1,0:T(8,128)(2,1)} %get-tuple-element.50) | copy-start | bytes 73732
  64.2 10.4 %collective-permute-start.4 = (bf16[4,24,512]{2,1,0:T(8,128)(2,1)S(1)}, bf16[4,24,512]{2,1,0:T(8,128)(2,1)S(1)}, u32[]{:S(2)}, u32[]{:S(2)}) collective-permute-start(bf16[4,24,512]{2,1,0:T(8,128)(2,1)S(1)} %get-tuple-element.33), channel_id=1, source_target_pairs={{0,2},{2,4},{4,6},{6,0},{1,3},{3,5},{5,7},{7,1},{8,10},{10,12},{12... | collective-permute-start | bytes 294920 | tf_op jit(solution)/shard_map/ppermute | solution.py:31
  65.1 9.5 %collective-permute-start.6 = (bf16[4,24,512]{2,1,0:T(8,128)(2,1)S(1)}, bf16[4,24,512]{2,1,0:T(8,128)(2,1)S(1)}, u32[]{:S(2)}, u32[]{:S(2)}) collective-permute-start(bf16[4,24,512]{2,1,0:T(8,128)(2,1)S(1)} %get-tuple-element.34), channel_id=1, source_target_pairs={{0,6},{2,0},{4,2},{6,4},{1,7},{3,1},{5,3},{7,5},{8,14},{10,8},{12,... | collective-permute-start | bytes 294920 | tf_op jit(solution)/shard_map/ppermute | solution.py:31
  70.6 6.1 %collective-permute-start.5 = (bf16[4,24,512]{2,1,0:T(8,128)(2,1)S(1)}, bf16[4,24,512]{2,1,0:T(8,128)(2,1)S(1)}, u32[]{:S(2)}, u32[]{:S(2)}) collective-permute-start(bf16[4,24,512]{2,1,0:T(8,128)(2,1)S(1)} %get-tuple-element.35), channel_id=1, source_target_pairs={{0,4},{2,6},{4,0},{6,2},{1,5},{3,7},{5,1},{7,3},{8,12},{10,14},{12... | collective-permute-start | bytes 294920 | tf_op jit(solution)/shard_map/ppermute | solution.py:31
  73.8 0.8 copy-start
  76.8 1.1 copy-start.1
  77.9 1.0 copy-start.2
  84.5 1.1 copy-start.3
  85.7 1.0 copy-start.4
  86.6 41.3 %all-to-all-start.2 = ((bf16[8,80,1024]{2,1,0:T(8,128)(2,1)}), bf16[8,80,1024]{2,1,0:T(8,128)(2,1)S(1)}, u32[]{:S(2)}, u32[]{:S(2)}) async-start(bf16[8,80,1024]{2,1,0:T(8,128)(2,1)} %copy-done.3), calls=%async_computation.2 | async-start | bytes 2621440 | tf_op jit(solution)/shard_map/all_to_all | solution.py:286
  92.3 1.2 copy-start.5
  95.1 7.8 %collective-permute-start.10 = (bf16[4,4,24,512]{3,2,1,0:T(8,128)(2,1)S(1)}, bf16[4,4,24,512]{3,2,1,0:T(8,128)(2,1)S(1)}, u32[]{:S(2)}, u32[]{:S(2)}) collective-permute-start(bf16[4,4,24,512]{3,2,1,0:T(8,128)(2,1)S(1)} %get-tuple-element.18), channel_id=1, source_target_pairs={{0,1},{1,0},{2,3},{3,2},{4,5},{5,4},{6,7},{7,6},{8,9},{9,8},{10,11... | collective-permute-start | bytes 1179656 | tf_op jit(solution)/shard_map/ppermute | solution.py:31
  95.2 13.3 %collective-permute-start.7 = (bf16[24,512]{1,0:T(8,128)(2,1)S(1)}, bf16[24,512]{1,0:T(8,128)(2,1)S(1)}, u32[]{:S(2)}, u32[]{:S(2)}) collective-permute-start(bf16[24,512]{1,0:T(8,128)(2,1)S(1)} %get-tuple-element.41), channel_id=1, source_target_pairs={{0,8},{8,16},{16,24},{24,0},{1,9},{9,17},{17,25},{25,1},{2,10},{10... | collective-permute-start | bytes 73736 | tf_op jit(solution)/shard_map/ppermute | solution.py:31
  98.9 10.0 %collective-permute-start.9 = (bf16[24,512]{1,0:T(8,128)(2,1)S(1)}, bf16[24,512]{1,0:T(8,128)(2,1)S(1)}, u32[]{:S(2)}, u32[]{:S(2)}) collective-permute-start(bf16[24,512]{1,0:T(8,128)(2,1)S(1)} %get-tuple-element.42), channel_id=1, source_target_pairs={{0,24},{8,0},{16,8},{24,16},{1,25},{9,1},{17,9},{25,17},{2,26},{10... | collective-permute-start | bytes 73736 | tf_op jit(solution)/shard_map/ppermute | solution.py:31
  99.5 11.2 %collective-permute-start.8 = (bf16[24,512]{1,0:T(8,128)(2,1)S(1)}, bf16[24,512]{1,0:T(8,128)(2,1)S(1)}, u32[]{:S(2)}, u32[]{:S(2)}) collective-permute-start(bf16[24,512]{1,0:T(8,128)(2,1)S(1)} %get-tuple-element.43), channel_id=1, source_target_pairs={{0,16},{8,24},{16,0},{24,8},{1,17},{9,25},{17,1},{25,9},{2,18},{10... | collective-permute-start | bytes 73736 | tf_op jit(solution)/shard_map/ppermute | solution.py:31
  103.1 8.3 %collective-permute-start.11 = (bf16[4,24,512]{2,1,0:T(8,128)(2,1)S(1)}, bf16[4,24,512]{2,1,0:T(8,128)(2,1)S(1)}, u32[]{:S(2)}, u32[]{:S(2)}) collective-permute-start(bf16[4,24,512]{2,1,0:T(8,128)(2,1)S(1)} %get-tuple-element.30), channel_id=1, source_target_pairs={{0,2},{2,4},{4,6},{6,0},{1,3},{3,5},{5,7},{7,1},{8,10},{10,12},{12... | collective-permute-start | bytes 294920 | tf_op jit(solution)/shard_map/ppermute | solution.py:31
  103.9 7.5 %collective-permute-start.13 = (bf16[4,24,512]{2,1,0:T(8,128)(2,1)S(1)}, bf16[4,24,512]{2,1,0:T(8,128)(2,1)S(1)}, u32[]{:S(2)}, u32[]{:S(2)}) collective-permute-start(bf16[4,24,512]{2,1,0:T(8,128)(2,1)S(1)} %get-tuple-element.31), channel_id=1, source_target_pairs={{0,6},{2,0},{4,2},{6,4},{1,7},{3,1},{5,3},{7,5},{8,14},{10,8},{12,... | collective-permute-start | bytes 294920 | tf_op jit(solution)/shard_map/ppermute | solution.py:31
  108.5 6.1 %collective-permute-start.12 = (bf16[4,24,512]{2,1,0:T(8,128)(2,1)S(1)}, bf16[4,24,512]{2,1,0:T(8,128)(2,1)S(1)}, u32[]{:S(2)}, u32[]{:S(2)}) collective-permute-start(bf16[4,24,512]{2,1,0:T(8,128)(2,1)S(1)} %get-tuple-element.32), channel_id=1, source_target_pairs={{0,4},{2,6},{4,0},{6,2},{1,5},{3,7},{5,1},{7,3},{8,12},{10,14},{12... | collective-permute-start | bytes 294920 | tf_op jit(solution)/shard_map/ppermute | solution.py:31
  114.7 10.3 %collective-permute-start.14 = (bf16[24,512]{1,0:T(8,128)(2,1)S(1)}, bf16[24,512]{1,0:T(8,128)(2,1)S(1)}, u32[]{:S(2)}, u32[]{:S(2)}) collective-permute-start(bf16[24,512]{1,0:T(8,128)(2,1)S(1)} %get-tuple-element.38), channel_id=1, source_target_pairs={{0,8},{8,16},{16,24},{24,0},{1,9},{9,17},{17,25},{25,1},{2,10},{10... | collective-permute-start | bytes 73736 | tf_op jit(solution)/shard_map/ppermute | solution.py:31
  116.9 8.2 %collective-permute-start.16 = (bf16[24,512]{1,0:T(8,128)(2,1)S(1)}, bf16[24,512]{1,0:T(8,128)(2,1)S(1)}, u32[]{:S(2)}, u32[]{:S(2)}) collective-permute-start(bf16[24,512]{1,0:T(8,128)(2,1)S(1)} %get-tuple-element.39), channel_id=1, source_target_pairs={{0,24},{8,0},{16,8},{24,16},{1,25},{9,1},{17,9},{25,17},{2,26},{10... | collective-permute-start | bytes 73736 | tf_op jit(solution)/shard_map/ppermute | solution.py:31
  119.0 7.9 %collective-permute-start.15 = (bf16[24,512]{1,0:T(8,128)(2,1)S(1)}, bf16[24,512]{1,0:T(8,128)(2,1)S(1)}, u32[]{:S(2)}, u32[]{:S(2)}) collective-permute-start(bf16[24,512]{1,0:T(8,128)(2,1)S(1)} %get-tuple-element.40), channel_id=1, source_target_pairs={{0,16},{8,24},{16,0},{24,8},{1,17},{9,25},{17,1},{25,9},{2,18},{10... | collective-permute-start | bytes 73736 | tf_op jit(solution)/shard_map/ppermute | solution.py:31

commit v3 on v2

--- a/solution.py
+++ b/solution.py
@@ -1,3 +1,4 @@
+import functools
 import math
 
 import jax
@@ -14,7 +15,7 @@
 NZ, NY, NC = 4, 4, 2
 BF = jnp.bfloat16
 F32 = jnp.float32
-PARAMS = pltpu.CompilerParams(vmem_limit_bytes=40 * 1024 * 1024)
+PARAMS = pltpu.CompilerParams(vmem_limit_bytes=16 * 1024 * 1024)
 VMEM = pl.BlockSpec(memory_space=pltpu.VMEM)
 SMEM = pl.BlockSpec(memory_space=pltpu.SMEM)
 HBM = pl.BlockSpec(memory_space=pltpu.HBM)
@@ -31,12 +32,89 @@
     return lax.ppermute(block, axis, [(i, (i + step) % count) for i in range(count)])
 
 
-def scatter_rows(keep, send):
-    total = keep + shifted(send, "c", NC, 1).astype(F32)
-    parts = [shifted(total[s].astype(BF), "y", NY, s) for s in range(1, NY)]
-    total = total[0] + sum(p.astype(F32) for p in parts)
-    parts = [shifted(total[s].astype(BF), "zh", NZ, s) for s in range(1, NZ)]
-    return total[0] + sum(p.astype(F32) for p in parts)
+def join_kernel(*refs):
+    out_ref = refs[-1]
+    for s in range(NY):
+        out_ref[NZ * s : NZ * s + NZ] = refs[s][...]
+
+
+def join(levels):
+    shape = (NY * NZ,) + levels[0].shape[1:]
+    return pl.pallas_call(
+        join_kernel,
+        out_shape=jax.ShapeDtypeStruct(shape, BF),
+        in_specs=[VMEM] * NY,
+        out_specs=VMEM,
+        compiler_params=PARAMS,
+        name="join",
+    )(*levels)
+
+
+def core_sum_kernel(keep_upper_ref, got_upper_ref, keep_lower_ref, got_lower_ref, own_ref, *send_refs):
+    pairs = ((keep_upper_ref, got_upper_ref), (keep_lower_ref, got_lower_ref))
+    for half, (keep_ref, got_ref) in enumerate(pairs):
+        rows = slice(24 * half, 24 * half + 24)
+        for s in range(NY):
+            for z in range(NZ):
+                total = keep_ref[s, z] + got_ref[s, z].astype(F32)
+                if s == 0:
+                    own_ref[z, rows] = total
+                else:
+                    send_refs[s - 1][z, rows] = total.astype(BF)
+
+
+def y_sum_kernel(own_ref, *refs):
+    got_refs, total_ref, send_refs = refs[: NY - 1], refs[NY - 1], refs[NY:]
+    for z in range(NZ):
+        total = own_ref[z]
+        for got_ref in got_refs:
+            total = total + got_ref[z].astype(F32)
+        if z == 0:
+            total_ref[...] = total
+        else:
+            send_refs[z - 1][...] = total.astype(BF)
+
+
+def z_sum_kernel(scales, own_ref, *refs):
+    got_refs, upper_ref, lower_ref = refs[: NZ - 1], refs[NZ - 1], refs[NZ]
+    total = own_ref[...]
+    for got_ref in got_refs:
+        total = total + got_ref[...].astype(F32)
+    lane = lax.broadcasted_iota(jnp.int32, (24, 512), 1)
+    for k in range(KWIDTH):
+        upper_ref[k] = pltpu.roll(total[0:24], (512 - 96 * k) % 512, 1)[0:22, 0:96] * scales[0]
+        lower = pltpu.roll(total[24:48], (512 - 96 * k) % 512, 1)
+        packed = lower
+        for group in range(1, 4):
+            packed = jnp.where(lane >= 22 * group, pltpu.roll(lower, 512 - 2 * group, 1), packed)
+        lower_ref[k] = packed[0:20, 0:88] * scales[1]
+
+
+def small_call(kernel, name, out_shape, *operands):
+    return pl.pallas_call(
+        kernel,
+        out_shape=out_shape,
+        in_specs=[VMEM] * len(operands),
+        out_specs=tuple(VMEM for _ in out_shape),
+        compiler_params=PARAMS,
+        name=name,
+    )(*operands)
+
+
+def core_sum(upper, lower):
+    level = jax.ShapeDtypeStruct((NZ, 48, 512), BF)
+    outs = (jax.ShapeDtypeStruct(level.shape, F32),) + (level,) * (NY - 1)
+    return small_call(core_sum_kernel, "core_sum", outs, *upper, *lower)
+
+
+def z_sum(own, got, scales, upper_shape, lower_shape):
+    block = jax.ShapeDtypeStruct((48, 512), BF)
+    own, *sends = small_call(
+        y_sum_kernel, "y_sum", (jax.ShapeDtypeStruct(block.shape, F32),) + (block,) * (NZ - 1), own, *got
+    )
+    got = [shifted(send, "zh", NZ, s + 1) for s, send in enumerate(sends)]
+    outs = (jax.ShapeDtypeStruct(upper_shape, F32), jax.ShapeDtypeStruct(lower_shape, F32))
+    return small_call(functools.partial(z_sum_kernel, scales), "z_sum", outs, own, *got)
 
 
 def doubling():
@@ -59,11 +137,23 @@
     return (place == col).astype(F32).astype(BF)
 
 
-def pack_kernel(tower_ref, upper_ref, lower_ref, out_ref, weight_ref, tower_rows_ref, buf_ref, sem):
+def pack_kernel(
+    tower_hbm, upper_hbm, lower_hbm, out_ref, lower_out_ref,
+    tower_ref, upper_ref, lower_ref, weight_ref, tower_rows_ref, buf_ref, sem, in_sem,
+):
+    copies = [
+        pltpu.make_async_copy(source, target, in_sem.at[i])
+        for i, (source, target) in enumerate(((upper_hbm, upper_ref), (lower_hbm, lower_ref), (tower_hbm, tower_ref)))
+    ]
+    for copy in copies:
+        copy.start()
+    for copy in copies:
+        copy.wait()
     weight_ref[...] = jnp.zeros((48, 512), F32)
     weight_ref[0:22, :] = sum(mm(upper_ref[k], one_hot(96, 96 * k, False)) for k in range(KWIDTH))
     weight_ref[24:44, :] = sum(mm(lower_ref[k], one_hot(88, 96 * k, True)) for k in range(KWIDTH))
-    weight = weight_ref[...].astype(BF)
+    weight = weight_ref[0:24, :].astype(BF)
+    lower_out_ref[...] = weight_ref[24:48, :].astype(BF)
     tower = tower_ref[...].astype(F32)
     tower_rows_ref[...] = jnp.zeros((128, 512), F32)
     for p in range(16):
@@ -75,8 +165,8 @@
         tower_rows_ref[row + 3 : row + 6, 256:384] = tower[:, at + 128 : at + 256]
         if p < 15:
             tower_rows_ref[row + 3 : row + 6, 384:512] = tower[:, at + 512 : at + 640]
-        buf_ref[p, 0:48, :] = weight
-        buf_ref[p, 48:56, :] = tower_rows_ref[row : row + 8, :].astype(BF)
+        buf_ref[p, 0:24, :] = weight
+        buf_ref[p, 24:32, :] = tower_rows_ref[row : row + 8, :].astype(BF)
         pltpu.make_async_copy(buf_ref.at[p], out_ref.at[p], sem.at[p]).start()
     for p in range(16):
         pltpu.make_async_copy(buf_ref.at[p], out_ref.at[p], sem.at[p]).wait()
@@ -87,7 +177,7 @@
 ):
     first = pos_ref[2] == 0
     for p in range(16):
-        own, other = own_ref[p, 48:56, :].astype(F32), other_ref[p, 48:56, :].astype(F32)
+        own, other = own_ref[p, 24:32, :].astype(F32), other_ref[p, 24:32, :].astype(F32)
         for j in range(2):
             rows = jnp.where(first, own, other) if j == 0 else jnp.where(first, other, own)
             rows = jnp.where(first, rows[:, 0:256], rows[:, 256:512])
@@ -121,12 +211,17 @@
     outside = lax.dot_general(
         halo_ref[...].T.astype(BF), w_ref[...], (((1,), (1,)), ((), ())), preferred_element_type=F32
     )[120:128]
-    row = lax.broadcasted_iota(jnp.int32, (8, 512), 0)
-    taps = taps_ref[...]
+    row = lax.broadcasted_iota(jnp.int32, (8, 256), 0)
+    for half in range(2):
+        lanes = slice(256 * half, 256 * half + 256)
+        mid = mm(w_ref[...], taps_ref[:, lanes])
+        for d in range(8):
+            part = mid[96 * d : 96 * d + 96]
+            if half == 0:
+                moved = pltpu.roll(outside, (768 - 96 * d) % 768, 1)[:, 0:256]
+                part = jnp.concatenate([part[0:16], jnp.where(row >= 6, moved, part[16:24]), part[24:]], axis=0)
+            buf_ref[d, :, lanes] = part.astype(BF)
     for d in range(8):
-        mid = mm(w_ref[96 * d : 96 * d + 96, :], taps)
-        moved = pltpu.roll(outside, (768 - 96 * d) % 768, 1)[:, 0:512]
-        buf_ref[d] = jnp.concatenate([mid[0:16], jnp.where(row >= 6, moved, mid[16:24]), mid[24:]], axis=0).astype(BF)
         pltpu.make_async_copy(buf_ref.at[d], mid_ref.at[d], sem.at[d]).start()
     for d in range(8):
         pltpu.make_async_copy(buf_ref.at[d], mid_ref.at[d], sem.at[d]).wait()
@@ -135,7 +230,8 @@
 def lower_weight_kernel(pos_ref, own_ref, other_ref, out_ref, rows_ref):
     first = pos_ref[2] == 0
     for p in range(16):
-        own, other = own_ref[p, 24:48, :].astype(F32), other_ref[p, 24:48, :].astype(F32)
+        slot = lax.rem(pos_ref[1] - p % NY + NY, NY) * NZ + lax.rem(pos_ref[0] - p // NY + NZ, NZ)
+        own, other = own_ref[slot].astype(F32), other_ref[slot].astype(F32)
         rows_ref[40 * p : 40 * p + 24, :] = jnp.where(first, own, other)
         rows_ref[40 * p + 20 : 40 * p + 44, :] = jnp.where(first, other, own)
     out_ref[...] = rows_ref[0:640, :].astype(BF)
@@ -159,12 +255,15 @@
     for k in range(KWIDTH):
         moved = pltpu.roll(grad, 1280 - (130 - k), 1)
         taps_ref[96 * k : 96 * k + 96, :] = moved[:, 0:1024].astype(BF)
-    taps = taps_ref[...]
-    for d in range(8):
-        buf_ref[d] = mm(w_ref[80 * d : 80 * d + 80, :], taps).astype(BF)
-        pltpu.make_async_copy(buf_ref.at[d], low_ref.at[d], sem.at[d]).start()
-    for d in range(8):
-        pltpu.make_async_copy(buf_ref.at[d], low_ref.at[d], sem.at[d]).wait()
+    for quarter in range(4):
+        lanes = slice(256 * quarter, 256 * quarter + 256)
+        low = mm(w_ref[...], taps_ref[:, lanes])
+        for d in range(8):
+            buf_ref[d, :, lanes] = low[80 * d : 80 * d + 80].astype(BF)
+        pltpu.make_async_copy(buf_ref.at[:, :, lanes], low_ref.at[:, :, lanes], sem.at[quarter]).start()
+    for quarter in range(4):
+        lanes = slice(256 * quarter, 256 * quarter + 256)
+        pltpu.make_async_copy(buf_ref.at[:, :, lanes], low_ref.at[:, :, lanes], sem.at[quarter]).wait()
 
 
 def total_kernel(low_ref, out_ref):
@@ -216,23 +315,24 @@
 
 def local(tower_grad, act_mid, pre_mid, act_low, pre_low, weight_upper, weight_lower):
     pos = jnp.stack([lax.axis_index("zh"), lax.axis_index("y"), lax.axis_index("c")]).astype(jnp.int32)
-    packed = pl.pallas_call(
+    packed, lower_block = pl.pallas_call(
         pack_kernel,
-        out_shape=jax.ShapeDtypeStruct((16, 56, 512), BF),
-        in_specs=[VMEM] * 3,
-        out_specs=HBM,
+        out_shape=(jax.ShapeDtypeStruct((16, 32, 512), BF), jax.ShapeDtypeStruct((24, 512), BF)),
+        in_specs=[HBM] * 3,
+        out_specs=(HBM, VMEM),
         scratch_shapes=[
+            pltpu.VMEM((3, 8192), BF),
+            pltpu.VMEM(weight_upper.shape, BF),
+            pltpu.VMEM(weight_lower.shape, BF),
             pltpu.VMEM((48, 512), F32),
             pltpu.VMEM((128, 512), F32),
-            pltpu.VMEM((16, 56, 512), BF),
+            pltpu.VMEM((16, 32, 512), BF),
             pltpu.SemaphoreType.DMA((16,)),
+            pltpu.SemaphoreType.DMA((3,)),
         ],
         compiler_params=PARAMS,
         name="pack",
-    )(tower_grad.T, weight_upper, weight_lower)
-    own = lax.all_to_all(packed, ("zh", "y"), split_axis=0, concat_axis=0, tiled=True)
-    other = shifted(own, "c", NC, 1)
-
+    )(*(pltpu.with_memory_space_constraint(v, pltpu.HBM) for v in (tower_grad.T, weight_upper, weight_lower)))
     pre_upper = pre_mid.T
     pre_lower = jnp.pad(pre_low.T.reshape(4, 22, 1024), ((0, 0), (0, 2), (0, 0))).reshape(96, 1024)
     edges = jnp.stack(
@@ -242,6 +342,10 @@
         ]
     )
     low_side, high_side = neighbours(edges)
+    lower_level = jnp.stack([lower_block] + [shifted(lower_block, "zh", NZ, s) for s in range(1, NZ)])
+    own = lax.all_to_all(packed, ("zh", "y"), split_axis=0, concat_axis=0, tiled=True)
+    own, low_side, high_side, lower_level = lax.optimization_barrier((own, low_side, high_side, lower_level))
+    other = shifted(own, "c", NC, 1)
     slope_upper = half_slope(jnp.concatenate([low_side[0], pre_upper, high_side[0]], axis=1))
     slope_lower = half_slope(jnp.concatenate([low_side[1], pre_lower, high_side[1]], axis=1))
 
@@ -263,7 +367,12 @@
     )(pos, slope_upper, own, other)
     mid_parts = lax.all_to_all(mid_part, DP, split_axis=0, concat_axis=0, tiled=True)
 
-    upper_sum = scatter_rows(*weight_grad(pos, act_mid.T, upper_taps))
+    lower_levels = [lower_level] + [shifted(lower_level, "y", NY, s) for s in range(1, NY)]
+    upper_keep, upper_send = weight_grad(pos, act_mid.T, upper_taps)
+    upper_got = shifted(upper_send, "c", NC, 1)
+    lower_levels, upper_send = lax.optimization_barrier((lower_levels, upper_send))
+    lower_own = join(lower_levels)
+    lower_other = shifted(lower_own, "c", NC, 1)
     lower_full = pl.pallas_call(
         lower_weight_kernel,
         out_shape=jax.ShapeDtypeStruct((640, 512), BF),
@@ -272,19 +381,28 @@
         scratch_shapes=[pltpu.VMEM((648, 512), F32)],
         compiler_params=PARAMS,
         name="lower_weight",
-    )(pos, own, other)
-
+    )(pos, lower_own, lower_other)
+
+    lower_full, act_low = lax.optimization_barrier((lower_full, act_low))
+    act_low_rows = act_low.T
+    mid_parts, upper_got, act_low_rows = lax.optimization_barrier((mid_parts, upper_got, act_low_rows))
     low_part, lower_taps = pl.pallas_call(
         lower_kernel,
         out_shape=(jax.ShapeDtypeStruct((8, 80, 1024), BF), jax.ShapeDtypeStruct((512, 1024), BF)),
         in_specs=[SMEM] + [VMEM] * 3,
         out_specs=(HBM, VMEM),
-        scratch_shapes=[pltpu.VMEM((8, 80, 1024), BF), pltpu.SemaphoreType.DMA((8,))],
+        scratch_shapes=[pltpu.VMEM((8, 80, 1024), BF), pltpu.SemaphoreType.DMA((4,))],
         compiler_params=PARAMS,
         name="lower",
     )(pos, mid_parts, slope_lower, lower_full)
+    lower_keep, lower_send = weight_grad(pos, act_low_rows, lower_taps)
+    low_part, _ = lax.optimization_barrier((low_part, lower_keep))
+    lower_got = shifted(lower_send, "c", NC, 1)
+    own_sum, *sends = core_sum((upper_keep, upper_got), (lower_keep, lower_got))
+    got = [shifted(send, "y", NY, s + 1) for s, send in enumerate(sends)]
     low_parts = lax.all_to_all(low_part, DP, split_axis=0, concat_axis=0, tiled=True)
-    lower_sum = scatter_rows(*weight_grad(pos, act_low.T, lower_taps))
+    scales = tuple(1.0 / math.sqrt(act.shape[0] * NZ * NY * NC) for act in (act_mid, act_low))
+    grad_upper, grad_lower = z_sum(own_sum, got, scales, weight_upper.shape, weight_lower.shape)
 
     low_grad = pl.pallas_call(
         total_kernel,
@@ -294,11 +412,6 @@
         compiler_params=PARAMS,
         name="low_total",
     )(low_parts).T
-    mid_total = act_mid.shape[0] * NZ * NY * NC
-    low_total = act_low.shape[0] * NZ * NY * NC
-    grad_upper = upper_sum[:22, :480].reshape(22, 5, 96).transpose(1, 0, 2) * (1.0 / math.sqrt(mid_total))
-    grad_lower = lower_sum[:20, :480].reshape(20, 5, 4, 24)[:, :, :, :22].reshape(20, 5, 88)
-    grad_lower = grad_lower.transpose(1, 0, 2) * (1.0 / math.sqrt(low_total))
     return low_grad, grad_upper, grad_lower
 
 

time: 130 us -> 98.6 us (0.76)
  the two profiles are of different devices: /device:TPU:2 before, /device:TPU:8 now
where the time goes in v3:
time: 98.6 us; the launch traced here: 96.7 us
  starting transfers between devices  54.9 us (56%)
  waiting for transfers between devices  22.2 us (23%)
  Pallas kernels  14.9 us (15%)
  local copies, waits for them, and re-layouts  3.4 us (3%)
    ppermute x16, starting transfers between devices, shifted(): lax.ppermute(block, axis, [(i, (i + step) % count) for i in range(count)])  28.7 us
    ppermute x16, waiting for transfers between devices, shifted(): lax.ppermute(block, axis, [(i, (i + step) % count) for i in range(count)])  21.6 us
    all_to_all x1, starting transfers between devices, local(): lax.all_to_all(packed, ('zh', 'y'), split_axis=0, concat_axis=0, tiled=True)  11.6 us
    all_to_all x1, starting transfers between devices, local(): lax.all_to_all(mid_part, DP, split_axis=0, concat_axis=0, tiled=True)  5.27 us
    all_to_all x1, starting transfers between devices, local(): lax.all_to_all(low_part, DP, split_axis=0, concat_axis=0, tiled=True)  5.06 us
    pallas_call x2, Pallas kernels, weight_grad(): pl.pallas_call(weight_grad_kernel, out_shape=(jax.ShapeDtypeStruct(block,...  3.56 us
    pallas_call x1, Pallas kernels, local(): pl.pallas_call(upper_kernel, out_shape=(jax.ShapeDtypeStruct((8, 96, 512)...  2.74 us
    pallas_call x1, Pallas kernels, local(): pl.pallas_call(lower_kernel, out_shape=(jax.ShapeDtypeStruct((8, 80, 1024...  2.73 us
  transfers between devices with their start and end apart: 21, of which 13 were waited for; matrix products, arithmetic and copies ran while one was open for 3% of the time, Pallas kernels for 5%

profile of v3, /device:TPU:8, one launch (start us, length us, event | category | flops | bytes accessed | tf_op | source)
XLA Modules:
  0.0 96.7 jit_solution(12044048666178354798)
XLA Ops:
  0.6 2.1 %pack.1 = (bf16[16,32,512]{2,1,0:T(8,128)(2,1)}, bf16[24,512]{1,0:T(8,128)(2,1)S(1)}) custom-call(bf16[3,8192]{1,0:T(4,128)(2,1)} %bitcast.35, bf16[5,22,96]{2,1,0:T(8,128)(2,1)} %upper_hbm.1, bf16[5,20,88]{2,1,0:T(8,128)(2,1)} %lower_hbm.1), custom_call_target="tpu_custom_call" | custom-call | tf_op jit(solution)/shard_map/pack/pallas_call | solution.py:318
  2.7 11.6 %all-to-all-start = ((bf16[16,32,512]{2,1,0:T(8,128)(2,1)}), bf16[16,32,512]{2,1,0:T(8,128)(2,1)S(1)}, u32[]{:S(2)}, u32[]{:S(2)}) async-start(bf16[16,32,512]{2,1,0:T(8,128)(2,1)} %get-tuple-element.37), calls=%async_computation | async-start | bytes 1048576 | tf_op jit(solution)/shard_map/all_to_all | solution.py:346
  14.3 3.6 %collective-permute-start.4 = (bf16[24,512]{1,0:T(8,128)(2,1)S(1)}, bf16[24,512]{1,0:T(8,128)(2,1)S(1)}, u32[]{:S(2)}, u32[]{:S(2)}) collective-permute-start(bf16[24,512]{1,0:T(8,128)(2,1)S(1)} %get-tuple-element.38), channel_id=1, source_target_pairs={{0,24},{8,0},{16,8},{24,16},{1,25},{9,1},{17,9},{25,17},{2,26},{10... | collective-permute-start | bytes 73736 | tf_op jit(solution)/shard_map/ppermute | solution.py:32
  17.9 2.4 %collective-permute-start.3 = (bf16[24,512]{1,0:T(8,128)(2,1)S(1)}, bf16[24,512]{1,0:T(8,128)(2,1)S(1)}, u32[]{:S(2)}, u32[]{:S(2)}) collective-permute-start(bf16[24,512]{1,0:T(8,128)(2,1)S(1)} %get-tuple-element.38), channel_id=1, source_target_pairs={{0,16},{8,24},{16,0},{24,8},{1,17},{9,25},{17,1},{25,9},{2,18},{10... | collective-permute-start | bytes 73736 | tf_op jit(solution)/shard_map/ppermute | solution.py:32
  20.2 2.4 %collective-permute-start.2 = (bf16[24,512]{1,0:T(8,128)(2,1)S(1)}, bf16[24,512]{1,0:T(8,128)(2,1)S(1)}, u32[]{:S(2)}, u32[]{:S(2)}) collective-permute-start(bf16[24,512]{1,0:T(8,128)(2,1)S(1)} %get-tuple-element.38), channel_id=1, source_target_pairs={{0,8},{8,16},{16,24},{24,0},{1,9},{9,17},{17,25},{25,1},{2,10},{10... | collective-permute-start | bytes 73736 | tf_op jit(solution)/shard_map/ppermute | solution.py:32
  22.6 1.0 %reshape.12 = bf16[4,22,1024]{2,1,0:T(8,128)(2,1)S(1)} reshape(bf16[88,1024]{1,0:T(8,128)(2,1)} %bitcast.33) | data formatting | bytes 360448 | tf_op jit(solution)/shard_map/reshape | solution.py:337
  23.7 1.9 %collective-permute-start.1 = (bf16[2,96,128]{2,1,0:T(8,128)(2,1)S(1)}, bf16[2,96,128]{2,1,0:T(8,128)(2,1)S(1)}, u32[]{:S(2)}, u32[]{:S(2)}) collective-permute-start(bf16[2,96,128]{2,1,0:T(8,128)(2,1)S(1)} %get-tuple-element.73), channel_id=1, source_target_pairs={{1,0},{2,1},{3,2},{4,3},{5,4},{6,5},{7,6},{8,7},{9,8},{10,9},{11,1... | collective-permute-start | bytes 147464 | tf_op jit(solution)/shard_map/ppermute | solution.py:312
  25.6 2.4 %collective-permute-start = (bf16[2,96,128]{2,1,0:T(8,128)(2,1)S(1)}, bf16[2,96,128]{2,1,0:T(8,128)(2,1)S(1)}, u32[]{:S(2)}, u32[]{:S(2)}) collective-permute-start(bf16[2,96,128]{2,1,0:T(8,128)(2,1)S(1)} %get-tuple-element.74), channel_id=1, source_target_pairs={{0,1},{1,2},{2,3},{3,4},{4,5},{5,6},{6,7},{7,8},{8,9},{9,10},{10,1... | collective-permute-start | bytes 147464 | tf_op jit(solution)/shard_map/ppermute | solution.py:311
  28.1 1.8 %collective-permute-done.4 = bf16[24,512]{1,0:T(8,128)(2,1)S(1)} collective-permute-done((bf16[24,512]{1,0:T(8,128)(2,1)S(1)}, bf16[24,512]{1,0:T(8,128)(2,1)S(1)}, u32[]{:S(2)}, u32[]{:S(2)}) %collective-permute-start.4) | collective-permute-done | bytes 24608 | tf_op jit(solution)/shard_map/ppermute | solution.py:32
  29.9 2.1 %collective-permute-done.3 = bf16[24,512]{1,0:T(8,128)(2,1)S(1)} collective-permute-done((bf16[24,512]{1,0:T(8,128)(2,1)S(1)}, bf16[24,512]{1,0:T(8,128)(2,1)S(1)}, u32[]{:S(2)}, u32[]{:S(2)}) %collective-permute-start.3) | collective-permute-done | bytes 24608 | tf_op jit(solution)/shard_map/ppermute | solution.py:32
  32.1 0.1 collective-permute-start.5
  32.2 0.1 fusion.13.slope_ref
  32.4 1.7 %collective-permute-done.5.other_ref = bf16[16,32,512]{2,1,0:T(8,128)(2,1)S(1)} collective-permute-done((bf16[16,32,512]{2,1,0:T(8,128)(2,1)S(1)}, bf16[16,32,512]{2,1,0:T(8,128)(2,1)S(1)}, u32[]{:S(2)}, u32[]{:S(2)}) %collective-permute-start.5) | collective-permute-done | bytes 524320 | tf_op jit(solution)/shard_map/ppermute | solution.py:32
  34.1 2.7 %upper.1 = (bf16[8,96,512]{2,1,0:T(8,128)(2,1)}, bf16[512,512]{1,0:T(8,128)(2,1)S(1)}) custom-call(s32[3]{0:T(128)S(1)} %pad_add_fusion.pos_ref, f32[96,768]{1,0:T(8,128)S(1)} %fusion.13.slope_ref, bf16[16,32,512]{2,1,0:T(8,128)(2,1)S(1)} %all-to-all-done.own_ref, bf16[16,32,512]{2,1,0:T(8,128)(2,1)S(1)} %collective-permute-done.5.other_ref), custom_call_target="tpu_custom_call" | custom-call | tf_op jit(solution)/shard_map/upper/pallas_call | solution.py:352
  36.9 5.3 %all-to-all-start.1 = ((bf16[8,96,512]{2,1,0:T(8,128)(2,1)}), bf16[8,96,512]{2,1,0:T(8,128)(2,1)S(1)}, u32[]{:S(2)}, u32[]{:S(2)}) async-start(bf16[8,96,512]{2,1,0:T(8,128)(2,1)} %get-tuple-element.42), calls=%async_computation.1 | async-start | bytes 1572864 | tf_op jit(solution)/shard_map/all_to_all | solution.py:368
  42.1 1.1 %collective-permute-start.9 = (bf16[4,24,512]{2,1,0:T(8,128)(2,1)S(1)}, bf16[4,24,512]{2,1,0:T(8,128)(2,1)S(1)}, u32[]{:S(2)}, u32[]{:S(2)}) collective-permute-start(bf16[4,24,512]{2,1,0:T(8,128)(2,1)S(1)} %pad_maximum_fusion.refs_0_), channel_id=1, source_target_pairs={{0,6},{2,0},{4,2},{6,4},{1,7},{3,1},{5,3},{7,5},{8,14},{10,8},{12,... | collective-permute-start | bytes 294920 | tf_op jit(solution)/shard_map/ppermute | solution.py:32
  43.2 1.9 %collective-permute-start.8 = (bf16[4,24,512]{2,1,0:T(8,128)(2,1)S(1)}, bf16[4,24,512]{2,1,0:T(8,128)(2,1)S(1)}, u32[]{:S(2)}, u32[]{:S(2)}) collective-permute-start(bf16[4,24,512]{2,1,0:T(8,128)(2,1)S(1)} %pad_maximum_fusion.refs_0_), channel_id=1, source_target_pairs={{0,4},{2,6},{4,0},{6,2},{1,5},{3,7},{5,1},{7,3},{8,12},{10,14},{12... | collective-permute-start | bytes 294920 | tf_op jit(solution)/shard_map/ppermute | solution.py:32
  45.1 1.8 %collective-permute-start.7 = (bf16[4,24,512]{2,1,0:T(8,128)(2,1)S(1)}, bf16[4,24,512]{2,1,0:T(8,128)(2,1)S(1)}, u32[]{:S(2)}, u32[]{:S(2)}) collective-permute-start(bf16[4,24,512]{2,1,0:T(8,128)(2,1)S(1)} %pad_maximum_fusion.refs_0_), channel_id=1, source_target_pairs={{0,2},{2,4},{4,6},{6,0},{1,3},{3,5},{5,7},{7,1},{8,10},{10,12},{12... | collective-permute-start | bytes 294920 | tf_op jit(solution)/shard_map/ppermute | solution.py:32
  46.8 2.0 %weight_grad.2 = (f32[4,4,24,512]{3,2,1,0:T(8,128)S(1)}, bf16[4,4,24,512]{3,2,1,0:T(8,128)(2,1)}) custom-call(s32[3]{0:T(128)S(1)} %pad_add_fusion.pos_ref, bf16[704,512]{1,0:T(8,128)(2,1)S(1)} %bitcast.27, bf16[512,512]{1,0:T(8,128)(2,1)S(1)} %get-tuple-element.43.taps_ref), custom_call_target="tpu_custom_call" | custom-call | tf_op jit(solution)/shard_map/weight_grad/pallas_call | solution.py:296
  48.8 0.9 collective-permute-done.8.refs_2_
  49.8 0.8 collective-permute-done.7.refs_1_
  50.6 0.1 collective-permute-start.10
  50.7 0.5 collective-permute-start.6
  51.2 0.2 fusion.6.slope_ref
  51.4 1.0 %collective-permute-done.10.other_ref = bf16[16,24,512]{2,1,0:T(8,128)(2,1)S(1)} collective-permute-done((bf16[16,24,512]{2,1,0:T(8,128)(2,1)S(1)}, bf16[16,24,512]{2,1,0:T(8,128)(2,1)S(1)}, u32[]{:S(2)}, u32[]{:S(2)}) %collective-permute-start.10) | collective-permute-done | bytes 393248 | tf_op jit(solution)/shard_map/ppermute | solution.py:32
  52.4 0.8 lower_weight.1.w_ref
  53.2 1.6 %copy.11 = bf16[1024,640]{0,1:T(8,128)(2,1)S(1)} copy(bf16[1024,640]{1,0:T(8,128)(2,1)} %param.10) | data formatting | bytes 2621440 | tf_op jit(solution)/shard_map/optimization_barrier | solution.py:386
  54.8 0.5 all-to-all-done.1.mid_ref
  55.3 2.7 %lower.1 = (bf16[8,80,1024]{2,1,0:T(8,128)(2,1)}, bf16[512,1024]{1,0:T(8,128)(2,1)S(1)}) custom-call(s32[3]{0:T(128)S(1)} %pad_add_fusion.pos_ref, bf16[8,96,512]{2,1,0:T(8,128)(2,1)S(1)} %all-to-all-done.1.mid_ref, f32[96,1280]{1,0:T(8,128)S(1)} %fusion.6.slope_ref, bf16[640,512]{1,0:T(8,128)(2,1)S(1)} %lower_weight.1.w_ref), custom_call_target="tpu_custom_call" | custom-call | tf_op jit(solution)/shard_map/lower/pallas_call | solution.py:389
  58.1 1.6 %weight_grad.3 = (f32[4,4,24,512]{3,2,1,0:T(8,128)S(1)}, bf16[4,4,24,512]{3,2,1,0:T(8,128)(2,1)S(1)}) custom-call(s32[3]{0:T(128)S(1)} %pad_add_fusion.pos_ref, bf16[640,1024]{1,0:T(8,128)(2,1)S(1)} %bitcast.26, bf16[512,1024]{1,0:T(8,128)(2,1)S(1)} %get-tuple-element.55.taps_ref), custom_call_target="tpu_custom_call" | custom-call | tf_op jit(solution)/shard_map/weight_grad/pallas_call | solution.py:296
  59.6 0.7 copy-done.3
  60.4 5.1 %all-to-all-start.2 = ((bf16[8,80,1024]{2,1,0:T(8,128)(2,1)}), bf16[8,80,1024]{2,1,0:T(8,128)(2,1)S(1)}, u32[]{:S(2)}, u32[]{:S(2)}) async-start(bf16[8,80,1024]{2,1,0:T(8,128)(2,1)} %get-tuple-element.57), calls=%async_computation.2 | async-start | bytes 2621440 | tf_op jit(solution)/shard_map/all_to_all | solution.py:403
  65.5 0.3 collective-permute-start.11
  65.7 1.7 %collective-permute-done.11.got_lower_ref = bf16[4,4,24,512]{3,2,1,0:T(8,128)(2,1)S(1)} collective-permute-done((bf16[4,4,24,512]{3,2,1,0:T(8,128)(2,1)S(1)}, bf16[4,4,24,512]{3,2,1,0:T(8,128)(2,1)S(1)}, u32[]{:S(2)}, u32[]{:S(2)}) %collective-permute-start.11) | collective-permute-done | bytes 393248 | tf_op jit(solution)/shard_map/ppermute | solution.py:32
  67.5 1.1 %core_sum.1 = (f32[4,48,512]{2,1,0:T(8,128)S(1)}, bf16[4,48,512]{2,1,0:T(8,128)(2,1)S(1)}, bf16[4,48,512]{2,1,0:T(8,128)(2,1)S(1)}, bf16[4,48,512]{2,1,0:T(8,128)(2,1)S(1)}) custom-call(f32[4,4,24,512]{3,2,1,0:T(8,128)S(1)} %copy-done.1, bf16[4,4,24,512]{3,2,1,0:T(8,128)(2,1)} %collective-permute-done.6.got_upper_ref, ...), custom_call_target="tpu_custom_call" | custom-call | tf_op jit(solution)/shard_map/core_sum/pallas_call | solution.py:94
  68.6 1.5 %collective-permute-start.12 = (bf16[4,48,512]{2,1,0:T(8,128)(2,1)S(1)}, bf16[4,48,512]{2,1,0:T(8,128)(2,1)S(1)}, u32[]{:S(2)}, u32[]{:S(2)}) collective-permute-start(bf16[4,48,512]{2,1,0:T(8,128)(2,1)S(1)} %get-tuple-element.62), channel_id=1, source_target_pairs={{0,2},{2,4},{4,6},{6,0},{1,3},{3,5},{5,7},{7,1},{8,10},{10,12},{12... | collective-permute-start | bytes 589832 | tf_op jit(solution)/shard_map/ppermute | solution.py:32
  70.1 3.3 %collective-permute-start.13 = (bf16[4,48,512]{2,1,0:T(8,128)(2,1)S(1)}, bf16[4,48,512]{2,1,0:T(8,128)(2,1)S(1)}, u32[]{:S(2)}, u32[]{:S(2)}) collective-permute-start(bf16[4,48,512]{2,1,0:T(8,128)(2,1)S(1)} %get-tuple-element.63), channel_id=1, source_target_pairs={{0,4},{2,6},{4,0},{6,2},{1,5},{3,7},{5,1},{7,3},{8,12},{10,14},{12... | collective-permute-start | bytes 589832 | tf_op jit(solution)/shard_map/ppermute | solution.py:32
  73.4 3.6 %collective-permute-done.12.refs_0_ = bf16[4,48,512]{2,1,0:T(8,128)(2,1)S(1)} collective-permute-done((bf16[4,48,512]{2,1,0:T(8,128)(2,1)S(1)}, bf16[4,48,512]{2,1,0:T(8,128)(2,1)S(1)}, u32[]{:S(2)}, u32[]{:S(2)}) %collective-permute-start.12) | collective-permute-done | bytes 196640 | tf_op jit(solution)/shard_map/ppermute | solution.py:32
  77.0 2.4 %collective-permute-done.13.refs_1_ = bf16[4,48,512]{2,1,0:T(8,128)(2,1)S(1)} collective-permute-done((bf16[4,48,512]{2,1,0:T(8,128)(2,1)S(1)}, bf16[4,48,512]{2,1,0:T(8,128)(2,1)S(1)}, u32[]{:S(2)}, u32[]{:S(2)}) %collective-permute-start.13) | collective-permute-done | bytes 196640 | tf_op jit(solution)/shard_map/ppermute | solution.py:32
  79.4 3.1 %collective-permute-done.14.refs_2_ = bf16[4,48,512]{2,1,0:T(8,128)(2,1)S(1)} collective-permute-done((bf16[4,48,512]{2,1,0:T(8,128)(2,1)S(1)}, bf16[4,48,512]{2,1,0:T(8,128)(2,1)S(1)}, u32[]{:S(2)}, u32[]{:S(2)}) %collective-permute-start.14) | collective-permute-done | bytes 196640 | tf_op jit(solution)/shard_map/ppermute | solution.py:32
  82.5 0.1 y_sum.1
  82.6 2.1 %collective-permute-start.15 = (bf16[48,512]{1,0:T(8,128)(2,1)S(1)}, bf16[48,512]{1,0:T(8,128)(2,1)S(1)}, u32[]{:S(2)}, u32[]{:S(2)}) collective-permute-start(bf16[48,512]{1,0:T(8,128)(2,1)S(1)} %get-tuple-element.66), channel_id=1, source_target_pairs={{0,8},{8,16},{16,24},{24,0},{1,9},{9,17},{17,25},{25,1},{2,10},{10... | collective-permute-start | bytes 147464 | tf_op jit(solution)/shard_map/ppermute | solution.py:32
  84.7 3.7 %collective-permute-start.16 = (bf16[48,512]{1,0:T(8,128)(2,1)S(1)}, bf16[48,512]{1,0:T(8,128)(2,1)S(1)}, u32[]{:S(2)}, u32[]{:S(2)}) collective-permute-start(bf16[48,512]{1,0:T(8,128)(2,1)S(1)} %get-tuple-element.67), channel_id=1, source_target_pairs={{0,16},{8,24},{16,0},{24,8},{1,17},{9,25},{17,1},{25,9},{2,18},{10... | collective-permute-start | bytes 147464 | tf_op jit(solution)/shard_map/ppermute | solution.py:32
  88.5 4.0 %collective-permute-start.17 = (bf16[48,512]{1,0:T(8,128)(2,1)S(1)}, bf16[48,512]{1,0:T(8,128)(2,1)S(1)}, u32[]{:S(2)}, u32[]{:S(2)}) collective-permute-start(bf16[48,512]{1,0:T(8,128)(2,1)S(1)} %get-tuple-element.68), channel_id=1, source_target_pairs={{0,24},{8,0},{16,8},{24,16},{1,25},{9,1},{17,9},{25,17},{2,26},{10... | collective-permute-start | bytes 147464 | tf_op jit(solution)/shard_map/ppermute | solution.py:32
  92.5 0.2 collective-permute-done.16.refs_1_
  92.7 2.2 %collective-permute-done.17.refs_2_ = bf16[48,512]{1,0:T(8,128)(2,1)S(1)} collective-permute-done((bf16[48,512]{1,0:T(8,128)(2,1)S(1)}, bf16[48,512]{1,0:T(8,128)(2,1)S(1)}, u32[]{:S(2)}, u32[]{:S(2)}) %collective-permute-start.17) | collective-permute-done | bytes 49184 | tf_op jit(solution)/shard_map/ppermute | solution.py:32
  94.9 0.9 z_sum.1
  95.9 0.8 low_total.1
  (30 shorter events, 0.2 us)
Async XLA Ops:
  0.6 23.0 %copy-start.5 = (bf16[512,96]{0,1:T(8,128)(2,1)S(1)}, bf16[512,96]{0,1:T(8,128)(2,1)}, u32[]{:S(2)}) copy-start(bf16[512,96]{0,1:T(8,128)(2,1)} %param.9) | copy-start | bytes 294916
  2.7 29.4 %all-to-all-start = ((bf16[16,32,512]{2,1,0:T(8,128)(2,1)}), bf16[16,32,512]{2,1,0:T(8,128)(2,1)S(1)}, u32[]{:S(2)}, u32[]{:S(2)}) async-start(bf16[16,32,512]{2,1,0:T(8,128)(2,1)} %get-tuple-element.37), calls=%async_computation | async-start | bytes 1048576 | tf_op jit(solution)/shard_map/all_to_all | solution.py:346
  14.3 15.6 %collective-permute-start.4 = (bf16[24,512]{1,0:T(8,128)(2,1)S(1)}, bf16[24,512]{1,0:T(8,128)(2,1)S(1)}, u32[]{:S(2)}, u32[]{:S(2)}) collective-permute-start(bf16[24,512]{1,0:T(8,128)(2,1)S(1)} %get-tuple-element.38), channel_id=1, source_target_pairs={{0,24},{8,0},{16,8},{24,16},{1,25},{9,1},{17,9},{25,17},{2,26},{10... | collective-permute-start | bytes 73736 | tf_op jit(solution)/shard_map/ppermute | solution.py:32
  17.9 14.2 %collective-permute-start.3 = (bf16[24,512]{1,0:T(8,128)(2,1)S(1)}, bf16[24,512]{1,0:T(8,128)(2,1)S(1)}, u32[]{:S(2)}, u32[]{:S(2)}) collective-permute-start(bf16[24,512]{1,0:T(8,128)(2,1)S(1)} %get-tuple-element.38), channel_id=1, source_target_pairs={{0,16},{8,24},{16,0},{24,8},{1,17},{9,25},{17,1},{25,9},{2,18},{10... | collective-permute-start | bytes 73736 | tf_op jit(solution)/shard_map/ppermute | solution.py:32
  20.2 11.8 %collective-permute-start.2 = (bf16[24,512]{1,0:T(8,128)(2,1)S(1)}, bf16[24,512]{1,0:T(8,128)(2,1)S(1)}, u32[]{:S(2)}, u32[]{:S(2)}) collective-permute-start(bf16[24,512]{1,0:T(8,128)(2,1)S(1)} %get-tuple-element.38), channel_id=1, source_target_pairs={{0,8},{8,16},{16,24},{24,0},{1,9},{9,17},{17,25},{25,1},{2,10},{10... | collective-permute-start | bytes 73736 | tf_op jit(solution)/shard_map/ppermute | solution.py:32
  23.7 8.4 %collective-permute-start.1 = (bf16[2,96,128]{2,1,0:T(8,128)(2,1)S(1)}, bf16[2,96,128]{2,1,0:T(8,128)(2,1)S(1)}, u32[]{:S(2)}, u32[]{:S(2)}) collective-permute-start(bf16[2,96,128]{2,1,0:T(8,128)(2,1)S(1)} %get-tuple-element.73), channel_id=1, source_target_pairs={{1,0},{2,1},{3,2},{4,3},{5,4},{6,5},{7,6},{8,7},{9,8},{10,9},{11,1... | collective-permute-start | bytes 147464 | tf_op jit(solution)/shard_map/ppermute | solution.py:312
  25.6 6.5 %collective-permute-start = (bf16[2,96,128]{2,1,0:T(8,128)(2,1)S(1)}, bf16[2,96,128]{2,1,0:T(8,128)(2,1)S(1)}, u32[]{:S(2)}, u32[]{:S(2)}) collective-permute-start(bf16[2,96,128]{2,1,0:T(8,128)(2,1)S(1)} %get-tuple-element.74), channel_id=1, source_target_pairs={{0,1},{1,2},{2,3},{3,4},{4,5},{5,6},{6,7},{7,8},{8,9},{9,10},{10,1... | collective-permute-start | bytes 147464 | tf_op jit(solution)/shard_map/ppermute | solution.py:311
  32.1 2.0 %collective-permute-start.5 = (bf16[16,32,512]{2,1,0:T(8,128)(2,1)S(1)}, bf16[16,32,512]{2,1,0:T(8,128)(2,1)S(1)}, u32[]{:S(2)}, u32[]{:S(2)}) collective-permute-start(bf16[16,32,512]{2,1,0:T(8,128)(2,1)S(1)} %all-to-all-done.own_ref), channel_id=1, source_target_pairs={{0,1},{1,0},{2,3},{3,2},{4,5},{5,4},{6,7},{7,6},{8,9},{9,8},{10,11... | collective-permute-start | bytes 1572872 | tf_op jit(solution)/shard_map/ppermute | solution.py:32
  32.4 14.5 %copy-start.2 = (bf16[512,704]{0,1:T(8,128)(2,1)S(1)}, bf16[512,704]{0,1:T(8,128)(2,1)}, u32[]{:S(2)}) copy-start(bf16[512,704]{0,1:T(8,128)(2,1)} %param.8) | copy-start | bytes 2162692
  36.9 18.5 %all-to-all-start.1 = ((bf16[8,96,512]{2,1,0:T(8,128)(2,1)}), bf16[8,96,512]{2,1,0:T(8,128)(2,1)S(1)}, u32[]{:S(2)}, u32[]{:S(2)}) async-start(bf16[8,96,512]{2,1,0:T(8,128)(2,1)} %get-tuple-element.42), calls=%async_computation.1 | async-start | bytes 1572864 | tf_op jit(solution)/shard_map/all_to_all | solution.py:368
  42.1 6.7 %collective-permute-start.9 = (bf16[4,24,512]{2,1,0:T(8,128)(2,1)S(1)}, bf16[4,24,512]{2,1,0:T(8,128)(2,1)S(1)}, u32[]{:S(2)}, u32[]{:S(2)}) collective-permute-start(bf16[4,24,512]{2,1,0:T(8,128)(2,1)S(1)} %pad_maximum_fusion.refs_0_), channel_id=1, source_target_pairs={{0,6},{2,0},{4,2},{6,4},{1,7},{3,1},{5,3},{7,5},{8,14},{10,8},{12,... | collective-permute-start | bytes 294920 | tf_op jit(solution)/shard_map/ppermute | solution.py:32
  43.2 6.6 %collective-permute-start.8 = (bf16[4,24,512]{2,1,0:T(8,128)(2,1)S(1)}, bf16[4,24,512]{2,1,0:T(8,128)(2,1)S(1)}, u32[]{:S(2)}, u32[]{:S(2)}) collective-permute-start(bf16[4,24,512]{2,1,0:T(8,128)(2,1)S(1)} %pad_maximum_fusion.refs_0_), channel_id=1, source_target_pairs={{0,4},{2,6},{4,0},{6,2},{1,5},{3,7},{5,1},{7,3},{8,12},{10,14},{12... | collective-permute-start | bytes 294920 | tf_op jit(solution)/shard_map/ppermute | solution.py:32
  45.1 5.5 %collective-permute-start.7 = (bf16[4,24,512]{2,1,0:T(8,128)(2,1)S(1)}, bf16[4,24,512]{2,1,0:T(8,128)(2,1)S(1)}, u32[]{:S(2)}, u32[]{:S(2)}) collective-permute-start(bf16[4,24,512]{2,1,0:T(8,128)(2,1)S(1)} %pad_maximum_fusion.refs_0_), channel_id=1, source_target_pairs={{0,2},{2,4},{4,6},{6,0},{1,3},{3,5},{5,7},{7,1},{8,10},{10,12},{12... | collective-permute-start | bytes 294920 | tf_op jit(solution)/shard_map/ppermute | solution.py:32
  48.8 3.6 %copy-start = (f32[4,4,24,512]{3,2,1,0:T(8,128)}, f32[4,4,24,512]{3,2,1,0:T(8,128)S(1)}, u32[]{:S(2)}) copy-start(f32[4,4,24,512]{3,2,1,0:T(8,128)S(1)} %get-tuple-element.58.keep_upper_ref) | copy-start | bytes 2359300
  50.6 1.8 %collective-permute-start.10 = (bf16[16,24,512]{2,1,0:T(8,128)(2,1)S(1)}, bf16[16,24,512]{2,1,0:T(8,128)(2,1)S(1)}, u32[]{:S(2)}, u32[]{:S(2)}) collective-permute-start(bf16[16,24,512]{2,1,0:T(8,128)(2,1)S(1)} %join.1.own_ref), channel_id=1, source_target_pairs={{0,1},{1,0},{2,3},{3,2},{4,5},{5,4},{6,7},{7,6},{8,9},{9,8},{10,11... | collective-permute-start | bytes 1179656 | tf_op jit(solution)/shard_map/ppermute | solution.py:32
  50.7 4.1 %collective-permute-start.6 = (bf16[4,4,24,512]{3,2,1,0:T(8,128)(2,1)}, bf16[4,4,24,512]{3,2,1,0:T(8,128)(2,1)}, u32[]{:S(2)}, u32[]{:S(2)}) collective-permute-start(bf16[4,4,24,512]{3,2,1,0:T(8,128)(2,1)} %get-tuple-element.44), channel_id=1, source_target_pairs={{0,1},{1,0},{2,3},{3,2},{4,5},{5,4},{6,7},{7,6},{8,9},{9,8},{10,11... | collective-permute-start | bytes 1179656 | tf_op jit(solution)/shard_map/ppermute | solution.py:32
  59.6 0.8 copy-start.3
  60.4 5.1 %copy-start.4 = (bf16[4,4,24,512]{3,2,1,0:T(8,128)(2,1)S(1)}, bf16[4,4,24,512]{3,2,1,0:T(8,128)(2,1)}, u32[]{:S(2)}) copy-start(bf16[4,4,24,512]{3,2,1,0:T(8,128)(2,1)} %copy-done.3) | copy-start | bytes 1179652
  60.4 7.1 %copy-start.1 = (f32[4,4,24,512]{3,2,1,0:T(8,128)S(1)}, f32[4,4,24,512]{3,2,1,0:T(8,128)}, u32[]{:S(2)}) copy-start(f32[4,4,24,512]{3,2,1,0:T(8,128)} %copy-done) | copy-start | bytes 2359300
  60.4 35.5 %all-to-all-start.2 = ((bf16[8,80,1024]{2,1,0:T(8,128)(2,1)}), bf16[8,80,1024]{2,1,0:T(8,128)(2,1)S(1)}, u32[]{:S(2)}, u32[]{:S(2)}) async-start(bf16[8,80,1024]{2,1,0:T(8,128)(2,1)} %get-tuple-element.57), calls=%async_computation.2 | async-start | bytes 2621440 | tf_op jit(solution)/shard_map/all_to_all | solution.py:403
  65.5 2.0 %collective-permute-start.11 = (bf16[4,4,24,512]{3,2,1,0:T(8,128)(2,1)S(1)}, bf16[4,4,24,512]{3,2,1,0:T(8,128)(2,1)S(1)}, u32[]{:S(2)}, u32[]{:S(2)}) collective-permute-start(bf16[4,4,24,512]{3,2,1,0:T(8,128)(2,1)S(1)} %copy-done.4), channel_id=1, source_target_pairs={{0,1},{1,0},{2,3},{3,2},{4,5},{5,4},{6,7},{7,6},{8,9},{9,8},{10,11... | collective-permute-start | bytes 1179656 | tf_op jit(solution)/shard_map/ppermute | solution.py:32
  68.6 8.4 %collective-permute-start.12 = (bf16[4,48,512]{2,1,0:T(8,128)(2,1)S(1)}, bf16[4,48,512]{2,1,0:T(8,128)(2,1)S(1)}, u32[]{:S(2)}, u32[]{:S(2)}) collective-permute-start(bf16[4,48,512]{2,1,0:T(8,128)(2,1)S(1)} %get-tuple-element.62), channel_id=1, source_target_pairs={{0,2},{2,4},{4,6},{6,0},{1,3},{3,5},{5,7},{7,1},{8,10},{10,12},{12... | collective-permute-start | bytes 589832 | tf_op jit(solution)/shard_map/ppermute | solution.py:32
  70.1 9.3 %collective-permute-start.13 = (bf16[4,48,512]{2,1,0:T(8,128)(2,1)S(1)}, bf16[4,48,512]{2,1,0:T(8,128)(2,1)S(1)}, u32[]{:S(2)}, u32[]{:S(2)}) collective-permute-start(bf16[4,48,512]{2,1,0:T(8,128)(2,1)S(1)} %get-tuple-element.63), channel_id=1, source_target_pairs={{0,4},{2,6},{4,0},{6,2},{1,5},{3,7},{5,1},{7,3},{8,12},{10,14},{12... | collective-permute-start | bytes 589832 | tf_op jit(solution)/shard_map/ppermute | solution.py:32
  73.4 9.1 %collective-permute-start.14 = (bf16[4,48,512]{2,1,0:T(8,128)(2,1)S(1)}, bf16[4,48,512]{2,1,0:T(8,128)(2,1)S(1)}, u32[]{:S(2)}, u32[]{:S(2)}) collective-permute-start(bf16[4,48,512]{2,1,0:T(8,128)(2,1)S(1)} %get-tuple-element.64), channel_id=1, source_target_pairs={{0,6},{2,0},{4,2},{6,4},{1,7},{3,1},{5,3},{7,5},{8,14},{10,8},{12,... | collective-permute-start | bytes 589832 | tf_op jit(solution)/shard_map/ppermute | solution.py:32
  82.6 9.9 %collective-permute-start.15 = (bf16[48,512]{1,0:T(8,128)(2,1)S(1)}, bf16[48,512]{1,0:T(8,128)(2,1)S(1)}, u32[]{:S(2)}, u32[]{:S(2)}) collective-permute-start(bf16[48,512]{1,0:T(8,128)(2,1)S(1)} %get-tuple-element.66), channel_id=1, source_target_pairs={{0,8},{8,16},{16,24},{24,0},{1,9},{9,17},{17,25},{25,1},{2,10},{10... | collective-permute-start | bytes 147464 | tf_op jit(solution)/shard_map/ppermute | solution.py:32
  84.7 8.0 %collective-permute-start.16 = (bf16[48,512]{1,0:T(8,128)(2,1)S(1)}, bf16[48,512]{1,0:T(8,128)(2,1)S(1)}, u32[]{:S(2)}, u32[]{:S(2)}) collective-permute-start(bf16[48,512]{1,0:T(8,128)(2,1)S(1)} %get-tuple-element.67), channel_id=1, source_target_pairs={{0,16},{8,24},{16,0},{24,8},{1,17},{9,25},{17,1},{25,9},{2,18},{10... | collective-permute-start | bytes 147464 | tf_op jit(solution)/shard_map/ppermute | solution.py:32
  88.5 6.5 %collective-permute-start.17 = (bf16[48,512]{1,0:T(8,128)(2,1)S(1)}, bf16[48,512]{1,0:T(8,128)(2,1)S(1)}, u32[]{:S(2)}, u32[]{:S(2)}) collective-permute-start(bf16[48,512]{1,0:T(8,128)(2,1)S(1)} %get-tuple-element.68), channel_id=1, source_target_pairs={{0,24},{8,0},{16,8},{24,16},{1,25},{9,1},{17,9},{25,17},{2,26},{10... | collective-permute-start | bytes 147464 | tf_op jit(solution)/shard_map/ppermute | solution.py:32

commit v4 on v3

--- a/solution.py
+++ b/solution.py
@@ -50,9 +50,13 @@
     )(*levels)
 
 
-def core_sum_kernel(keep_upper_ref, got_upper_ref, keep_lower_ref, got_lower_ref, own_ref, *send_refs):
-    pairs = ((keep_upper_ref, got_upper_ref), (keep_lower_ref, got_lower_ref))
-    for half, (keep_ref, got_ref) in enumerate(pairs):
+def core_sum_kernel(keep_upper_ref, got_upper_hbm, keep_lower_ref, got_lower_ref, own_ref, *refs):
+    send_refs, (got_upper_ref, sem) = refs[: NY - 1], refs[NY - 1 :]
+    fetch = pltpu.make_async_copy(got_upper_hbm, got_upper_ref, sem)
+    fetch.start()
+    for half, (keep_ref, got_ref) in ((1, (keep_lower_ref, got_lower_ref)), (0, (keep_upper_ref, got_upper_ref))):
+        if half == 0:
+            fetch.wait()
         rows = slice(24 * half, 24 * half + 24)
         for s in range(NY):
             for z in range(NZ):
@@ -104,7 +108,16 @@
 def core_sum(upper, lower):
     level = jax.ShapeDtypeStruct((NZ, 48, 512), BF)
     outs = (jax.ShapeDtypeStruct(level.shape, F32),) + (level,) * (NY - 1)
-    return small_call(core_sum_kernel, "core_sum", outs, *upper, *lower)
+    got_upper = pltpu.with_memory_space_constraint(upper[1], pltpu.HBM)
+    return pl.pallas_call(
+        core_sum_kernel,
+        out_shape=outs,
+        in_specs=[VMEM, HBM, VMEM, VMEM],
+        out_specs=tuple(VMEM for _ in outs),
+        scratch_shapes=[pltpu.VMEM(got_upper.shape, BF), pltpu.SemaphoreType.DMA(())],
+        compiler_params=PARAMS,
+        name="core_sum",
+    )(upper[0], got_upper, *lower)
 
 
 def z_sum(own, got, scales, upper_shape, lower_shape):
@@ -138,13 +151,14 @@
 
 
 def pack_kernel(
-    tower_hbm, upper_hbm, lower_hbm, out_ref, lower_out_ref,
-    tower_ref, upper_ref, lower_ref, weight_ref, tower_rows_ref, buf_ref, sem, in_sem,
+    tower_hbm, upper_hbm, lower_hbm, pre_upper_hbm, pre_lower_hbm, out_ref, lower_out_ref,
+    tower_ref, upper_ref, lower_ref, pre_upper_ref, pre_lower_ref, weight_ref, tower_rows_ref, buf_ref, sem, in_sem,
 ):
-    copies = [
-        pltpu.make_async_copy(source, target, in_sem.at[i])
-        for i, (source, target) in enumerate(((upper_hbm, upper_ref), (lower_hbm, lower_ref), (tower_hbm, tower_ref)))
-    ]
+    pieces = [(upper_hbm, upper_ref), (lower_hbm, lower_ref), (tower_hbm, tower_ref)]
+    for source, target in ((pre_upper_hbm, pre_upper_ref), (pre_lower_hbm, pre_lower_ref)):
+        pieces.append((source.at[:, pl.ds(source.shape[1] - 128, 128)], target.at[0]))
+        pieces.append((source.at[:, pl.ds(0, 128)], target.at[1]))
+    copies = [pltpu.make_async_copy(source, target, in_sem.at[i]) for i, (source, target) in enumerate(pieces)]
     for copy in copies:
         copy.start()
     for copy in copies:
@@ -152,10 +166,19 @@
     weight_ref[...] = jnp.zeros((48, 512), F32)
     weight_ref[0:22, :] = sum(mm(upper_ref[k], one_hot(96, 96 * k, False)) for k in range(KWIDTH))
     weight_ref[24:44, :] = sum(mm(lower_ref[k], one_hot(88, 96 * k, True)) for k in range(KWIDTH))
+    last, first = (pre_upper_ref[i].astype(F32).T for i in range(2))
+    low_last, low_first = (pre_lower_ref[i].astype(F32).T for i in range(2))
+    weight_ref[22:24, 0:96] = last[126:128]
+    weight_ref[23:24, 128:224] = last[125:126]
+    weight_ref[22:24, 256:344] = low_last[126:128]
+    tower_rows_ref[...] = jnp.zeros((128, 512), F32)
+    for p in range(16):
+        tower_rows_ref[8 * p + 6 : 8 * p + 8, 0:96] = first[0:2]
+        tower_rows_ref[8 * p + 6 : 8 * p + 7, 128:224] = first[2:3]
+        tower_rows_ref[8 * p + 6 : 8 * p + 8, 256:344] = low_first[0:2]
     weight = weight_ref[0:24, :].astype(BF)
     lower_out_ref[...] = weight_ref[24:48, :].astype(BF)
     tower = tower_ref[...].astype(F32)
-    tower_rows_ref[...] = jnp.zeros((128, 512), F32)
     for p in range(16):
         at, row = 512 * p, 8 * p
         tower_rows_ref[row : row + 3, :] = tower[:, at : at + 512]
@@ -172,8 +195,23 @@
         pltpu.make_async_copy(buf_ref.at[p], out_ref.at[p], sem.at[p]).wait()
 
 
+def edge_tiles(pos_ref, other_ref, at, deep):
+    chip = pos_ref[0] * NY + pos_ref[1]
+    before = other_ref[jnp.maximum(chip - 1 + pos_ref[2], 0), 16:24, :].astype(F32)
+    after = other_ref[jnp.minimum(chip + pos_ref[2], NZ * NY - 1), 24:32, :].astype(F32)
+    row = lax.broadcasted_iota(jnp.int32, (8, 128), 0)
+    low = before[:, at : at + 128]
+    high = pltpu.roll(after[:, at : at + 128], 2, 0)
+    if deep:
+        low = jnp.where(row == 5, pltpu.roll(before[:, at + 128 : at + 256], 6, 0), low)
+        high = jnp.where(row == 2, pltpu.roll(after[:, at + 128 : at + 256], 4, 0), high)
+    rest = jnp.zeros((120, 128), F32)
+    return jnp.concatenate([rest, low], axis=0).T, jnp.concatenate([high, rest], axis=0).T
+
+
 def upper_kernel(
-    pos_ref, slope_ref, own_ref, other_ref, mid_ref, taps_ref, main_ref, edge_ref, w_ref, halo_ref, buf_ref, sem
+    pos_ref, slope_ref, own_ref, other_ref, mid_ref, taps_out_ref, edge_out_ref,
+    main_ref, edge_ref, w_ref, halo_ref, buf_ref, taps_ref, edge_rows_ref, sem,
 ):
     first = pos_ref[2] == 0
     for p in range(16):
@@ -199,7 +237,9 @@
         ],
         axis=1,
     )
-    grad = grad * slope_ref[...]
+    low, high = edge_tiles(pos_ref, other_ref, 0, True)
+    slope = jnp.concatenate([half_slope(low[0:96]), slope_ref[...], half_slope(high[0:96])], axis=1)
+    grad = grad * slope
     lane = lax.broadcasted_iota(jnp.int32, (96, 128), 1)
     taps_ref[480:512, :] = jnp.zeros((32, 512), BF)
     halo_ref[480:512, :] = jnp.zeros((32, 128), F32)
@@ -208,6 +248,11 @@
         after = pltpu.roll(moved[:, 512:640], 126, 1)
         taps_ref[96 * k : 96 * k + 96, :] = moved[:, 0:512].astype(BF)
         halo_ref[96 * k : 96 * k + 96, :] = jnp.where(lane == 127, moved[:, 640:768], after)
+    out_copies = [
+        pltpu.make_async_copy(taps_ref, taps_out_ref, sem.at[8]),
+        pltpu.make_async_copy(edge_rows_ref, edge_out_ref, sem.at[9]),
+    ]
+    out_copies[0].start()
     outside = lax.dot_general(
         halo_ref[...].T.astype(BF), w_ref[...], (((1,), (1,)), ((), ())), preferred_element_type=F32
     )[120:128]
@@ -223,8 +268,16 @@
             buf_ref[d, :, lanes] = part.astype(BF)
     for d in range(8):
         pltpu.make_async_copy(buf_ref.at[d], mid_ref.at[d], sem.at[d]).start()
+    edge_rows_ref[...] = jnp.zeros((96, 256), F32)
+    for half, tile in enumerate(edge_tiles(pos_ref, other_ref, 256, False)):
+        for group in range(4):
+            rows, lanes = slice(24 * group, 24 * group + 22), slice(128 * half, 128 * half + 128)
+            edge_rows_ref[rows, lanes] = tile[22 * group : 22 * group + 22]
+    out_copies[1].start()
     for d in range(8):
         pltpu.make_async_copy(buf_ref.at[d], mid_ref.at[d], sem.at[d]).wait()
+    for copy in out_copies:
+        copy.wait()
 
 
 def lower_weight_kernel(pos_ref, own_ref, other_ref, out_ref, rows_ref):
@@ -237,7 +290,7 @@
     out_ref[...] = rows_ref[0:640, :].astype(BF)
 
 
-def lower_kernel(pos_ref, mid_ref, slope_ref, w_ref, low_ref, taps_ref, buf_ref, sem):
+def lower_taps_kernel(pos_ref, mid_ref, slope_ref, edge_ref, taps_ref):
     place = pos_ref[0] * (NY * NC) + pos_ref[1] * NC + pos_ref[2]
     total = mid_ref[0].astype(F32)
     for d in range(1, 8):
@@ -246,15 +299,19 @@
     ends = mid[:, 0:128].astype(F32).T
     left = jnp.broadcast_to(jnp.where(place == 0, 0.0, ends[0:96, 23:24]), (96, 128))
     right = jnp.broadcast_to(jnp.where(place == 31, 0.0, ends[0:96, 22:23]), (96, 128))
+    edge = half_slope(edge_ref[...])
     spread = doubling()
+    grad = jnp.concatenate([mm(mid[:, 128 * j : 128 * j + 128], spread) for j in range(4)], axis=1)
     grad = jnp.concatenate(
-        [left] + [mm(mid[:, 128 * j : 128 * j + 128], spread) for j in range(4)] + [right], axis=1
+        [left * edge[:, 0:128], grad * slope_ref[...], right * edge[:, 128:256]], axis=1
     )
-    grad = grad * slope_ref[...]
     taps_ref[480:512, :] = jnp.zeros((32, 1024), BF)
     for k in range(KWIDTH):
         moved = pltpu.roll(grad, 1280 - (130 - k), 1)
         taps_ref[96 * k : 96 * k + 96, :] = moved[:, 0:1024].astype(BF)
+
+
+def low_kernel(taps_ref, w_ref, low_ref, buf_ref, sem):
     for quarter in range(4):
         lanes = slice(256 * quarter, 256 * quarter + 256)
         low = mm(w_ref[...], taps_ref[:, lanes])
@@ -271,6 +328,20 @@
     for d in range(1, 8):
         total = total + low_ref[d].astype(F32)
     out_ref[...] = total.astype(BF)
+
+
+def fetched_weight_grad_kernel(
+    pos_ref, act_hbm, taps_hbm, keep_ref, send_ref, rows_ref, block_ref, act_ref, taps_ref, sem
+):
+    copies = [
+        pltpu.make_async_copy(act_hbm, act_ref, sem.at[0]),
+        pltpu.make_async_copy(taps_hbm, taps_ref, sem.at[1]),
+    ]
+    for copy in copies:
+        copy.start()
+    for copy in copies:
+        copy.wait()
+    weight_grad_kernel(pos_ref, act_ref, taps_ref, keep_ref, send_ref, rows_ref, block_ref)
 
 
 def weight_grad_kernel(pos_ref, act_ref, taps_ref, keep_ref, send_ref, rows_ref, block_ref):
@@ -291,87 +362,85 @@
             send_ref[ry, rz] = block_ref[base + 1 - pos_ref[2]].astype(BF)
 
 
-def weight_grad(pos, act, taps):
+def weight_grad(pos, act, taps, fetch):
     block = (NY, NZ, 24, taps.shape[0])
+    scratch = [pltpu.VMEM((act.shape[0] + 8, taps.shape[0]), F32), pltpu.VMEM((32, 24, taps.shape[0]), F32)]
+    if fetch:
+        scratch += [pltpu.VMEM(act.shape, BF), pltpu.VMEM(taps.shape, BF), pltpu.SemaphoreType.DMA((2,))]
+        act, taps = (pltpu.with_memory_space_constraint(v, pltpu.HBM) for v in (act, taps))
     return pl.pallas_call(
-        weight_grad_kernel,
+        fetched_weight_grad_kernel if fetch else weight_grad_kernel,
         out_shape=(jax.ShapeDtypeStruct(block, F32), jax.ShapeDtypeStruct(block, BF)),
-        in_specs=[SMEM, VMEM, VMEM],
+        in_specs=[SMEM] + [HBM if fetch else VMEM] * 2,
         out_specs=(VMEM, VMEM),
-        scratch_shapes=[pltpu.VMEM((act.shape[0] + 8, taps.shape[0]), F32), pltpu.VMEM((32, 24, taps.shape[0]), F32)],
+        scratch_shapes=scratch,
         compiler_params=PARAMS,
         name="weight_grad",
     )(pos, act, taps)
 
 
-def neighbours(block):
-    count = NZ * NY * NC
-    forward = [(i, i + 1) for i in range(count - 1)]
-    backward = [(i + 1, i) for i in range(count - 1)]
-    low = lax.ppermute(block[:, :, -128:], SEQ, forward)
-    high = lax.ppermute(block[:, :, :128], SEQ, backward)
-    return low, high
-
-
 def local(tower_grad, act_mid, pre_mid, act_low, pre_low, weight_upper, weight_lower):
     pos = jnp.stack([lax.axis_index("zh"), lax.axis_index("y"), lax.axis_index("c")]).astype(jnp.int32)
+    sources = (tower_grad.T, weight_upper, weight_lower, pre_mid.T, pre_low.T)
     packed, lower_block = pl.pallas_call(
         pack_kernel,
-        out_shape=(jax.ShapeDtypeStruct((16, 32, 512), BF), jax.ShapeDtypeStruct((24, 512), BF)),
-        in_specs=[HBM] * 3,
+        out_shape=(pltpu.HBM((16, 32, 512), BF), jax.ShapeDtypeStruct((24, 512), BF)),
+        in_specs=[HBM] * 5,
         out_specs=(HBM, VMEM),
         scratch_shapes=[
             pltpu.VMEM((3, 8192), BF),
             pltpu.VMEM(weight_upper.shape, BF),
             pltpu.VMEM(weight_lower.shape, BF),
+            pltpu.VMEM((2, 96, 128), BF),
+            pltpu.VMEM((2, 88, 128), BF),
             pltpu.VMEM((48, 512), F32),
             pltpu.VMEM((128, 512), F32),
             pltpu.VMEM((16, 32, 512), BF),
             pltpu.SemaphoreType.DMA((16,)),
-            pltpu.SemaphoreType.DMA((3,)),
+            pltpu.SemaphoreType.DMA((7,)),
         ],
         compiler_params=PARAMS,
         name="pack",
-    )(*(pltpu.with_memory_space_constraint(v, pltpu.HBM) for v in (tower_grad.T, weight_upper, weight_lower)))
-    pre_upper = pre_mid.T
+    )(*(pltpu.with_memory_space_constraint(v, pltpu.HBM) for v in sources))
     pre_lower = jnp.pad(pre_low.T.reshape(4, 22, 1024), ((0, 0), (0, 2), (0, 0))).reshape(96, 1024)
-    edges = jnp.stack(
-        [
-            jnp.concatenate([pre_upper[:, :128], pre_upper[:, -128:]], axis=1),
-            jnp.concatenate([pre_lower[:, :128], pre_lower[:, -128:]], axis=1),
-        ]
+    slope_upper = half_slope(pre_mid.T)
+    slope_lower = half_slope(pre_lower)
+    act_low_rows = act_low.T
+    lower_blocks = [lower_block] + [shifted(lower_block, "zh", NZ, s) for s in range(1, NZ)]
+    own = lax.all_to_all(packed, ("zh", "y"), split_axis=0, concat_axis=0, tiled=True)
+    own, slope_upper, slope_lower, act_low_rows, lower_blocks = lax.optimization_barrier(
+        (own, slope_upper, slope_lower, act_low_rows, lower_blocks)
     )
-    low_side, high_side = neighbours(edges)
-    lower_level = jnp.stack([lower_block] + [shifted(lower_block, "zh", NZ, s) for s in range(1, NZ)])
-    own = lax.all_to_all(packed, ("zh", "y"), split_axis=0, concat_axis=0, tiled=True)
-    own, low_side, high_side, lower_level = lax.optimization_barrier((own, low_side, high_side, lower_level))
     other = shifted(own, "c", NC, 1)
-    slope_upper = half_slope(jnp.concatenate([low_side[0], pre_upper, high_side[0]], axis=1))
-    slope_lower = half_slope(jnp.concatenate([low_side[1], pre_lower, high_side[1]], axis=1))
-
-    mid_part, upper_taps = pl.pallas_call(
+
+    mid_part, upper_taps, edges = pl.pallas_call(
         upper_kernel,
-        out_shape=(jax.ShapeDtypeStruct((8, 96, 512), BF), jax.ShapeDtypeStruct((512, 512), BF)),
+        out_shape=(pltpu.HBM((8, 96, 512), BF), pltpu.HBM((512, 512), BF), pltpu.HBM((96, 256), F32)),
         in_specs=[SMEM] + [VMEM] * 3,
-        out_specs=(HBM, VMEM),
+        out_specs=(HBM, HBM, HBM),
         scratch_shapes=[
             pltpu.VMEM((96, 256), F32),
             pltpu.VMEM((96, 256), F32),
             pltpu.VMEM((768, 512), BF),
             pltpu.VMEM((512, 128), F32),
             pltpu.VMEM((8, 96, 512), BF),
-            pltpu.SemaphoreType.DMA((8,)),
+            pltpu.VMEM((512, 512), BF),
+            pltpu.VMEM((96, 256), F32),
+            pltpu.SemaphoreType.DMA((10,)),
         ],
         compiler_params=PARAMS,
         name="upper",
     )(pos, slope_upper, own, other)
     mid_parts = lax.all_to_all(mid_part, DP, split_axis=0, concat_axis=0, tiled=True)
 
+    lower_blocks, _ = lax.optimization_barrier((lower_blocks, upper_taps))
+    lower_level = jnp.stack(lower_blocks)
     lower_levels = [lower_level] + [shifted(lower_level, "y", NY, s) for s in range(1, NY)]
-    upper_keep, upper_send = weight_grad(pos, act_mid.T, upper_taps)
-    upper_got = shifted(upper_send, "c", NC, 1)
+    upper_keep, upper_send = weight_grad(pos, act_mid.T, upper_taps, True)
     lower_levels, upper_send = lax.optimization_barrier((lower_levels, upper_send))
     lower_own = join(lower_levels)
+    lower_own, upper_send = lax.optimization_barrier((lower_own, upper_send))
+    upper_got = shifted(upper_send, "c", NC, 1)
     lower_other = shifted(lower_own, "c", NC, 1)
     lower_full = pl.pallas_call(
         lower_weight_kernel,
@@ -383,24 +452,31 @@
         name="lower_weight",
     )(pos, lower_own, lower_other)
 
-    lower_full, act_low = lax.optimization_barrier((lower_full, act_low))
-    act_low_rows = act_low.T
-    mid_parts, upper_got, act_low_rows = lax.optimization_barrier((mid_parts, upper_got, act_low_rows))
-    low_part, lower_taps = pl.pallas_call(
-        lower_kernel,
-        out_shape=(jax.ShapeDtypeStruct((8, 80, 1024), BF), jax.ShapeDtypeStruct((512, 1024), BF)),
+    mid_parts, upper_got = lax.optimization_barrier((mid_parts, upper_got))
+    lower_taps = pl.pallas_call(
+        lower_taps_kernel,
+        out_shape=jax.ShapeDtypeStruct((512, 1024), BF),
         in_specs=[SMEM] + [VMEM] * 3,
-        out_specs=(HBM, VMEM),
-        scratch_shapes=[pltpu.VMEM((8, 80, 1024), BF), pltpu.SemaphoreType.DMA((4,))],
-        compiler_params=PARAMS,
-        name="lower",
-    )(pos, mid_parts, slope_lower, lower_full)
-    lower_keep, lower_send = weight_grad(pos, act_low_rows, lower_taps)
-    low_part, _ = lax.optimization_barrier((low_part, lower_keep))
+        out_specs=VMEM,
+        compiler_params=PARAMS,
+        name="lower_taps",
+    )(pos, mid_parts, slope_lower, edges)
+    lower_keep, lower_send = weight_grad(pos, act_low_rows, lower_taps, False)
     lower_got = shifted(lower_send, "c", NC, 1)
     own_sum, *sends = core_sum((upper_keep, upper_got), (lower_keep, lower_got))
+    lower_taps, _ = lax.optimization_barrier((lower_taps, lower_keep))
+    low_part = pl.pallas_call(
+        low_kernel,
+        out_shape=pltpu.HBM((8, 80, 1024), BF),
+        in_specs=[VMEM] * 2,
+        out_specs=HBM,
+        scratch_shapes=[pltpu.VMEM((8, 80, 1024), BF), pltpu.SemaphoreType.DMA((4,))],
+        compiler_params=PARAMS,
+        name="low",
+    )(lower_taps, lower_full)
+    low_part, _ = lax.optimization_barrier((low_part, lower_got))
+    low_parts = lax.all_to_all(low_part, DP, split_axis=0, concat_axis=0, tiled=True)
     got = [shifted(send, "y", NY, s + 1) for s, send in enumerate(sends)]
-    low_parts = lax.all_to_all(low_part, DP, split_axis=0, concat_axis=0, tiled=True)
     scales = tuple(1.0 / math.sqrt(act.shape[0] * NZ * NY * NC) for act in (act_mid, act_low))
     grad_upper, grad_lower = z_sum(own_sum, got, scales, weight_upper.shape, weight_lower.shape)
 

time: 98.6 us -> 94.3 us (0.956); the launches traced: 96.7 us -> 93.8 us
  starting transfers between devices: 54.9 us -> 44.7 us
  waiting for transfers between devices: 22.2 us -> 29.1 us
  Pallas kernels: 14.9 us -> 16.2 us
    ppermute x16, waiting for transfers between devices: 21.6 us -> 26.4 us  [shifted(): lax.ppermute(block, axis, [(i, (i + step) % count) for i in range(count)])]
    ppermute x16, starting transfers between devices: 28.7 us -> 24.1 us  [shifted(): lax.ppermute(block, axis, [(i, (i + step) % count) for i in range(count)])]
    ppermute x2 -> x0, starting transfers between devices: 4.33 us -> none  [the longest x1 2.41 us: neighbours(): low = lax.ppermute(block[:, :, -128:], SEQ, forward)]
    all_to_all x1, waiting for transfers between devices: 0.5 us -> 2.66 us  [local(): lax.all_to_all(mid_part, DP, split_axis=0, concat_axis=0, tiled=True)]
    pallas_call x5 -> x7, Pallas kernels: 11.1 us -> 12.9 us  [the longest x2 4.09 us: weight_grad(): pl.pallas_call(fetched_weight_grad_kernel if fetch else weight_grad_kerne...]
    unnamed x12 -> x15, local copies, waits for them, and re-layouts: 0.77 us -> 2.51 us
    optimization_barrier x1 -> x0, local copies, waits for them, and re-layouts: 1.61 us -> none  [local(): lower_full, act_low = lax.optimization_barrier((lower_full, act_low))]
    all_to_all x1, starting transfers between devices: 5.06 us -> 3.71 us  [local(): lax.all_to_all(low_part, DP, split_axis=0, concat_axis=0, tiled=True)]
  transfers between devices with their start and end apart: 21 -> 19, of which waited for: 13 -> 12; matrix products, arithmetic and copies ran while one was open for 3% -> 2% of each run, Pallas kernels for 5% -> 11%
where the time goes in v4:
time: 94.3 us; the launch traced here: 93.8 us
  starting transfers between devices  44.7 us (47%)
  waiting for transfers between devices  29.1 us (31%)
  Pallas kernels  16.2 us (17%)
  local copies, waits for them, and re-layouts  2.58 us (3%)
    ppermute x16, waiting for transfers between devices, shifted(): lax.ppermute(block, axis, [(i, (i + step) % count) for i in range(count)])  26.4 us
    ppermute x16, starting transfers between devices, shifted(): lax.ppermute(block, axis, [(i, (i + step) % count) for i in range(count)])  24.1 us
    all_to_all x1, starting transfers between devices, local(): lax.all_to_all(packed, ('zh', 'y'), split_axis=0, concat_axis=0, tiled=True)  11.6 us
    all_to_all x1, starting transfers between devices, local(): lax.all_to_all(mid_part, DP, split_axis=0, concat_axis=0, tiled=True)  5.27 us
    pallas_call x2, Pallas kernels, weight_grad(): pl.pallas_call(fetched_weight_grad_kernel if fetch else weight_grad_kerne...  4.09 us
    all_to_all x1, starting transfers between devices, local(): lax.all_to_all(low_part, DP, split_axis=0, concat_axis=0, tiled=True)  3.71 us
    pallas_call x1, Pallas kernels, local(): pl.pallas_call(upper_kernel, out_shape=(pltpu.HBM((8, 96, 512), BF), pltp...  2.75 us
    all_to_all x1, waiting for transfers between devices, local(): lax.all_to_all(mid_part, DP, split_axis=0, concat_axis=0, tiled=True)  2.66 us
  transfers between devices with their start and end apart: 19, of which 12 were waited for; matrix products, arithmetic and copies ran while one was open for 2% of the time, Pallas kernels for 11%

profile of v4, /device:TPU:8, one launch (start us, length us, event | category | flops | bytes accessed | tf_op | source)
XLA Modules:
  0.0 93.8 jit_solution(449498164276517675)
XLA Ops:
  0.7 2.2 %pack.1 = (bf16[16,32,512]{2,1,0:T(8,128)(2,1)}, bf16[24,512]{1,0:T(8,128)(2,1)S(1)}) custom-call(bf16[3,8192]{1,0:T(4,128)(2,1)} %bitcast.24, bf16[5,22,96]{2,1,0:T(8,128)(2,1)} %upper_hbm.1, bf16[5,20,88]{2,1,0:T(8,128)(2,1)} %lower_hbm.1, bf16[96,512]{1,0:T(8,128)(2,1)} %bitcast.22, bf16[88,1024]{1,0:T(8,128)(2,1)} %bitcast.20), custom_call_target="tpu_custom_call" | custom-call | tf_op jit(solution)/shard_map/pack/pallas_call | solution.py:385
  2.8 11.6 %all-to-all-start = ((bf16[16,32,512]{2,1,0:T(8,128)(2,1)}), bf16[16,32,512]{2,1,0:T(8,128)(2,1)S(1)}, u32[]{:S(2)}, u32[]{:S(2)}) async-start(bf16[16,32,512]{2,1,0:T(8,128)(2,1)} %get-tuple-element.45), calls=%async_computation | async-start | bytes 1048576 | tf_op jit(solution)/shard_map/all_to_all | solution.py:410
  14.4 3.6 %collective-permute-start.2 = (bf16[24,512]{1,0:T(8,128)(2,1)S(1)}, bf16[24,512]{1,0:T(8,128)(2,1)S(1)}, u32[]{:S(2)}, u32[]{:S(2)}) collective-permute-start(bf16[24,512]{1,0:T(8,128)(2,1)S(1)} %get-tuple-element.55), channel_id=1, source_target_pairs={{0,24},{8,0},{16,8},{24,16},{1,25},{9,1},{17,9},{25,17},{2,26},{10... | collective-permute-start | bytes 73736 | tf_op jit(solution)/shard_map/ppermute | solution.py:32
  18.0 2.4 %collective-permute-start.1 = (bf16[24,512]{1,0:T(8,128)(2,1)S(1)}, bf16[24,512]{1,0:T(8,128)(2,1)S(1)}, u32[]{:S(2)}, u32[]{:S(2)}) collective-permute-start(bf16[24,512]{1,0:T(8,128)(2,1)S(1)} %get-tuple-element.55), channel_id=1, source_target_pairs={{0,16},{8,24},{16,0},{24,8},{1,17},{9,25},{17,1},{25,9},{2,18},{10... | collective-permute-start | bytes 73736 | tf_op jit(solution)/shard_map/ppermute | solution.py:32
  20.3 2.4 %collective-permute-start = (bf16[24,512]{1,0:T(8,128)(2,1)S(1)}, bf16[24,512]{1,0:T(8,128)(2,1)S(1)}, u32[]{:S(2)}, u32[]{:S(2)}) collective-permute-start(bf16[24,512]{1,0:T(8,128)(2,1)S(1)} %get-tuple-element.55), channel_id=1, source_target_pairs={{0,8},{8,16},{16,24},{24,0},{1,9},{9,17},{17,25},{25,1},{2,10},{10... | collective-permute-start | bytes 73736 | tf_op jit(solution)/shard_map/ppermute | solution.py:32
  22.7 0.1 reshape.12
  22.8 0.2 fusion.6.slope_ref
  23.0 0.1 fusion.13.slope_ref
  23.1 1.6 %copy.11 = bf16[1024,640]{0,1:T(8,128)(2,1)S(1)} copy(bf16[1024,640]{1,0:T(8,128)(2,1)} %param.10) | data formatting | bytes 2621440 | tf_op args[3]
  24.7 5.3 %collective-permute-done.2 = bf16[24,512]{1,0:T(8,128)(2,1)S(1)} collective-permute-done((bf16[24,512]{1,0:T(8,128)(2,1)S(1)}, bf16[24,512]{1,0:T(8,128)(2,1)S(1)}, u32[]{:S(2)}, u32[]{:S(2)}) %collective-permute-start.2) | collective-permute-done | bytes 24608 | tf_op jit(solution)/shard_map/ppermute | solution.py:32
  30.0 2.1 %collective-permute-done.1 = bf16[24,512]{1,0:T(8,128)(2,1)S(1)} collective-permute-done((bf16[24,512]{1,0:T(8,128)(2,1)S(1)}, bf16[24,512]{1,0:T(8,128)(2,1)S(1)}, u32[]{:S(2)}, u32[]{:S(2)}) %collective-permute-start.1) | collective-permute-done | bytes 24608 | tf_op jit(solution)/shard_map/ppermute | solution.py:32
  32.1 0.0 collective-permute-done
  32.2 0.1 pad_add_fusion.pos_ref
  32.2 1.8 %collective-permute-done.3.other_ref = bf16[16,32,512]{2,1,0:T(8,128)(2,1)S(1)} collective-permute-done((bf16[16,32,512]{2,1,0:T(8,128)(2,1)S(1)}, bf16[16,32,512]{2,1,0:T(8,128)(2,1)S(1)}, u32[]{:S(2)}, u32[]{:S(2)}) %collective-permute-start.3) | collective-permute-done | bytes 524320 | tf_op jit(solution)/shard_map/ppermute | solution.py:32
  34.1 2.8 %upper.1 = (bf16[8,96,512]{2,1,0:T(8,128)(2,1)}, bf16[512,512]{1,0:T(8,128)(2,1)}, f32[96,256]{1,0:T(8,128)}) custom-call(s32[3]{0:T(128)S(1)} %pad_add_fusion.pos_ref, f32[96,512]{1,0:T(8,128)S(1)} %fusion.13.slope_ref, bf16[16,32,512]{2,1,0:T(8,128)(2,1)S(1)} %all-to-all-done.own_ref, bf16[16,32,512]{2,1,0:T(8,128)(2,1)S(1)} %collective-permute-done.3.other_ref), custom_call_target="tpu_custom_call" | custom-call | tf_op jit(solution)/shard_map/upper/pallas_call | solution.py:416
  36.8 5.3 %all-to-all-start.1 = ((bf16[8,96,512]{2,1,0:T(8,128)(2,1)}), bf16[8,96,512]{2,1,0:T(8,128)(2,1)S(1)}, u32[]{:S(2)}, u32[]{:S(2)}) async-start(bf16[8,96,512]{2,1,0:T(8,128)(2,1)} %get-tuple-element.49), calls=%async_computation.1 | async-start | bytes 1572864 | tf_op jit(solution)/shard_map/all_to_all | solution.py:434
  42.1 1.3 %collective-permute-start.6 = (bf16[4,24,512]{2,1,0:T(8,128)(2,1)S(1)}, bf16[4,24,512]{2,1,0:T(8,128)(2,1)S(1)}, u32[]{:S(2)}, u32[]{:S(2)}) collective-permute-start(bf16[4,24,512]{2,1,0:T(8,128)(2,1)S(1)} %pad_maximum_fusion.refs_0_), channel_id=1, source_target_pairs={{0,6},{2,0},{4,2},{6,4},{1,7},{3,1},{5,3},{7,5},{8,14},{10,8},{12,... | collective-permute-start | bytes 294920 | tf_op jit(solution)/shard_map/ppermute | solution.py:32
  43.4 1.7 %collective-permute-start.5 = (bf16[4,24,512]{2,1,0:T(8,128)(2,1)S(1)}, bf16[4,24,512]{2,1,0:T(8,128)(2,1)S(1)}, u32[]{:S(2)}, u32[]{:S(2)}) collective-permute-start(bf16[4,24,512]{2,1,0:T(8,128)(2,1)S(1)} %pad_maximum_fusion.refs_0_), channel_id=1, source_target_pairs={{0,4},{2,6},{4,0},{6,2},{1,5},{3,7},{5,1},{7,3},{8,12},{10,14},{12... | collective-permute-start | bytes 294920 | tf_op jit(solution)/shard_map/ppermute | solution.py:32
  45.1 1.8 %collective-permute-start.4 = (bf16[4,24,512]{2,1,0:T(8,128)(2,1)S(1)}, bf16[4,24,512]{2,1,0:T(8,128)(2,1)S(1)}, u32[]{:S(2)}, u32[]{:S(2)}) collective-permute-start(bf16[4,24,512]{2,1,0:T(8,128)(2,1)S(1)} %pad_maximum_fusion.refs_0_), channel_id=1, source_target_pairs={{0,2},{2,4},{4,6},{6,0},{1,3},{3,5},{5,7},{7,1},{8,10},{10,12},{12... | collective-permute-start | bytes 294920 | tf_op jit(solution)/shard_map/ppermute | solution.py:32
  46.9 2.5 %weight_grad.2 = (f32[4,4,24,512]{3,2,1,0:T(8,128)S(1)}, bf16[4,4,24,512]{3,2,1,0:T(8,128)(2,1)S(1)}) custom-call(s32[3]{0:T(128)S(1)} %pad_add_fusion.pos_ref, bf16[704,512]{1,0:T(8,128)(2,1)} %bitcast.19, bf16[512,512]{1,0:T(8,128)(2,1)} %get-tuple-element.54.taps_hbm), custom_call_target="tpu_custom_call" | custom-call | tf_op jit(solution)/shard_map/weight_grad/pallas_call | solution.py:371
  49.4 0.9 copy-done
  50.3 0.3 collective-permute-done.4.refs_1_
  50.7 0.1 collective-permute-start.7
  50.8 0.5 collective-permute-start.8
  51.3 1.3 %collective-permute-done.7.got_upper_hbm = bf16[4,4,24,512]{3,2,1,0:T(8,128)(2,1)} collective-permute-done((bf16[4,4,24,512]{3,2,1,0:T(8,128)(2,1)S(1)}, bf16[4,4,24,512]{3,2,1,0:T(8,128)(2,1)}, u32[]{:S(2)}, u32[]{:S(2)}) %collective-permute-start.7) | collective-permute-done | bytes 393248 | tf_op jit(solution)/shard_map/ppermute | solution.py:32
  52.6 2.7 %all-to-all-done.1.mid_ref = bf16[8,96,512]{2,1,0:T(8,128)(2,1)S(1)} async-done(((bf16[8,96,512]{2,1,0:T(8,128)(2,1)}), bf16[8,96,512]{2,1,0:T(8,128)(2,1)S(1)}, u32[]{:S(2)}, u32[]{:S(2)}) %all-to-all-start.1) | async-done | bytes 786464 | tf_op jit(solution)/shard_map/all_to_all | solution.py:434
  55.3 1.0 %lower_taps.1.taps_ref = bf16[512,1024]{1,0:T(8,128)(2,1)S(1)} custom-call(s32[3]{0:T(128)S(1)} %pad_add_fusion.pos_ref, bf16[8,96,512]{2,1,0:T(8,128)(2,1)S(1)} %all-to-all-done.1.mid_ref, f32[96,1024]{1,0:T(8,128)S(1)} %fusion.6.slope_ref, f32[96,256]{1,0:T(8,128)S(1)} %copy-done.4), custom_call_target="tpu_custom_call" | custom-call | tf_op jit(solution)/shard_map/lower_taps/pallas_call | solution.py:456
  56.3 1.6 %weight_grad.3 = (f32[4,4,24,512]{3,2,1,0:T(8,128)S(1)}, bf16[4,4,24,512]{3,2,1,0:T(8,128)(2,1)S(1)}) custom-call(s32[3]{0:T(128)S(1)} %pad_add_fusion.pos_ref, bf16[640,1024]{1,0:T(8,128)(2,1)S(1)} %bitcast.17, bf16[512,1024]{1,0:T(8,128)(2,1)S(1)} %lower_taps.1.taps_ref), custom_call_target="tpu_custom_call" | custom-call | tf_op jit(solution)/shard_map/weight_grad/pallas_call | solution.py:371
  57.9 0.1 collective-permute-start.9
  58.0 1.4 %lower_weight.1.w_ref = bf16[640,512]{1,0:T(8,128)(2,1)S(1)} custom-call(s32[3]{0:T(128)S(1)} %pad_add_fusion.pos_ref, bf16[16,24,512]{2,1,0:T(8,128)(2,1)S(1)} %join.1.own_ref, bf16[16,24,512]{2,1,0:T(8,128)(2,1)} %collective-permute-done.8.other_ref), custom_call_target="tpu_custom_call" | custom-call | tf_op jit(solution)/shard_map/lower_weight/pallas_call | solution.py:445
  59.4 1.9 %low.1 = bf16[8,80,1024]{2,1,0:T(8,128)(2,1)} custom-call(bf16[512,1024]{1,0:T(8,128)(2,1)S(1)} %lower_taps.1.taps_ref, bf16[640,512]{1,0:T(8,128)(2,1)S(1)} %lower_weight.1.w_ref), custom_call_target="tpu_custom_call" | custom-call | tf_op jit(solution)/shard_map/low/pallas_call | solution.py:468
  61.3 3.7 %all-to-all-start.2 = ((bf16[8,80,1024]{2,1,0:T(8,128)(2,1)}), bf16[8,80,1024]{2,1,0:T(8,128)(2,1)S(1)}, u32[]{:S(2)}, u32[]{:S(2)}) async-start(bf16[8,80,1024]{2,1,0:T(8,128)(2,1)} %low.1), calls=%async_computation.2 | async-start | bytes 2621440 | tf_op jit(solution)/shard_map/all_to_all | solution.py:478
  65.0 1.1 %core_sum.1 = (f32[4,48,512]{2,1,0:T(8,128)S(1)}, bf16[4,48,512]{2,1,0:T(8,128)(2,1)S(1)}, bf16[4,48,512]{2,1,0:T(8,128)(2,1)S(1)}, bf16[4,48,512]{2,1,0:T(8,128)(2,1)S(1)}) custom-call(f32[4,4,24,512]{3,2,1,0:T(8,128)S(1)} %copy-done.1, bf16[4,4,24,512]{3,2,1,0:T(8,128)(2,1)} %collective-permute-done.7.got_upper_hbm, f32[4,4,24,512]{3,2,1,0:T(8,128)S(1)} %copy-done.3, ...), custom_call_target="tpu_custom_call" | custom-call | tf_op jit(solution)/shard_map/core_sum/pallas_call | solution.py:112
  66.1 1.7 %collective-permute-start.10 = (bf16[4,48,512]{2,1,0:T(8,128)(2,1)S(1)}, bf16[4,48,512]{2,1,0:T(8,128)(2,1)S(1)}, u32[]{:S(2)}, u32[]{:S(2)}) collective-permute-start(bf16[4,48,512]{2,1,0:T(8,128)(2,1)S(1)} %get-tuple-element.78), channel_id=1, source_target_pairs={{0,2},{2,4},{4,6},{6,0},{1,3},{3,5},{5,7},{7,1},{8,10},{10,12},{12... | collective-permute-start | bytes 589832 | tf_op jit(solution)/shard_map/ppermute | solution.py:32
  67.8 2.4 %collective-permute-start.11 = (bf16[4,48,512]{2,1,0:T(8,128)(2,1)S(1)}, bf16[4,48,512]{2,1,0:T(8,128)(2,1)S(1)}, u32[]{:S(2)}, u32[]{:S(2)}) collective-permute-start(bf16[4,48,512]{2,1,0:T(8,128)(2,1)S(1)} %get-tuple-element.79), channel_id=1, source_target_pairs={{0,4},{2,6},{4,0},{6,2},{1,5},{3,7},{5,1},{7,3},{8,12},{10,14},{12... | collective-permute-start | bytes 589832 | tf_op jit(solution)/shard_map/ppermute | solution.py:32
  70.3 0.8 collective-permute-start.12
  71.1 3.0 %collective-permute-done.10.refs_0_ = bf16[4,48,512]{2,1,0:T(8,128)(2,1)S(1)} collective-permute-done((bf16[4,48,512]{2,1,0:T(8,128)(2,1)S(1)}, bf16[4,48,512]{2,1,0:T(8,128)(2,1)S(1)}, u32[]{:S(2)}, u32[]{:S(2)}) %collective-permute-start.10) | collective-permute-done | bytes 196640 | tf_op jit(solution)/shard_map/ppermute | solution.py:32
  74.1 3.0 %collective-permute-done.11.refs_1_ = bf16[4,48,512]{2,1,0:T(8,128)(2,1)S(1)} collective-permute-done((bf16[4,48,512]{2,1,0:T(8,128)(2,1)S(1)}, bf16[4,48,512]{2,1,0:T(8,128)(2,1)S(1)}, u32[]{:S(2)}, u32[]{:S(2)}) %collective-permute-start.11) | collective-permute-done | bytes 196640 | tf_op jit(solution)/shard_map/ppermute | solution.py:32
  77.1 3.2 %collective-permute-done.12.refs_2_ = bf16[4,48,512]{2,1,0:T(8,128)(2,1)S(1)} collective-permute-done((bf16[4,48,512]{2,1,0:T(8,128)(2,1)S(1)}, bf16[4,48,512]{2,1,0:T(8,128)(2,1)S(1)}, u32[]{:S(2)}, u32[]{:S(2)}) %collective-permute-start.12) | collective-permute-done | bytes 196640 | tf_op jit(solution)/shard_map/ppermute | solution.py:32
  80.4 0.1 y_sum.1
  80.5 1.0 %collective-permute-start.13 = (bf16[48,512]{1,0:T(8,128)(2,1)S(1)}, bf16[48,512]{1,0:T(8,128)(2,1)S(1)}, u32[]{:S(2)}, u32[]{:S(2)}) collective-permute-start(bf16[48,512]{1,0:T(8,128)(2,1)S(1)} %get-tuple-element.82), channel_id=1, source_target_pairs={{0,8},{8,16},{16,24},{24,0},{1,9},{9,17},{17,25},{25,1},{2,10},{10... | collective-permute-start | bytes 147464 | tf_op jit(solution)/shard_map/ppermute | solution.py:32
  81.5 2.6 %collective-permute-start.14 = (bf16[48,512]{1,0:T(8,128)(2,1)S(1)}, bf16[48,512]{1,0:T(8,128)(2,1)S(1)}, u32[]{:S(2)}, u32[]{:S(2)}) collective-permute-start(bf16[48,512]{1,0:T(8,128)(2,1)S(1)} %get-tuple-element.83), channel_id=1, source_target_pairs={{0,16},{8,24},{16,0},{24,8},{1,17},{9,25},{17,1},{25,9},{2,18},{10... | collective-permute-start | bytes 147464 | tf_op jit(solution)/shard_map/ppermute | solution.py:32
  84.1 1.8 %collective-permute-start.15 = (bf16[48,512]{1,0:T(8,128)(2,1)S(1)}, bf16[48,512]{1,0:T(8,128)(2,1)S(1)}, u32[]{:S(2)}, u32[]{:S(2)}) collective-permute-start(bf16[48,512]{1,0:T(8,128)(2,1)S(1)} %get-tuple-element.84), channel_id=1, source_target_pairs={{0,24},{8,0},{16,8},{24,16},{1,25},{9,1},{17,9},{25,17},{2,26},{10... | collective-permute-start | bytes 147464 | tf_op jit(solution)/shard_map/ppermute | solution.py:32
  85.9 2.0 %collective-permute-done.13.refs_0_ = bf16[48,512]{1,0:T(8,128)(2,1)S(1)} collective-permute-done((bf16[48,512]{1,0:T(8,128)(2,1)S(1)}, bf16[48,512]{1,0:T(8,128)(2,1)S(1)}, u32[]{:S(2)}, u32[]{:S(2)}) %collective-permute-start.13) | collective-permute-done | bytes 49184 | tf_op jit(solution)/shard_map/ppermute | solution.py:32
  87.8 1.7 %collective-permute-done.14.refs_1_ = bf16[48,512]{1,0:T(8,128)(2,1)S(1)} collective-permute-done((bf16[48,512]{1,0:T(8,128)(2,1)S(1)}, bf16[48,512]{1,0:T(8,128)(2,1)S(1)}, u32[]{:S(2)}, u32[]{:S(2)}) %collective-permute-start.14) | collective-permute-done | bytes 49184 | tf_op jit(solution)/shard_map/ppermute | solution.py:32
  89.5 2.5 %collective-permute-done.15.refs_2_ = bf16[48,512]{1,0:T(8,128)(2,1)S(1)} collective-permute-done((bf16[48,512]{1,0:T(8,128)(2,1)S(1)}, bf16[48,512]{1,0:T(8,128)(2,1)S(1)}, u32[]{:S(2)}, u32[]{:S(2)}) %collective-permute-start.15) | collective-permute-done | bytes 49184 | tf_op jit(solution)/shard_map/ppermute | solution.py:32
  92.0 0.9 z_sum.1
  93.0 0.8 low_total.1
  (23 shorter events, 0.1 us)
Async XLA Ops:
  0.6 22.1 %copy-start.5 = (bf16[1024,88]{0,1:T(8,128)(2,1)S(1)}, bf16[1024,88]{0,1:T(8,128)(2,1)}, u32[]{:S(2)}) copy-start(bf16[1024,88]{0,1:T(8,128)(2,1)} %param.11) | copy-start | bytes 540676
  0.6 22.3 %copy-start.6 = (bf16[512,96]{0,1:T(8,128)(2,1)S(1)}, bf16[512,96]{0,1:T(8,128)(2,1)}, u32[]{:S(2)}) copy-start(bf16[512,96]{0,1:T(8,128)(2,1)} %param.9) | copy-start | bytes 294916
  2.8 29.3 %all-to-all-start = ((bf16[16,32,512]{2,1,0:T(8,128)(2,1)}), bf16[16,32,512]{2,1,0:T(8,128)(2,1)S(1)}, u32[]{:S(2)}, u32[]{:S(2)}) async-start(bf16[16,32,512]{2,1,0:T(8,128)(2,1)} %get-tuple-element.45), calls=%async_computation | async-start | bytes 1048576 | tf_op jit(solution)/shard_map/all_to_all | solution.py:410
  14.4 15.6 %collective-permute-start.2 = (bf16[24,512]{1,0:T(8,128)(2,1)S(1)}, bf16[24,512]{1,0:T(8,128)(2,1)S(1)}, u32[]{:S(2)}, u32[]{:S(2)}) collective-permute-start(bf16[24,512]{1,0:T(8,128)(2,1)S(1)} %get-tuple-element.55), channel_id=1, source_target_pairs={{0,24},{8,0},{16,8},{24,16},{1,25},{9,1},{17,9},{25,17},{2,26},{10... | collective-permute-start | bytes 73736 | tf_op jit(solution)/shard_map/ppermute | solution.py:32
  18.0 14.2 %collective-permute-start.1 = (bf16[24,512]{1,0:T(8,128)(2,1)S(1)}, bf16[24,512]{1,0:T(8,128)(2,1)S(1)}, u32[]{:S(2)}, u32[]{:S(2)}) collective-permute-start(bf16[24,512]{1,0:T(8,128)(2,1)S(1)} %get-tuple-element.55), channel_id=1, source_target_pairs={{0,16},{8,24},{16,0},{24,8},{1,17},{9,25},{17,1},{25,9},{2,18},{10... | collective-permute-start | bytes 73736 | tf_op jit(solution)/shard_map/ppermute | solution.py:32
  20.3 11.8 %collective-permute-start = (bf16[24,512]{1,0:T(8,128)(2,1)S(1)}, bf16[24,512]{1,0:T(8,128)(2,1)S(1)}, u32[]{:S(2)}, u32[]{:S(2)}) collective-permute-start(bf16[24,512]{1,0:T(8,128)(2,1)S(1)} %get-tuple-element.55), channel_id=1, source_target_pairs={{0,8},{8,16},{16,24},{24,0},{1,9},{9,17},{17,25},{25,1},{2,10},{10... | collective-permute-start | bytes 73736 | tf_op jit(solution)/shard_map/ppermute | solution.py:32
  32.1 1.9 %collective-permute-start.3 = (bf16[16,32,512]{2,1,0:T(8,128)(2,1)S(1)}, bf16[16,32,512]{2,1,0:T(8,128)(2,1)S(1)}, u32[]{:S(2)}, u32[]{:S(2)}) collective-permute-start(bf16[16,32,512]{2,1,0:T(8,128)(2,1)S(1)} %all-to-all-done.own_ref), channel_id=1, source_target_pairs={{0,1},{1,0},{2,3},{3,2},{4,5},{5,4},{6,7},{7,6},{8,9},{9,8},{10,11... | collective-permute-start | bytes 1572872 | tf_op jit(solution)/shard_map/ppermute | solution.py:32
  36.8 18.5 %all-to-all-start.1 = ((bf16[8,96,512]{2,1,0:T(8,128)(2,1)}), bf16[8,96,512]{2,1,0:T(8,128)(2,1)S(1)}, u32[]{:S(2)}, u32[]{:S(2)}) async-start(bf16[8,96,512]{2,1,0:T(8,128)(2,1)} %get-tuple-element.49), calls=%async_computation.1 | async-start | bytes 1572864 | tf_op jit(solution)/shard_map/all_to_all | solution.py:434
  42.1 13.2 %copy-start.4 = (f32[96,256]{1,0:T(8,128)S(1)}, f32[96,256]{1,0:T(8,128)}, u32[]{:S(2)}) copy-start(f32[96,256]{1,0:T(8,128)} %get-tuple-element.68.edge_ref) | copy-start | bytes 294916
  42.1 8.2 %collective-permute-start.6 = (bf16[4,24,512]{2,1,0:T(8,128)(2,1)S(1)}, bf16[4,24,512]{2,1,0:T(8,128)(2,1)S(1)}, u32[]{:S(2)}, u32[]{:S(2)}) collective-permute-start(bf16[4,24,512]{2,1,0:T(8,128)(2,1)S(1)} %pad_maximum_fusion.refs_0_), channel_id=1, source_target_pairs={{0,6},{2,0},{4,2},{6,4},{1,7},{3,1},{5,3},{7,5},{8,14},{10,8},{12,... | collective-permute-start | bytes 294920 | tf_op jit(solution)/shard_map/ppermute | solution.py:32
  43.4 6.9 %collective-permute-start.5 = (bf16[4,24,512]{2,1,0:T(8,128)(2,1)S(1)}, bf16[4,24,512]{2,1,0:T(8,128)(2,1)S(1)}, u32[]{:S(2)}, u32[]{:S(2)}) collective-permute-start(bf16[4,24,512]{2,1,0:T(8,128)(2,1)S(1)} %pad_maximum_fusion.refs_0_), channel_id=1, source_target_pairs={{0,4},{2,6},{4,0},{6,2},{1,5},{3,7},{5,1},{7,3},{8,12},{10,14},{12... | collective-permute-start | bytes 294920 | tf_op jit(solution)/shard_map/ppermute | solution.py:32
  45.1 5.5 %collective-permute-start.4 = (bf16[4,24,512]{2,1,0:T(8,128)(2,1)S(1)}, bf16[4,24,512]{2,1,0:T(8,128)(2,1)S(1)}, u32[]{:S(2)}, u32[]{:S(2)}) collective-permute-start(bf16[4,24,512]{2,1,0:T(8,128)(2,1)S(1)} %pad_maximum_fusion.refs_0_), channel_id=1, source_target_pairs={{0,2},{2,4},{4,6},{6,0},{1,3},{3,5},{5,7},{7,1},{8,10},{10,12},{12... | collective-permute-start | bytes 294920 | tf_op jit(solution)/shard_map/ppermute | solution.py:32
  49.4 0.9 copy-start
  50.7 1.9 %collective-permute-start.7 = (bf16[4,4,24,512]{3,2,1,0:T(8,128)(2,1)S(1)}, bf16[4,4,24,512]{3,2,1,0:T(8,128)(2,1)}, u32[]{:S(2)}, u32[]{:S(2)}) collective-permute-start(bf16[4,4,24,512]{3,2,1,0:T(8,128)(2,1)S(1)} %get-tuple-element.65), channel_id=1, source_target_pairs={{0,1},{1,0},{2,3},{3,2},{4,5},{5,4},{6,7},{7,6},{8,9},{9,8},{10,11... | collective-permute-start | bytes 1179656 | tf_op jit(solution)/shard_map/ppermute | solution.py:32
  50.8 7.2 %collective-permute-start.8 = (bf16[16,24,512]{2,1,0:T(8,128)(2,1)S(1)}, bf16[16,24,512]{2,1,0:T(8,128)(2,1)}, u32[]{:S(2)}, u32[]{:S(2)}) collective-permute-start(bf16[16,24,512]{2,1,0:T(8,128)(2,1)S(1)} %join.1.own_ref), channel_id=1, source_target_pairs={{0,1},{1,0},{2,3},{3,2},{4,5},{5,4},{6,7},{7,6},{8,9},{9,8},{10,11... | collective-permute-start | bytes 1179656 | tf_op jit(solution)/shard_map/ppermute | solution.py:32
  57.9 1.5 %copy-start.2 = (f32[4,4,24,512]{3,2,1,0:T(8,128)}, f32[4,4,24,512]{3,2,1,0:T(8,128)S(1)}, u32[]{:S(2)}) copy-start(f32[4,4,24,512]{3,2,1,0:T(8,128)S(1)} %get-tuple-element.70.keep_lower_ref) | copy-start | bytes 2359300
  57.9 3.4 %collective-permute-start.9 = (bf16[4,4,24,512]{3,2,1,0:T(8,128)(2,1)S(1)}, bf16[4,4,24,512]{3,2,1,0:T(8,128)(2,1)S(1)}, u32[]{:S(2)}, u32[]{:S(2)}) collective-permute-start(bf16[4,4,24,512]{3,2,1,0:T(8,128)(2,1)S(1)} %get-tuple-element.73), channel_id=1, source_target_pairs={{0,1},{1,0},{2,3},{3,2},{4,5},{5,4},{6,7},{7,6},{8,9},{9,8},{10,11... | collective-permute-start | bytes 1179656 | tf_op jit(solution)/shard_map/ppermute | solution.py:32
  61.3 3.8 %copy-start.1 = (f32[4,4,24,512]{3,2,1,0:T(8,128)S(1)}, f32[4,4,24,512]{3,2,1,0:T(8,128)}, u32[]{:S(2)}) copy-start(f32[4,4,24,512]{3,2,1,0:T(8,128)} %copy-done) | copy-start | bytes 2359300
  61.3 3.8 %copy-start.3 = (f32[4,4,24,512]{3,2,1,0:T(8,128)S(1)}, f32[4,4,24,512]{3,2,1,0:T(8,128)}, u32[]{:S(2)}) copy-start(f32[4,4,24,512]{3,2,1,0:T(8,128)} %copy-done.2) | copy-start | bytes 2359300
  61.3 31.7 %all-to-all-start.2 = ((bf16[8,80,1024]{2,1,0:T(8,128)(2,1)}), bf16[8,80,1024]{2,1,0:T(8,128)(2,1)S(1)}, u32[]{:S(2)}, u32[]{:S(2)}) async-start(bf16[8,80,1024]{2,1,0:T(8,128)(2,1)} %low.1), calls=%async_computation.2 | async-start | bytes 2621440 | tf_op jit(solution)/shard_map/all_to_all | solution.py:478
  66.1 8.0 %collective-permute-start.10 = (bf16[4,48,512]{2,1,0:T(8,128)(2,1)S(1)}, bf16[4,48,512]{2,1,0:T(8,128)(2,1)S(1)}, u32[]{:S(2)}, u32[]{:S(2)}) collective-permute-start(bf16[4,48,512]{2,1,0:T(8,128)(2,1)S(1)} %get-tuple-element.78), channel_id=1, source_target_pairs={{0,2},{2,4},{4,6},{6,0},{1,3},{3,5},{5,7},{7,1},{8,10},{10,12},{12... | collective-permute-start | bytes 589832 | tf_op jit(solution)/shard_map/ppermute | solution.py:32
  67.8 9.3 %collective-permute-start.11 = (bf16[4,48,512]{2,1,0:T(8,128)(2,1)S(1)}, bf16[4,48,512]{2,1,0:T(8,128)(2,1)S(1)}, u32[]{:S(2)}, u32[]{:S(2)}) collective-permute-start(bf16[4,48,512]{2,1,0:T(8,128)(2,1)S(1)} %get-tuple-element.79), channel_id=1, source_target_pairs={{0,4},{2,6},{4,0},{6,2},{1,5},{3,7},{5,1},{7,3},{8,12},{10,14},{12... | collective-permute-start | bytes 589832 | tf_op jit(solution)/shard_map/ppermute | solution.py:32
  70.3 10.1 %collective-permute-start.12 = (bf16[4,48,512]{2,1,0:T(8,128)(2,1)S(1)}, bf16[4,48,512]{2,1,0:T(8,128)(2,1)S(1)}, u32[]{:S(2)}, u32[]{:S(2)}) collective-permute-start(bf16[4,48,512]{2,1,0:T(8,128)(2,1)S(1)} %get-tuple-element.80), channel_id=1, source_target_pairs={{0,6},{2,0},{4,2},{6,4},{1,7},{3,1},{5,3},{7,5},{8,14},{10,8},{12,... | collective-permute-start | bytes 589832 | tf_op jit(solution)/shard_map/ppermute | solution.py:32
  80.5 7.4 %collective-permute-start.13 = (bf16[48,512]{1,0:T(8,128)(2,1)S(1)}, bf16[48,512]{1,0:T(8,128)(2,1)S(1)}, u32[]{:S(2)}, u32[]{:S(2)}) collective-permute-start(bf16[48,512]{1,0:T(8,128)(2,1)S(1)} %get-tuple-element.82), channel_id=1, source_target_pairs={{0,8},{8,16},{16,24},{24,0},{1,9},{9,17},{17,25},{25,1},{2,10},{10... | collective-permute-start | bytes 147464 | tf_op jit(solution)/shard_map/ppermute | solution.py:32
  81.5 8.0 %collective-permute-start.14 = (bf16[48,512]{1,0:T(8,128)(2,1)S(1)}, bf16[48,512]{1,0:T(8,128)(2,1)S(1)}, u32[]{:S(2)}, u32[]{:S(2)}) collective-permute-start(bf16[48,512]{1,0:T(8,128)(2,1)S(1)} %get-tuple-element.83), channel_id=1, source_target_pairs={{0,16},{8,24},{16,0},{24,8},{1,17},{9,25},{17,1},{25,9},{2,18},{10... | collective-permute-start | bytes 147464 | tf_op jit(solution)/shard_map/ppermute | solution.py:32
  84.1 7.9 %collective-permute-start.15 = (bf16[48,512]{1,0:T(8,128)(2,1)S(1)}, bf16[48,512]{1,0:T(8,128)(2,1)S(1)}, u32[]{:S(2)}, u32[]{:S(2)}) collective-permute-start(bf16[48,512]{1,0:T(8,128)(2,1)S(1)} %get-tuple-element.84), channel_id=1, source_target_pairs={{0,24},{8,0},{16,8},{24,16},{1,25},{9,1},{17,9},{25,17},{2,26},{10... | collective-permute-start | bytes 147464 | tf_op jit(solution)/shard_map/ppermute | solution.py:32

commit v5 on v4

--- a/solution.py
+++ b/solution.py
@@ -120,14 +120,15 @@
     )(upper[0], got_upper, *lower)
 
 
-def z_sum(own, got, scales, upper_shape, lower_shape):
+def z_sum(own, got, low_grad, scales, upper_shape, lower_shape):
     block = jax.ShapeDtypeStruct((48, 512), BF)
     own, *sends = small_call(
         y_sum_kernel, "y_sum", (jax.ShapeDtypeStruct(block.shape, F32),) + (block,) * (NZ - 1), own, *got
     )
     got = [shifted(send, "zh", NZ, s + 1) for s, send in enumerate(sends)]
+    got, low_grad = lax.optimization_barrier((got, low_grad))
     outs = (jax.ShapeDtypeStruct(upper_shape, F32), jax.ShapeDtypeStruct(lower_shape, F32))
-    return small_call(functools.partial(z_sum_kernel, scales), "z_sum", outs, own, *got)
+    return low_grad, *small_call(functools.partial(z_sum_kernel, scales), "z_sum", outs, own, *got)
 
 
 def doubling():
@@ -161,11 +162,10 @@
     copies = [pltpu.make_async_copy(source, target, in_sem.at[i]) for i, (source, target) in enumerate(pieces)]
     for copy in copies:
         copy.start()
-    for copy in copies:
+    for copy in copies[:1] + copies[2:]:
         copy.wait()
     weight_ref[...] = jnp.zeros((48, 512), F32)
     weight_ref[0:22, :] = sum(mm(upper_ref[k], one_hot(96, 96 * k, False)) for k in range(KWIDTH))
-    weight_ref[24:44, :] = sum(mm(lower_ref[k], one_hot(88, 96 * k, True)) for k in range(KWIDTH))
     last, first = (pre_upper_ref[i].astype(F32).T for i in range(2))
     low_last, low_first = (pre_lower_ref[i].astype(F32).T for i in range(2))
     weight_ref[22:24, 0:96] = last[126:128]
@@ -177,7 +177,6 @@
         tower_rows_ref[8 * p + 6 : 8 * p + 7, 128:224] = first[2:3]
         tower_rows_ref[8 * p + 6 : 8 * p + 8, 256:344] = low_first[0:2]
     weight = weight_ref[0:24, :].astype(BF)
-    lower_out_ref[...] = weight_ref[24:48, :].astype(BF)
     tower = tower_ref[...].astype(F32)
     for p in range(16):
         at, row = 512 * p, 8 * p
@@ -191,6 +190,9 @@
         buf_ref[p, 0:24, :] = weight
         buf_ref[p, 24:32, :] = tower_rows_ref[row : row + 8, :].astype(BF)
         pltpu.make_async_copy(buf_ref.at[p], out_ref.at[p], sem.at[p]).start()
+    copies[1].wait()
+    weight_ref[24:44, :] = sum(mm(lower_ref[k], one_hot(88, 96 * k, True)) for k in range(KWIDTH))
+    lower_out_ref[...] = weight_ref[24:48, :].astype(BF)
     for p in range(16):
         pltpu.make_async_copy(buf_ref.at[p], out_ref.at[p], sem.at[p]).wait()
 
@@ -249,8 +251,8 @@
         taps_ref[96 * k : 96 * k + 96, :] = moved[:, 0:512].astype(BF)
         halo_ref[96 * k : 96 * k + 96, :] = jnp.where(lane == 127, moved[:, 640:768], after)
     out_copies = [
-        pltpu.make_async_copy(taps_ref, taps_out_ref, sem.at[8]),
-        pltpu.make_async_copy(edge_rows_ref, edge_out_ref, sem.at[9]),
+        pltpu.make_async_copy(taps_ref, taps_out_ref, sem.at[2]),
+        pltpu.make_async_copy(edge_rows_ref, edge_out_ref, sem.at[3]),
     ]
     out_copies[0].start()
     outside = lax.dot_general(
@@ -266,16 +268,14 @@
                 moved = pltpu.roll(outside, (768 - 96 * d) % 768, 1)[:, 0:256]
                 part = jnp.concatenate([part[0:16], jnp.where(row >= 6, moved, part[16:24]), part[24:]], axis=0)
             buf_ref[d, :, lanes] = part.astype(BF)
-    for d in range(8):
-        pltpu.make_async_copy(buf_ref.at[d], mid_ref.at[d], sem.at[d]).start()
+        out_copies.append(pltpu.make_async_copy(buf_ref.at[:, :, lanes], mid_ref.at[:, :, lanes], sem.at[half]))
+        out_copies[-1].start()
     edge_rows_ref[...] = jnp.zeros((96, 256), F32)
     for half, tile in enumerate(edge_tiles(pos_ref, other_ref, 256, False)):
         for group in range(4):
             rows, lanes = slice(24 * group, 24 * group + 22), slice(128 * half, 128 * half + 128)
             edge_rows_ref[rows, lanes] = tile[22 * group : 22 * group + 22]
     out_copies[1].start()
-    for d in range(8):
-        pltpu.make_async_copy(buf_ref.at[d], mid_ref.at[d], sem.at[d]).wait()
     for copy in out_copies:
         copy.wait()
 
@@ -426,7 +426,7 @@
             pltpu.VMEM((8, 96, 512), BF),
             pltpu.VMEM((512, 512), BF),
             pltpu.VMEM((96, 256), F32),
-            pltpu.SemaphoreType.DMA((10,)),
+            pltpu.SemaphoreType.DMA((4,)),
         ],
         compiler_params=PARAMS,
         name="upper",
@@ -477,9 +477,6 @@
     low_part, _ = lax.optimization_barrier((low_part, lower_got))
     low_parts = lax.all_to_all(low_part, DP, split_axis=0, concat_axis=0, tiled=True)
     got = [shifted(send, "y", NY, s + 1) for s, send in enumerate(sends)]
-    scales = tuple(1.0 / math.sqrt(act.shape[0] * NZ * NY * NC) for act in (act_mid, act_low))
-    grad_upper, grad_lower = z_sum(own_sum, got, scales, weight_upper.shape, weight_lower.shape)
-
     low_grad = pl.pallas_call(
         total_kernel,
         out_shape=jax.ShapeDtypeStruct((80, 1024), BF),
@@ -487,8 +484,10 @@
         out_specs=VMEM,
         compiler_params=PARAMS,
         name="low_total",
-    )(low_parts).T
-    return low_grad, grad_upper, grad_lower
+    )(low_parts)
+    scales = tuple(1.0 / math.sqrt(act.shape[0] * NZ * NY * NC) for act in (act_mid, act_low))
+    low_grad, grad_upper, grad_lower = z_sum(own_sum, got, low_grad, scales, weight_upper.shape, weight_lower.shape)
+    return low_grad.T, grad_upper, grad_lower
 
 
 def solution(mesh):

time: 94.3 us -> 93.1 us (0.987)
  waiting for transfers between devices: 29.1 us -> 27.2 us
    ppermute x16, starting transfers between devices: 24.1 us -> 25.7 us  [shifted(): lax.ppermute(block, axis, [(i, (i + step) % count) for i in range(count)])]
    ppermute x16, waiting for transfers between devices: 26.4 us -> 25.2 us  [shifted(): lax.ppermute(block, axis, [(i, (i + step) % count) for i in range(count)])]
  transfers between devices with their start and end apart: 19 -> 19, of which waited for: 12 -> 13; matrix products, arithmetic and copies ran while one was open for 2% -> 2% of each run, Pallas kernels for 11% -> 11%
where the time goes in v5:
time: 93.1 us; the launch traced here: 92.6 us
  starting transfers between devices  45.5 us (49%)
  waiting for transfers between devices  27.2 us (29%)
  Pallas kernels  16.1 us (17%)
  local copies, waits for them, and re-layouts  2.58 us (3%)
    ppermute x16, starting transfers between devices, shifted(): lax.ppermute(block, axis, [(i, (i + step) % count) for i in range(count)])  25.7 us
    ppermute x16, waiting for transfers between devices, shifted(): lax.ppermute(block, axis, [(i, (i + step) % count) for i in range(count)])  25.2 us
    all_to_all x1, starting transfers between devices, local(): lax.all_to_all(packed, ('zh', 'y'), split_axis=0, concat_axis=0, tiled=True)  11.6 us
    all_to_all x1, starting transfers between devices, local(): lax.all_to_all(mid_part, DP, split_axis=0, concat_axis=0, tiled=True)  4.55 us
    pallas_call x2, Pallas kernels, weight_grad(): pl.pallas_call(fetched_weight_grad_kernel if fetch else weight_grad_kerne...  4.09 us
    all_to_all x1, starting transfers between devices, local(): lax.all_to_all(low_part, DP, split_axis=0, concat_axis=0, tiled=True)  3.71 us
    pallas_call x1, Pallas kernels, local(): pl.pallas_call(upper_kernel, out_shape=(pltpu.HBM((8, 96, 512), BF), pltp...  2.67 us
    unnamed x15, local copies, waits for them, and re-layouts  2.51 us
  transfers between devices with their start and end apart: 19, of which 13 were waited for; matrix products, arithmetic and copies ran while one was open for 2% of the time, Pallas kernels for 11%

profile of v5, /device:TPU:8, one launch (start us, length us, event | category | flops | bytes accessed | tf_op | source)
XLA Modules:
  0.0 92.6 jit_solution(2525723384383712496)
XLA Ops:
  0.7 2.1 %pack.1 = (bf16[16,32,512]{2,1,0:T(8,128)(2,1)}, bf16[24,512]{1,0:T(8,128)(2,1)S(1)}) custom-call(bf16[3,8192]{1,0:T(4,128)(2,1)} %bitcast.24, bf16[5,22,96]{2,1,0:T(8,128)(2,1)} %upper_hbm.1, bf16[5,20,88]{2,1,0:T(8,128)(2,1)} %lower_hbm.1, bf16[96,512]{1,0:T(8,128)(2,1)} %bitcast.22, bf16[88,1024]{1,0:T(8,128)(2,1)} %bitcast.20), custom_call_target="tpu_custom_call" | custom-call | tf_op jit(solution)/shard_map/pack/pallas_call | solution.py:385
  2.8 11.6 %all-to-all-start = ((bf16[16,32,512]{2,1,0:T(8,128)(2,1)}), bf16[16,32,512]{2,1,0:T(8,128)(2,1)S(1)}, u32[]{:S(2)}, u32[]{:S(2)}) async-start(bf16[16,32,512]{2,1,0:T(8,128)(2,1)} %get-tuple-element.49), calls=%async_computation | async-start | bytes 1048576 | tf_op jit(solution)/shard_map/all_to_all | solution.py:410
  14.3 2.4 %collective-permute-start = (bf16[24,512]{1,0:T(8,128)(2,1)S(1)}, bf16[24,512]{1,0:T(8,128)(2,1)S(1)}, u32[]{:S(2)}, u32[]{:S(2)}) collective-permute-start(bf16[24,512]{1,0:T(8,128)(2,1)S(1)} %get-tuple-element.60), channel_id=1, source_target_pairs={{0,8},{8,16},{16,24},{24,0},{1,9},{9,17},{17,25},{25,1},{2,10},{10... | collective-permute-start | bytes 73736 | tf_op jit(solution)/shard_map/ppermute | solution.py:32
  16.7 3.6 %collective-permute-start.1 = (bf16[24,512]{1,0:T(8,128)(2,1)S(1)}, bf16[24,512]{1,0:T(8,128)(2,1)S(1)}, u32[]{:S(2)}, u32[]{:S(2)}) collective-permute-start(bf16[24,512]{1,0:T(8,128)(2,1)S(1)} %get-tuple-element.60), channel_id=1, source_target_pairs={{0,16},{8,24},{16,0},{24,8},{1,17},{9,25},{17,1},{25,9},{2,18},{10... | collective-permute-start | bytes 73736 | tf_op jit(solution)/shard_map/ppermute | solution.py:32
  20.3 3.6 %collective-permute-start.2 = (bf16[24,512]{1,0:T(8,128)(2,1)S(1)}, bf16[24,512]{1,0:T(8,128)(2,1)S(1)}, u32[]{:S(2)}, u32[]{:S(2)}) collective-permute-start(bf16[24,512]{1,0:T(8,128)(2,1)S(1)} %get-tuple-element.60), channel_id=1, source_target_pairs={{0,24},{8,0},{16,8},{24,16},{1,25},{9,1},{17,9},{25,17},{2,26},{10... | collective-permute-start | bytes 73736 | tf_op jit(solution)/shard_map/ppermute | solution.py:32
  23.9 0.1 reshape.12
  23.9 0.2 fusion.6.slope_ref
  24.1 0.1 fusion.13.slope_ref
  24.2 1.6 %copy.11 = bf16[1024,640]{0,1:T(8,128)(2,1)S(1)} copy(bf16[1024,640]{1,0:T(8,128)(2,1)} %param.10) | data formatting | bytes 2621440 | tf_op args[3]
  25.9 3.5 %collective-permute-done = bf16[24,512]{1,0:T(8,128)(2,1)S(1)} collective-permute-done((bf16[24,512]{1,0:T(8,128)(2,1)S(1)}, bf16[24,512]{1,0:T(8,128)(2,1)S(1)}, u32[]{:S(2)}, u32[]{:S(2)}) %collective-permute-start) | collective-permute-done | bytes 24608 | tf_op jit(solution)/shard_map/ppermute | solution.py:32
  29.3 3.3 %collective-permute-done.1 = bf16[24,512]{1,0:T(8,128)(2,1)S(1)} collective-permute-done((bf16[24,512]{1,0:T(8,128)(2,1)S(1)}, bf16[24,512]{1,0:T(8,128)(2,1)S(1)}, u32[]{:S(2)}, u32[]{:S(2)}) %collective-permute-start.1) | collective-permute-done | bytes 24608 | tf_op jit(solution)/shard_map/ppermute | solution.py:32
  32.7 0.1 pad_add_fusion.pos_ref
  32.8 1.8 %collective-permute-done.3.other_ref = bf16[16,32,512]{2,1,0:T(8,128)(2,1)S(1)} collective-permute-done((bf16[16,32,512]{2,1,0:T(8,128)(2,1)S(1)}, bf16[16,32,512]{2,1,0:T(8,128)(2,1)S(1)}, u32[]{:S(2)}, u32[]{:S(2)}) %collective-permute-start.3) | collective-permute-done | bytes 524320 | tf_op jit(solution)/shard_map/ppermute | solution.py:32
  34.6 2.7 %upper.1 = (bf16[8,96,512]{2,1,0:T(8,128)(2,1)}, bf16[512,512]{1,0:T(8,128)(2,1)}, f32[96,256]{1,0:T(8,128)}) custom-call(s32[3]{0:T(128)S(1)} %pad_add_fusion.pos_ref, f32[96,512]{1,0:T(8,128)S(1)} %fusion.13.slope_ref, bf16[16,32,512]{2,1,0:T(8,128)(2,1)S(1)} %all-to-all-done.own_ref, bf16[16,32,512]{2,1,0:T(8,128)(2,1)S(1)} %collective-permute-done.3.other_ref), custom_call_target="tpu_custom_call" | custom-call | tf_op jit(solution)/shard_map/upper/pallas_call | solution.py:416
  37.3 4.6 %all-to-all-start.1 = ((bf16[8,96,512]{2,1,0:T(8,128)(2,1)}), bf16[8,96,512]{2,1,0:T(8,128)(2,1)S(1)}, u32[]{:S(2)}, u32[]{:S(2)}) async-start(bf16[8,96,512]{2,1,0:T(8,128)(2,1)} %get-tuple-element.55), calls=%async_computation.1 | async-start | bytes 1572864 | tf_op jit(solution)/shard_map/all_to_all | solution.py:434
  41.9 1.4 %collective-permute-start.4 = (bf16[4,24,512]{2,1,0:T(8,128)(2,1)S(1)}, bf16[4,24,512]{2,1,0:T(8,128)(2,1)S(1)}, u32[]{:S(2)}, u32[]{:S(2)}) collective-permute-start(bf16[4,24,512]{2,1,0:T(8,128)(2,1)S(1)} %pad_maximum_fusion.refs_0_), channel_id=1, source_target_pairs={{0,2},{2,4},{4,6},{6,0},{1,3},{3,5},{5,7},{7,1},{8,10},{10,12},{12... | collective-permute-start | bytes 294920 | tf_op jit(solution)/shard_map/ppermute | solution.py:32
  43.2 2.2 %collective-permute-start.5 = (bf16[4,24,512]{2,1,0:T(8,128)(2,1)S(1)}, bf16[4,24,512]{2,1,0:T(8,128)(2,1)S(1)}, u32[]{:S(2)}, u32[]{:S(2)}) collective-permute-start(bf16[4,24,512]{2,1,0:T(8,128)(2,1)S(1)} %pad_maximum_fusion.refs_0_), channel_id=1, source_target_pairs={{0,4},{2,6},{4,0},{6,2},{1,5},{3,7},{5,1},{7,3},{8,12},{10,14},{12... | collective-permute-start | bytes 294920 | tf_op jit(solution)/shard_map/ppermute | solution.py:32
  45.5 1.0 %collective-permute-start.6 = (bf16[4,24,512]{2,1,0:T(8,128)(2,1)S(1)}, bf16[4,24,512]{2,1,0:T(8,128)(2,1)S(1)}, u32[]{:S(2)}, u32[]{:S(2)}) collective-permute-start(bf16[4,24,512]{2,1,0:T(8,128)(2,1)S(1)} %pad_maximum_fusion.refs_0_), channel_id=1, source_target_pairs={{0,6},{2,0},{4,2},{6,4},{1,7},{3,1},{5,3},{7,5},{8,14},{10,8},{12,... | collective-permute-start | bytes 294920 | tf_op jit(solution)/shard_map/ppermute | solution.py:32
  46.5 2.5 %weight_grad.2 = (f32[4,4,24,512]{3,2,1,0:T(8,128)S(1)}, bf16[4,4,24,512]{3,2,1,0:T(8,128)(2,1)S(1)}) custom-call(s32[3]{0:T(128)S(1)} %pad_add_fusion.pos_ref, bf16[704,512]{1,0:T(8,128)(2,1)} %bitcast.19, bf16[512,512]{1,0:T(8,128)(2,1)} %get-tuple-element.53.taps_hbm), custom_call_target="tpu_custom_call" | custom-call | tf_op jit(solution)/shard_map/weight_grad/pallas_call | solution.py:371
  49.0 0.9 copy-done
  49.9 0.2 collective-permute-done.5.refs_2_
  50.1 1.0 %collective-permute-done.6.refs_3_ = bf16[4,24,512]{2,1,0:T(8,128)(2,1)S(1)} collective-permute-done((bf16[4,24,512]{2,1,0:T(8,128)(2,1)S(1)}, bf16[4,24,512]{2,1,0:T(8,128)(2,1)S(1)}, u32[]{:S(2)}, u32[]{:S(2)}) %collective-permute-start.6) | collective-permute-done | bytes 98336 | tf_op jit(solution)/shard_map/ppermute | solution.py:32
  51.2 0.1 collective-permute-start.7
  51.3 0.5 collective-permute-start.15
  51.8 1.3 %collective-permute-done.7.got_upper_hbm = bf16[4,4,24,512]{3,2,1,0:T(8,128)(2,1)} collective-permute-done((bf16[4,4,24,512]{3,2,1,0:T(8,128)(2,1)S(1)}, bf16[4,4,24,512]{3,2,1,0:T(8,128)(2,1)}, u32[]{:S(2)}, u32[]{:S(2)}) %collective-permute-start.7) | collective-permute-done | bytes 393248 | tf_op jit(solution)/shard_map/ppermute | solution.py:32
  53.1 1.9 %all-to-all-done.1.mid_ref = bf16[8,96,512]{2,1,0:T(8,128)(2,1)S(1)} async-done(((bf16[8,96,512]{2,1,0:T(8,128)(2,1)}), bf16[8,96,512]{2,1,0:T(8,128)(2,1)S(1)}, u32[]{:S(2)}, u32[]{:S(2)}) %all-to-all-start.1) | async-done | bytes 786464 | tf_op jit(solution)/shard_map/all_to_all | solution.py:434
  55.0 1.0 %lower_taps.1.taps_ref = bf16[512,1024]{1,0:T(8,128)(2,1)S(1)} custom-call(s32[3]{0:T(128)S(1)} %pad_add_fusion.pos_ref, bf16[8,96,512]{2,1,0:T(8,128)(2,1)S(1)} %all-to-all-done.1.mid_ref, f32[96,1024]{1,0:T(8,128)S(1)} %fusion.6.slope_ref, f32[96,256]{1,0:T(8,128)S(1)} %copy-done.4), custom_call_target="tpu_custom_call" | custom-call | tf_op jit(solution)/shard_map/lower_taps/pallas_call | solution.py:456
  56.0 1.6 %weight_grad.3 = (f32[4,4,24,512]{3,2,1,0:T(8,128)S(1)}, bf16[4,4,24,512]{3,2,1,0:T(8,128)(2,1)S(1)}) custom-call(s32[3]{0:T(128)S(1)} %pad_add_fusion.pos_ref, bf16[640,1024]{1,0:T(8,128)(2,1)S(1)} %bitcast.17, bf16[512,1024]{1,0:T(8,128)(2,1)S(1)} %lower_taps.1.taps_ref), custom_call_target="tpu_custom_call" | custom-call | tf_op jit(solution)/shard_map/weight_grad/pallas_call | solution.py:371
  57.6 0.1 collective-permute-start.8
  57.7 1.4 %lower_weight.1.w_ref = bf16[640,512]{1,0:T(8,128)(2,1)S(1)} custom-call(s32[3]{0:T(128)S(1)} %pad_add_fusion.pos_ref, bf16[16,24,512]{2,1,0:T(8,128)(2,1)S(1)} %join.1.own_ref, bf16[16,24,512]{2,1,0:T(8,128)(2,1)} %collective-permute-done.15.other_ref), custom_call_target="tpu_custom_call" | custom-call | tf_op jit(solution)/shard_map/lower_weight/pallas_call | solution.py:445
  59.1 1.9 %low.1 = bf16[8,80,1024]{2,1,0:T(8,128)(2,1)} custom-call(bf16[512,1024]{1,0:T(8,128)(2,1)S(1)} %lower_taps.1.taps_ref, bf16[640,512]{1,0:T(8,128)(2,1)S(1)} %lower_weight.1.w_ref), custom_call_target="tpu_custom_call" | custom-call | tf_op jit(solution)/shard_map/low/pallas_call | solution.py:468
  61.0 3.7 %all-to-all-start.2 = ((bf16[8,80,1024]{2,1,0:T(8,128)(2,1)}), bf16[8,80,1024]{2,1,0:T(8,128)(2,1)S(1)}, u32[]{:S(2)}, u32[]{:S(2)}) async-start(bf16[8,80,1024]{2,1,0:T(8,128)(2,1)} %low.1), calls=%async_computation.2 | async-start | bytes 2621440 | tf_op jit(solution)/shard_map/all_to_all | solution.py:478
  64.8 1.1 %core_sum.1 = (f32[4,48,512]{2,1,0:T(8,128)S(1)}, bf16[4,48,512]{2,1,0:T(8,128)(2,1)S(1)}, bf16[4,48,512]{2,1,0:T(8,128)(2,1)S(1)}, bf16[4,48,512]{2,1,0:T(8,128)(2,1)S(1)}) custom-call(f32[4,4,24,512]{3,2,1,0:T(8,128)S(1)} %copy-done.1, bf16[4,4,24,512]{3,2,1,0:T(8,128)(2,1)} %collective-permute-done.7.got_upper_hbm, f32[4,4,24,512]{3,2,1,0:T(8,128)S(1)} %copy-done.3, ...), custom_call_target="tpu_custom_call" | custom-call | tf_op jit(solution)/shard_map/core_sum/pallas_call | solution.py:112
  65.8 1.6 %collective-permute-start.9 = (bf16[4,48,512]{2,1,0:T(8,128)(2,1)S(1)}, bf16[4,48,512]{2,1,0:T(8,128)(2,1)S(1)}, u32[]{:S(2)}, u32[]{:S(2)}) collective-permute-start(bf16[4,48,512]{2,1,0:T(8,128)(2,1)S(1)} %get-tuple-element.79), channel_id=1, source_target_pairs={{0,2},{2,4},{4,6},{6,0},{1,3},{3,5},{5,7},{7,1},{8,10},{10,12},{12... | collective-permute-start | bytes 589832 | tf_op jit(solution)/shard_map/ppermute | solution.py:32
  67.4 2.2 %collective-permute-start.10 = (bf16[4,48,512]{2,1,0:T(8,128)(2,1)S(1)}, bf16[4,48,512]{2,1,0:T(8,128)(2,1)S(1)}, u32[]{:S(2)}, u32[]{:S(2)}) collective-permute-start(bf16[4,48,512]{2,1,0:T(8,128)(2,1)S(1)} %get-tuple-element.80), channel_id=1, source_target_pairs={{0,4},{2,6},{4,0},{6,2},{1,5},{3,7},{5,1},{7,3},{8,12},{10,14},{12... | collective-permute-start | bytes 589832 | tf_op jit(solution)/shard_map/ppermute | solution.py:32
  69.6 1.2 %collective-permute-start.11 = (bf16[4,48,512]{2,1,0:T(8,128)(2,1)S(1)}, bf16[4,48,512]{2,1,0:T(8,128)(2,1)S(1)}, u32[]{:S(2)}, u32[]{:S(2)}) collective-permute-start(bf16[4,48,512]{2,1,0:T(8,128)(2,1)S(1)} %get-tuple-element.81), channel_id=1, source_target_pairs={{0,6},{2,0},{4,2},{6,4},{1,7},{3,1},{5,3},{7,5},{8,14},{10,8},{12,... | collective-permute-start | bytes 589832 | tf_op jit(solution)/shard_map/ppermute | solution.py:32
  70.9 3.0 %collective-permute-done.9.refs_0_ = bf16[4,48,512]{2,1,0:T(8,128)(2,1)S(1)} collective-permute-done((bf16[4,48,512]{2,1,0:T(8,128)(2,1)S(1)}, bf16[4,48,512]{2,1,0:T(8,128)(2,1)S(1)}, u32[]{:S(2)}, u32[]{:S(2)}) %collective-permute-start.9) | collective-permute-done | bytes 196640 | tf_op jit(solution)/shard_map/ppermute | solution.py:32
  73.8 2.9 %collective-permute-done.10.refs_1_ = bf16[4,48,512]{2,1,0:T(8,128)(2,1)S(1)} collective-permute-done((bf16[4,48,512]{2,1,0:T(8,128)(2,1)S(1)}, bf16[4,48,512]{2,1,0:T(8,128)(2,1)S(1)}, u32[]{:S(2)}, u32[]{:S(2)}) %collective-permute-start.10) | collective-permute-done | bytes 196640 | tf_op jit(solution)/shard_map/ppermute | solution.py:32
  76.7 3.2 %collective-permute-done.11.refs_2_ = bf16[4,48,512]{2,1,0:T(8,128)(2,1)S(1)} collective-permute-done((bf16[4,48,512]{2,1,0:T(8,128)(2,1)S(1)}, bf16[4,48,512]{2,1,0:T(8,128)(2,1)S(1)}, u32[]{:S(2)}, u32[]{:S(2)}) %collective-permute-start.11) | collective-permute-done | bytes 196640 | tf_op jit(solution)/shard_map/ppermute | solution.py:32
  80.0 0.1 y_sum.1
  80.1 1.3 %collective-permute-start.12 = (bf16[48,512]{1,0:T(8,128)(2,1)S(1)}, bf16[48,512]{1,0:T(8,128)(2,1)S(1)}, u32[]{:S(2)}, u32[]{:S(2)}) collective-permute-start(bf16[48,512]{1,0:T(8,128)(2,1)S(1)} %get-tuple-element.82), channel_id=1, source_target_pairs={{0,8},{8,16},{16,24},{24,0},{1,9},{9,17},{17,25},{25,1},{2,10},{10... | collective-permute-start | bytes 147464 | tf_op jit(solution)/shard_map/ppermute | solution.py:32
  81.3 2.8 %collective-permute-start.13 = (bf16[48,512]{1,0:T(8,128)(2,1)S(1)}, bf16[48,512]{1,0:T(8,128)(2,1)S(1)}, u32[]{:S(2)}, u32[]{:S(2)}) collective-permute-start(bf16[48,512]{1,0:T(8,128)(2,1)S(1)} %get-tuple-element.83), channel_id=1, source_target_pairs={{0,16},{8,24},{16,0},{24,8},{1,17},{9,25},{17,1},{25,9},{2,18},{10... | collective-permute-start | bytes 147464 | tf_op jit(solution)/shard_map/ppermute | solution.py:32
  84.1 1.8 %collective-permute-start.14 = (bf16[48,512]{1,0:T(8,128)(2,1)S(1)}, bf16[48,512]{1,0:T(8,128)(2,1)S(1)}, u32[]{:S(2)}, u32[]{:S(2)}) collective-permute-start(bf16[48,512]{1,0:T(8,128)(2,1)S(1)} %get-tuple-element.84), channel_id=1, source_target_pairs={{0,24},{8,0},{16,8},{24,16},{1,25},{9,1},{17,9},{25,17},{2,26},{10... | collective-permute-start | bytes 147464 | tf_op jit(solution)/shard_map/ppermute | solution.py:32
  85.9 0.8 low_total.1
  86.8 0.4 collective-permute-done.12.refs_0_
  87.2 2.1 %collective-permute-done.13.refs_1_ = bf16[48,512]{1,0:T(8,128)(2,1)S(1)} collective-permute-done((bf16[48,512]{1,0:T(8,128)(2,1)S(1)}, bf16[48,512]{1,0:T(8,128)(2,1)S(1)}, u32[]{:S(2)}, u32[]{:S(2)}) %collective-permute-start.13) | collective-permute-done | bytes 49184 | tf_op jit(solution)/shard_map/ppermute | solution.py:32
  89.3 2.4 %collective-permute-done.14.refs_2_ = bf16[48,512]{1,0:T(8,128)(2,1)S(1)} collective-permute-done((bf16[48,512]{1,0:T(8,128)(2,1)S(1)}, bf16[48,512]{1,0:T(8,128)(2,1)S(1)}, u32[]{:S(2)}, u32[]{:S(2)}) %collective-permute-start.14) | collective-permute-done | bytes 49184 | tf_op jit(solution)/shard_map/ppermute | solution.py:32
  91.7 0.9 %z_sum.1 = (f32[5,22,96]{2,1,0:T(8,128)}, f32[5,20,88]{2,1,0:T(8,128)}) custom-call(f32[48,512]{1,0:T(8,128)S(1)} %get-tuple-element.89.own_ref, bf16[48,512]{1,0:T(8,128)(2,1)S(1)} %collective-permute-done.12.refs_0_, bf16[48,512]{1,0:T(8,128)(2,1)S(1)} %collective-permute-done.13.refs_1_, bf16[48,512]{1,0:T(8,128)(2,1)S(1)} %collective-permute-done.14.refs_2_), custom_call_target="tpu_custom_call" | custom-call | tf_op jit(solution)/shard_map/z_sum/pallas_call | solution.py:98
  (23 shorter events, 0.1 us)
Async XLA Ops:
  0.6 23.2 %copy-start.5 = (bf16[1024,88]{0,1:T(8,128)(2,1)S(1)}, bf16[1024,88]{0,1:T(8,128)(2,1)}, u32[]{:S(2)}) copy-start(bf16[1024,88]{0,1:T(8,128)(2,1)} %param.11) | copy-start | bytes 540676
  0.6 23.5 %copy-start.6 = (bf16[512,96]{0,1:T(8,128)(2,1)S(1)}, bf16[512,96]{0,1:T(8,128)(2,1)}, u32[]{:S(2)}) copy-start(bf16[512,96]{0,1:T(8,128)(2,1)} %param.9) | copy-start | bytes 294916
  2.8 29.9 %all-to-all-start = ((bf16[16,32,512]{2,1,0:T(8,128)(2,1)}), bf16[16,32,512]{2,1,0:T(8,128)(2,1)S(1)}, u32[]{:S(2)}, u32[]{:S(2)}) async-start(bf16[16,32,512]{2,1,0:T(8,128)(2,1)} %get-tuple-element.49), calls=%async_computation | async-start | bytes 1048576 | tf_op jit(solution)/shard_map/all_to_all | solution.py:410
  14.3 15.0 %collective-permute-start = (bf16[24,512]{1,0:T(8,128)(2,1)S(1)}, bf16[24,512]{1,0:T(8,128)(2,1)S(1)}, u32[]{:S(2)}, u32[]{:S(2)}) collective-permute-start(bf16[24,512]{1,0:T(8,128)(2,1)S(1)} %get-tuple-element.60), channel_id=1, source_target_pairs={{0,8},{8,16},{16,24},{24,0},{1,9},{9,17},{17,25},{25,1},{2,10},{10... | collective-permute-start | bytes 73736 | tf_op jit(solution)/shard_map/ppermute | solution.py:32
  16.7 16.0 %collective-permute-start.1 = (bf16[24,512]{1,0:T(8,128)(2,1)S(1)}, bf16[24,512]{1,0:T(8,128)(2,1)S(1)}, u32[]{:S(2)}, u32[]{:S(2)}) collective-permute-start(bf16[24,512]{1,0:T(8,128)(2,1)S(1)} %get-tuple-element.60), channel_id=1, source_target_pairs={{0,16},{8,24},{16,0},{24,8},{1,17},{9,25},{17,1},{25,9},{2,18},{10... | collective-permute-start | bytes 73736 | tf_op jit(solution)/shard_map/ppermute | solution.py:32
  20.3 12.4 %collective-permute-start.2 = (bf16[24,512]{1,0:T(8,128)(2,1)S(1)}, bf16[24,512]{1,0:T(8,128)(2,1)S(1)}, u32[]{:S(2)}, u32[]{:S(2)}) collective-permute-start(bf16[24,512]{1,0:T(8,128)(2,1)S(1)} %get-tuple-element.60), channel_id=1, source_target_pairs={{0,24},{8,0},{16,8},{24,16},{1,25},{9,1},{17,9},{25,17},{2,26},{10... | collective-permute-start | bytes 73736 | tf_op jit(solution)/shard_map/ppermute | solution.py:32
  32.7 1.9 %collective-permute-start.3 = (bf16[16,32,512]{2,1,0:T(8,128)(2,1)S(1)}, bf16[16,32,512]{2,1,0:T(8,128)(2,1)S(1)}, u32[]{:S(2)}, u32[]{:S(2)}) collective-permute-start(bf16[16,32,512]{2,1,0:T(8,128)(2,1)S(1)} %all-to-all-done.own_ref), channel_id=1, source_target_pairs={{0,1},{1,0},{2,3},{3,2},{4,5},{5,4},{6,7},{7,6},{8,9},{9,8},{10,11... | collective-permute-start | bytes 1572872 | tf_op jit(solution)/shard_map/ppermute | solution.py:32
  37.3 17.7 %all-to-all-start.1 = ((bf16[8,96,512]{2,1,0:T(8,128)(2,1)}), bf16[8,96,512]{2,1,0:T(8,128)(2,1)S(1)}, u32[]{:S(2)}, u32[]{:S(2)}) async-start(bf16[8,96,512]{2,1,0:T(8,128)(2,1)} %get-tuple-element.55), calls=%async_computation.1 | async-start | bytes 1572864 | tf_op jit(solution)/shard_map/all_to_all | solution.py:434
  41.8 13.2 %copy-start.4 = (f32[96,256]{1,0:T(8,128)S(1)}, f32[96,256]{1,0:T(8,128)}, u32[]{:S(2)}) copy-start(f32[96,256]{1,0:T(8,128)} %get-tuple-element.75.edge_ref) | copy-start | bytes 294916
  41.9 8.1 %collective-permute-start.4 = (bf16[4,24,512]{2,1,0:T(8,128)(2,1)S(1)}, bf16[4,24,512]{2,1,0:T(8,128)(2,1)S(1)}, u32[]{:S(2)}, u32[]{:S(2)}) collective-permute-start(bf16[4,24,512]{2,1,0:T(8,128)(2,1)S(1)} %pad_maximum_fusion.refs_0_), channel_id=1, source_target_pairs={{0,2},{2,4},{4,6},{6,0},{1,3},{3,5},{5,7},{7,1},{8,10},{10,12},{12... | collective-permute-start | bytes 294920 | tf_op jit(solution)/shard_map/ppermute | solution.py:32
  43.2 6.9 %collective-permute-start.5 = (bf16[4,24,512]{2,1,0:T(8,128)(2,1)S(1)}, bf16[4,24,512]{2,1,0:T(8,128)(2,1)S(1)}, u32[]{:S(2)}, u32[]{:S(2)}) collective-permute-start(bf16[4,24,512]{2,1,0:T(8,128)(2,1)S(1)} %pad_maximum_fusion.refs_0_), channel_id=1, source_target_pairs={{0,4},{2,6},{4,0},{6,2},{1,5},{3,7},{5,1},{7,3},{8,12},{10,14},{12... | collective-permute-start | bytes 294920 | tf_op jit(solution)/shard_map/ppermute | solution.py:32
  45.5 5.7 %collective-permute-start.6 = (bf16[4,24,512]{2,1,0:T(8,128)(2,1)S(1)}, bf16[4,24,512]{2,1,0:T(8,128)(2,1)S(1)}, u32[]{:S(2)}, u32[]{:S(2)}) collective-permute-start(bf16[4,24,512]{2,1,0:T(8,128)(2,1)S(1)} %pad_maximum_fusion.refs_0_), channel_id=1, source_target_pairs={{0,6},{2,0},{4,2},{6,4},{1,7},{3,1},{5,3},{7,5},{8,14},{10,8},{12,... | collective-permute-start | bytes 294920 | tf_op jit(solution)/shard_map/ppermute | solution.py:32
  49.0 0.9 copy-start
  51.2 1.9 %collective-permute-start.7 = (bf16[4,4,24,512]{3,2,1,0:T(8,128)(2,1)S(1)}, bf16[4,4,24,512]{3,2,1,0:T(8,128)(2,1)}, u32[]{:S(2)}, u32[]{:S(2)}) collective-permute-start(bf16[4,4,24,512]{3,2,1,0:T(8,128)(2,1)S(1)} %get-tuple-element.70), channel_id=1, source_target_pairs={{0,1},{1,0},{2,3},{3,2},{4,5},{5,4},{6,7},{7,6},{8,9},{9,8},{10,11... | collective-permute-start | bytes 1179656 | tf_op jit(solution)/shard_map/ppermute | solution.py:32
  51.3 6.4 %collective-permute-start.15 = (bf16[16,24,512]{2,1,0:T(8,128)(2,1)S(1)}, bf16[16,24,512]{2,1,0:T(8,128)(2,1)}, u32[]{:S(2)}, u32[]{:S(2)}) collective-permute-start(bf16[16,24,512]{2,1,0:T(8,128)(2,1)S(1)} %join.1.own_ref), channel_id=1, source_target_pairs={{0,1},{1,0},{2,3},{3,2},{4,5},{5,4},{6,7},{7,6},{8,9},{9,8},{10,11... | collective-permute-start | bytes 1179656 | tf_op jit(solution)/shard_map/ppermute | solution.py:32
  57.6 1.5 %copy-start.2 = (f32[4,4,24,512]{3,2,1,0:T(8,128)}, f32[4,4,24,512]{3,2,1,0:T(8,128)S(1)}, u32[]{:S(2)}) copy-start(f32[4,4,24,512]{3,2,1,0:T(8,128)S(1)} %get-tuple-element.76.keep_lower_ref) | copy-start | bytes 2359300
  57.6 3.4 %collective-permute-start.8 = (bf16[4,4,24,512]{3,2,1,0:T(8,128)(2,1)S(1)}, bf16[4,4,24,512]{3,2,1,0:T(8,128)(2,1)S(1)}, u32[]{:S(2)}, u32[]{:S(2)}) collective-permute-start(bf16[4,4,24,512]{3,2,1,0:T(8,128)(2,1)S(1)} %get-tuple-element.77), channel_id=1, source_target_pairs={{0,1},{1,0},{2,3},{3,2},{4,5},{5,4},{6,7},{7,6},{8,9},{9,8},{10,11... | collective-permute-start | bytes 1179656 | tf_op jit(solution)/shard_map/ppermute | solution.py:32
  61.0 3.8 %copy-start.1 = (f32[4,4,24,512]{3,2,1,0:T(8,128)S(1)}, f32[4,4,24,512]{3,2,1,0:T(8,128)}, u32[]{:S(2)}) copy-start(f32[4,4,24,512]{3,2,1,0:T(8,128)} %copy-done) | copy-start | bytes 2359300
  61.0 3.8 %copy-start.3 = (f32[4,4,24,512]{3,2,1,0:T(8,128)S(1)}, f32[4,4,24,512]{3,2,1,0:T(8,128)}, u32[]{:S(2)}) copy-start(f32[4,4,24,512]{3,2,1,0:T(8,128)} %copy-done.2) | copy-start | bytes 2359300
  61.0 24.9 %all-to-all-start.2 = ((bf16[8,80,1024]{2,1,0:T(8,128)(2,1)}), bf16[8,80,1024]{2,1,0:T(8,128)(2,1)S(1)}, u32[]{:S(2)}, u32[]{:S(2)}) async-start(bf16[8,80,1024]{2,1,0:T(8,128)(2,1)} %low.1), calls=%async_computation.2 | async-start | bytes 2621440 | tf_op jit(solution)/shard_map/all_to_all | solution.py:478
  65.8 8.0 %collective-permute-start.9 = (bf16[4,48,512]{2,1,0:T(8,128)(2,1)S(1)}, bf16[4,48,512]{2,1,0:T(8,128)(2,1)S(1)}, u32[]{:S(2)}, u32[]{:S(2)}) collective-permute-start(bf16[4,48,512]{2,1,0:T(8,128)(2,1)S(1)} %get-tuple-element.79), channel_id=1, source_target_pairs={{0,2},{2,4},{4,6},{6,0},{1,3},{3,5},{5,7},{7,1},{8,10},{10,12},{12... | collective-permute-start | bytes 589832 | tf_op jit(solution)/shard_map/ppermute | solution.py:32
  67.4 9.3 %collective-permute-start.10 = (bf16[4,48,512]{2,1,0:T(8,128)(2,1)S(1)}, bf16[4,48,512]{2,1,0:T(8,128)(2,1)S(1)}, u32[]{:S(2)}, u32[]{:S(2)}) collective-permute-start(bf16[4,48,512]{2,1,0:T(8,128)(2,1)S(1)} %get-tuple-element.80), channel_id=1, source_target_pairs={{0,4},{2,6},{4,0},{6,2},{1,5},{3,7},{5,1},{7,3},{8,12},{10,14},{12... | collective-permute-start | bytes 589832 | tf_op jit(solution)/shard_map/ppermute | solution.py:32
  69.6 10.3 %collective-permute-start.11 = (bf16[4,48,512]{2,1,0:T(8,128)(2,1)S(1)}, bf16[4,48,512]{2,1,0:T(8,128)(2,1)S(1)}, u32[]{:S(2)}, u32[]{:S(2)}) collective-permute-start(bf16[4,48,512]{2,1,0:T(8,128)(2,1)S(1)} %get-tuple-element.81), channel_id=1, source_target_pairs={{0,6},{2,0},{4,2},{6,4},{1,7},{3,1},{5,3},{7,5},{8,14},{10,8},{12,... | collective-permute-start | bytes 589832 | tf_op jit(solution)/shard_map/ppermute | solution.py:32
  80.1 7.1 %collective-permute-start.12 = (bf16[48,512]{1,0:T(8,128)(2,1)S(1)}, bf16[48,512]{1,0:T(8,128)(2,1)S(1)}, u32[]{:S(2)}, u32[]{:S(2)}) collective-permute-start(bf16[48,512]{1,0:T(8,128)(2,1)S(1)} %get-tuple-element.82), channel_id=1, source_target_pairs={{0,8},{8,16},{16,24},{24,0},{1,9},{9,17},{17,25},{25,1},{2,10},{10... | collective-permute-start | bytes 147464 | tf_op jit(solution)/shard_map/ppermute | solution.py:32
  81.3 8.0 %collective-permute-start.13 = (bf16[48,512]{1,0:T(8,128)(2,1)S(1)}, bf16[48,512]{1,0:T(8,128)(2,1)S(1)}, u32[]{:S(2)}, u32[]{:S(2)}) collective-permute-start(bf16[48,512]{1,0:T(8,128)(2,1)S(1)} %get-tuple-element.83), channel_id=1, source_target_pairs={{0,16},{8,24},{16,0},{24,8},{1,17},{9,25},{17,1},{25,9},{2,18},{10... | collective-permute-start | bytes 147464 | tf_op jit(solution)/shard_map/ppermute | solution.py:32
  84.1 7.5 %collective-permute-start.14 = (bf16[48,512]{1,0:T(8,128)(2,1)S(1)}, bf16[48,512]{1,0:T(8,128)(2,1)S(1)}, u32[]{:S(2)}, u32[]{:S(2)}) collective-permute-start(bf16[48,512]{1,0:T(8,128)(2,1)S(1)} %get-tuple-element.84), channel_id=1, source_target_pairs={{0,24},{8,0},{16,8},{24,16},{1,25},{9,1},{17,9},{25,17},{2,26},{10... | collective-permute-start | bytes 147464 | tf_op jit(solution)/shard_map/ppermute | solution.py:32

commit v6 on v5

--- a/solution.py
+++ b/solution.py
@@ -290,7 +290,7 @@
     out_ref[...] = rows_ref[0:640, :].astype(BF)
 
 
-def lower_taps_kernel(pos_ref, mid_ref, slope_ref, edge_ref, taps_ref):
+def lower_taps_kernel(pos_ref, mid_ref, slope_copy, slope_ref, edge_ref, taps_ref):
     place = pos_ref[0] * (NY * NC) + pos_ref[1] * NC + pos_ref[2]
     total = mid_ref[0].astype(F32)
     for d in range(1, 8):
@@ -302,6 +302,7 @@
     edge = half_slope(edge_ref[...])
     spread = doubling()
     grad = jnp.concatenate([mm(mid[:, 128 * j : 128 * j + 128], spread) for j in range(4)], axis=1)
+    slope_copy.wait()
     grad = jnp.concatenate(
         [left * edge[:, 0:128], grad * slope_ref[...], right * edge[:, 128:256]], axis=1
     )
@@ -360,6 +361,21 @@
             base = (zh * NY + y) * NC
             keep_ref[ry, rz] = block_ref[base + pos_ref[2]]
             send_ref[ry, rz] = block_ref[base + 1 - pos_ref[2]].astype(BF)
+
+
+def lower_kernel(
+    pos_ref, mid_ref, slope_hbm, edge_ref, act_hbm, taps_ref, keep_ref, send_ref,
+    rows_ref, block_ref, slope_ref, act_ref, sem,
+):
+    copies = [
+        pltpu.make_async_copy(slope_hbm, slope_ref, sem.at[0]),
+        pltpu.make_async_copy(act_hbm, act_ref, sem.at[1]),
+    ]
+    for copy in copies:
+        copy.start()
+    lower_taps_kernel(pos_ref, mid_ref, copies[0], slope_ref, edge_ref, taps_ref)
+    copies[1].wait()
+    weight_grad_kernel(pos_ref, act_ref, taps_ref, keep_ref, send_ref, rows_ref, block_ref)
 
 
 def weight_grad(pos, act, taps, fetch):
@@ -453,15 +469,27 @@
     )(pos, lower_own, lower_other)
 
     mid_parts, upper_got = lax.optimization_barrier((mid_parts, upper_got))
-    lower_taps = pl.pallas_call(
-        lower_taps_kernel,
-        out_shape=jax.ShapeDtypeStruct((512, 1024), BF),
-        in_specs=[SMEM] + [VMEM] * 3,
-        out_specs=VMEM,
-        compiler_params=PARAMS,
-        name="lower_taps",
-    )(pos, mid_parts, slope_lower, edges)
-    lower_keep, lower_send = weight_grad(pos, act_low_rows, lower_taps, False)
+    block = (NY, NZ, 24, 512)
+    fetched = [pltpu.with_memory_space_constraint(v, pltpu.HBM) for v in (slope_lower, act_low_rows)]
+    lower_taps, lower_keep, lower_send = pl.pallas_call(
+        lower_kernel,
+        out_shape=(
+            jax.ShapeDtypeStruct((512, 1024), BF),
+            jax.ShapeDtypeStruct(block, F32),
+            jax.ShapeDtypeStruct(block, BF),
+        ),
+        in_specs=[SMEM, VMEM, HBM, VMEM, HBM],
+        out_specs=(VMEM, VMEM, VMEM),
+        scratch_shapes=[
+            pltpu.VMEM((act_low_rows.shape[0] + 8, 512), F32),
+            pltpu.VMEM((32, 24, 512), F32),
+            pltpu.VMEM(slope_lower.shape, F32),
+            pltpu.VMEM(act_low_rows.shape, BF),
+            pltpu.SemaphoreType.DMA((2,)),
+        ],
+        compiler_params=PARAMS,
+        name="lower",
+    )(pos, mid_parts, fetched[0], edges, fetched[1])
     lower_got = shifted(lower_send, "c", NC, 1)
     own_sum, *sends = core_sum((upper_keep, upper_got), (lower_keep, lower_got))
     lower_taps, _ = lax.optimization_barrier((lower_taps, lower_keep))

time: 93.1 us -> 93.7 us (level)
    pallas_call x1, Pallas kernels: 1 us -> 3.03 us  [local(): pl.pallas_call(lower_kernel, out_shape=(jax.ShapeDtypeStruct((512, 1024),...]
    pallas_call x2 -> x1, Pallas kernels: 4.09 us -> 2.53 us  [weight_grad(): pl.pallas_call(fetched_weight_grad_kernel if fetch else weight_grad_kerne...]
    unnamed x15 -> x9, local copies, waits for them, and re-layouts: 2.51 us -> 1.58 us
  transfers between devices with their start and end apart: 19 -> 19, of which waited for: 13 -> 13; matrix products, arithmetic and copies ran while one was open for 2% -> 3% of each run, Pallas kernels for 11% -> 11%
where the time goes in v6:
time: 93.7 us; the launch traced here: 93.2 us
  starting transfers between devices  45.7 us (49%)
  waiting for transfers between devices  27.4 us (29%)
  Pallas kernels  16.5 us (18%)
  local copies, waits for them, and re-layouts  1.65 us (2%)
  other arithmetic  1.12 us (1%)
    ppermute x16, starting transfers between devices, shifted(): lax.ppermute(block, axis, [(i, (i + step) % count) for i in range(count)])  25.8 us
    ppermute x16, waiting for transfers between devices, shifted(): lax.ppermute(block, axis, [(i, (i + step) % count) for i in range(count)])  25.5 us
    all_to_all x1, starting transfers between devices, local(): lax.all_to_all(packed, ('zh', 'y'), split_axis=0, concat_axis=0, tiled=True)  11.7 us
    all_to_all x1, starting transfers between devices, local(): lax.all_to_all(mid_part, DP, split_axis=0, concat_axis=0, tiled=True)  4.55 us
    all_to_all x1, starting transfers between devices, local(): lax.all_to_all(low_part, DP, split_axis=0, concat_axis=0, tiled=True)  3.65 us
    pallas_call x1, Pallas kernels, local(): pl.pallas_call(lower_kernel, out_shape=(jax.ShapeDtypeStruct((512, 1024),...  3.03 us
    pallas_call x1, Pallas kernels, local(): pl.pallas_call(upper_kernel, out_shape=(pltpu.HBM((8, 96, 512), BF), pltp...  2.7 us
    pallas_call x1, Pallas kernels, weight_grad(): pl.pallas_call(fetched_weight_grad_kernel if fetch else weight_grad_kerne...  2.53 us
  transfers between devices with their start and end apart: 19, of which 13 were waited for; matrix products, arithmetic and copies ran while one was open for 3% of the time, Pallas kernels for 11%

profile of v6, /device:TPU:8, one launch (start us, length us, event | category | flops | bytes accessed | tf_op | source)
XLA Modules:
  0.0 93.2 jit_solution(16125224181470290411)
XLA Ops:
  0.7 2.2 %pack.1 = (bf16[16,32,512]{2,1,0:T(8,128)(2,1)}, bf16[24,512]{1,0:T(8,128)(2,1)S(1)}) custom-call(bf16[3,8192]{1,0:T(4,128)(2,1)} %bitcast.24, bf16[5,22,96]{2,1,0:T(8,128)(2,1)} %upper_hbm.1, bf16[5,20,88]{2,1,0:T(8,128)(2,1)} %lower_hbm.1, bf16[96,512]{1,0:T(8,128)(2,1)} %bitcast.22, bf16[88,1024]{1,0:T(8,128)(2,1)} %bitcast.20), custom_call_target="tpu_custom_call" | custom-call | tf_op jit(solution)/shard_map/pack/pallas_call | solution.py:401
  2.8 0.0 copy-start.1
  2.8 11.7 %all-to-all-start = ((bf16[16,32,512]{2,1,0:T(8,128)(2,1)}), bf16[16,32,512]{2,1,0:T(8,128)(2,1)S(1)}, u32[]{:S(2)}, u32[]{:S(2)}) async-start(bf16[16,32,512]{2,1,0:T(8,128)(2,1)} %get-tuple-element.50), calls=%async_computation | async-start | bytes 1048576 | tf_op jit(solution)/shard_map/all_to_all | solution.py:426
  14.5 2.4 %collective-permute-start = (bf16[24,512]{1,0:T(8,128)(2,1)S(1)}, bf16[24,512]{1,0:T(8,128)(2,1)S(1)}, u32[]{:S(2)}, u32[]{:S(2)}) collective-permute-start(bf16[24,512]{1,0:T(8,128)(2,1)S(1)} %get-tuple-element.61), channel_id=1, source_target_pairs={{0,8},{8,16},{16,24},{24,0},{1,9},{9,17},{17,25},{25,1},{2,10},{10... | collective-permute-start | bytes 73736 | tf_op jit(solution)/shard_map/ppermute | solution.py:32
  16.9 3.6 %collective-permute-start.1 = (bf16[24,512]{1,0:T(8,128)(2,1)S(1)}, bf16[24,512]{1,0:T(8,128)(2,1)S(1)}, u32[]{:S(2)}, u32[]{:S(2)}) collective-permute-start(bf16[24,512]{1,0:T(8,128)(2,1)S(1)} %get-tuple-element.61), channel_id=1, source_target_pairs={{0,16},{8,24},{16,0},{24,8},{1,17},{9,25},{17,1},{25,9},{2,18},{10... | collective-permute-start | bytes 73736 | tf_op jit(solution)/shard_map/ppermute | solution.py:32
  20.5 3.6 %collective-permute-start.2 = (bf16[24,512]{1,0:T(8,128)(2,1)S(1)}, bf16[24,512]{1,0:T(8,128)(2,1)S(1)}, u32[]{:S(2)}, u32[]{:S(2)}) collective-permute-start(bf16[24,512]{1,0:T(8,128)(2,1)S(1)} %get-tuple-element.61), channel_id=1, source_target_pairs={{0,24},{8,0},{16,8},{24,16},{1,25},{9,1},{17,9},{25,17},{2,26},{10... | collective-permute-start | bytes 73736 | tf_op jit(solution)/shard_map/ppermute | solution.py:32
  24.0 0.1 reshape.12
  24.1 0.9 %fusion.6.slope_hbm = f32[96,1024]{1,0:T(8,128)} fusion(bf16[4,24,1024]{2,1,0:T(8,128)(2,1)S(1)} %pad.4), kind=kLoop, calls=%fused_computation.10 | loop fusion | flops 983040 | bytes 589824 | tf_op jit(solution)/shard_map/mul | solution.py:28
  25.1 0.1 fusion.13.slope_ref
  25.2 1.6 %copy.11 = bf16[1024,640]{0,1:T(8,128)(2,1)} copy(bf16[1024,640]{1,0:T(8,128)(2,1)S(1)} %copy-done.1) | data formatting | bytes 2621440 | tf_op args[3]
  26.7 2.8 %collective-permute-done = bf16[24,512]{1,0:T(8,128)(2,1)S(1)} collective-permute-done((bf16[24,512]{1,0:T(8,128)(2,1)S(1)}, bf16[24,512]{1,0:T(8,128)(2,1)S(1)}, u32[]{:S(2)}, u32[]{:S(2)}) %collective-permute-start) | collective-permute-done | bytes 24608 | tf_op jit(solution)/shard_map/ppermute | solution.py:32
  29.5 3.3 %collective-permute-done.1 = bf16[24,512]{1,0:T(8,128)(2,1)S(1)} collective-permute-done((bf16[24,512]{1,0:T(8,128)(2,1)S(1)}, bf16[24,512]{1,0:T(8,128)(2,1)S(1)}, u32[]{:S(2)}, u32[]{:S(2)}) %collective-permute-start.1) | collective-permute-done | bytes 24608 | tf_op jit(solution)/shard_map/ppermute | solution.py:32
  32.9 0.0 collective-permute-start.3
  32.9 0.1 pad_add_fusion.pos_ref
  33.0 1.8 %collective-permute-done.3.other_ref = bf16[16,32,512]{2,1,0:T(8,128)(2,1)S(1)} collective-permute-done((bf16[16,32,512]{2,1,0:T(8,128)(2,1)S(1)}, bf16[16,32,512]{2,1,0:T(8,128)(2,1)S(1)}, u32[]{:S(2)}, u32[]{:S(2)}) %collective-permute-start.3) | collective-permute-done | bytes 524320 | tf_op jit(solution)/shard_map/ppermute | solution.py:32
  34.8 2.7 %upper.1 = (bf16[8,96,512]{2,1,0:T(8,128)(2,1)}, bf16[512,512]{1,0:T(8,128)(2,1)}, f32[96,256]{1,0:T(8,128)}) custom-call(s32[3]{0:T(128)S(1)} %pad_add_fusion.pos_ref, f32[96,512]{1,0:T(8,128)S(1)} %fusion.13.slope_ref, bf16[16,32,512]{2,1,0:T(8,128)(2,1)S(1)} %all-to-all-done.own_ref, bf16[16,32,512]{2,1,0:T(8,128)(2,1)S(1)} %collective-permute-done.3.other_ref), custom_call_target="tpu_custom_call" | custom-call | tf_op jit(solution)/shard_map/upper/pallas_call | solution.py:432
  37.5 4.6 %all-to-all-start.1 = ((bf16[8,96,512]{2,1,0:T(8,128)(2,1)}), bf16[8,96,512]{2,1,0:T(8,128)(2,1)S(1)}, u32[]{:S(2)}, u32[]{:S(2)}) async-start(bf16[8,96,512]{2,1,0:T(8,128)(2,1)} %get-tuple-element.56), calls=%async_computation.1 | async-start | bytes 1572864 | tf_op jit(solution)/shard_map/all_to_all | solution.py:450
  42.1 1.4 %collective-permute-start.4 = (bf16[4,24,512]{2,1,0:T(8,128)(2,1)S(1)}, bf16[4,24,512]{2,1,0:T(8,128)(2,1)S(1)}, u32[]{:S(2)}, u32[]{:S(2)}) collective-permute-start(bf16[4,24,512]{2,1,0:T(8,128)(2,1)S(1)} %pad_maximum_fusion.refs_0_), channel_id=1, source_target_pairs={{0,2},{2,4},{4,6},{6,0},{1,3},{3,5},{5,7},{7,1},{8,10},{10,12},{12... | collective-permute-start | bytes 294920 | tf_op jit(solution)/shard_map/ppermute | solution.py:32
  43.5 2.2 %collective-permute-start.5 = (bf16[4,24,512]{2,1,0:T(8,128)(2,1)S(1)}, bf16[4,24,512]{2,1,0:T(8,128)(2,1)S(1)}, u32[]{:S(2)}, u32[]{:S(2)}) collective-permute-start(bf16[4,24,512]{2,1,0:T(8,128)(2,1)S(1)} %pad_maximum_fusion.refs_0_), channel_id=1, source_target_pairs={{0,4},{2,6},{4,0},{6,2},{1,5},{3,7},{5,1},{7,3},{8,12},{10,14},{12... | collective-permute-start | bytes 294920 | tf_op jit(solution)/shard_map/ppermute | solution.py:32
  45.7 1.0 %collective-permute-start.6 = (bf16[4,24,512]{2,1,0:T(8,128)(2,1)S(1)}, bf16[4,24,512]{2,1,0:T(8,128)(2,1)S(1)}, u32[]{:S(2)}, u32[]{:S(2)}) collective-permute-start(bf16[4,24,512]{2,1,0:T(8,128)(2,1)S(1)} %pad_maximum_fusion.refs_0_), channel_id=1, source_target_pairs={{0,6},{2,0},{4,2},{6,4},{1,7},{3,1},{5,3},{7,5},{8,14},{10,8},{12,... | collective-permute-start | bytes 294920 | tf_op jit(solution)/shard_map/ppermute | solution.py:32
  46.7 2.5 %weight_grad.1 = (f32[4,4,24,512]{3,2,1,0:T(8,128)S(1)}, bf16[4,4,24,512]{3,2,1,0:T(8,128)(2,1)S(1)}) custom-call(s32[3]{0:T(128)S(1)} %pad_add_fusion.pos_ref, bf16[704,512]{1,0:T(8,128)(2,1)} %bitcast.19, bf16[512,512]{1,0:T(8,128)(2,1)} %get-tuple-element.54.taps_hbm), custom_call_target="tpu_custom_call" | custom-call | tf_op jit(solution)/shard_map/weight_grad/pallas_call | solution.py:387
  49.3 1.1 %collective-permute-done.5.refs_2_ = bf16[4,24,512]{2,1,0:T(8,128)(2,1)S(1)} collective-permute-done((bf16[4,24,512]{2,1,0:T(8,128)(2,1)S(1)}, bf16[4,24,512]{2,1,0:T(8,128)(2,1)S(1)}, u32[]{:S(2)}, u32[]{:S(2)}) %collective-permute-start.5) | collective-permute-done | bytes 98336 | tf_op jit(solution)/shard_map/ppermute | solution.py:32
  50.3 1.0 %collective-permute-done.6.refs_3_ = bf16[4,24,512]{2,1,0:T(8,128)(2,1)S(1)} collective-permute-done((bf16[4,24,512]{2,1,0:T(8,128)(2,1)S(1)}, bf16[4,24,512]{2,1,0:T(8,128)(2,1)S(1)}, u32[]{:S(2)}, u32[]{:S(2)}) %collective-permute-start.6) | collective-permute-done | bytes 98336 | tf_op jit(solution)/shard_map/ppermute | solution.py:32
  51.4 0.1 collective-permute-start.7
  51.5 0.5 collective-permute-start.15
  52.0 1.3 %collective-permute-done.7.got_upper_hbm = bf16[4,4,24,512]{3,2,1,0:T(8,128)(2,1)} collective-permute-done((bf16[4,4,24,512]{3,2,1,0:T(8,128)(2,1)S(1)}, bf16[4,4,24,512]{3,2,1,0:T(8,128)(2,1)}, u32[]{:S(2)}, u32[]{:S(2)}) %collective-permute-start.7) | collective-permute-done | bytes 393248 | tf_op jit(solution)/shard_map/ppermute | solution.py:32
  53.3 1.9 %all-to-all-done.1.mid_ref = bf16[8,96,512]{2,1,0:T(8,128)(2,1)S(1)} async-done(((bf16[8,96,512]{2,1,0:T(8,128)(2,1)}), bf16[8,96,512]{2,1,0:T(8,128)(2,1)S(1)}, u32[]{:S(2)}, u32[]{:S(2)}) %all-to-all-start.1) | async-done | bytes 786464 | tf_op jit(solution)/shard_map/all_to_all | solution.py:450
  55.2 3.0 %lower.1 = (bf16[512,1024]{1,0:T(8,128)(2,1)S(1)}, f32[4,4,24,512]{3,2,1,0:T(8,128)S(1)}, bf16[4,4,24,512]{3,2,1,0:T(8,128)(2,1)S(1)}) custom-call(s32[3]{0:T(128)S(1)} %pad_add_fusion.pos_ref, bf16[8,96,512]{2,1,0:T(8,128)(2,1)S(1)} %all-to-all-done.1.mid_ref, f32[96,1024]{1,0:T(8,128)} %fusion.6.slope_hbm, f32[96,256]{1,0:T(8,128)S(1)} %copy-done, ...), custom_call_target="tpu_custom_call" | custom-call | tf_op jit(solution)/shard_map/lower/pallas_call | solution.py:474
  58.3 0.1 collective-permute-start.8
  58.4 1.2 %lower_weight.1.w_ref = bf16[640,512]{1,0:T(8,128)(2,1)S(1)} custom-call(s32[3]{0:T(128)S(1)} %pad_add_fusion.pos_ref, bf16[16,24,512]{2,1,0:T(8,128)(2,1)S(1)} %join.1.own_ref, bf16[16,24,512]{2,1,0:T(8,128)(2,1)} %collective-permute-done.15.other_ref), custom_call_target="tpu_custom_call" | custom-call | tf_op jit(solution)/shard_map/lower_weight/pallas_call | solution.py:461
  59.6 1.9 %low.1 = bf16[8,80,1024]{2,1,0:T(8,128)(2,1)} custom-call(bf16[512,1024]{1,0:T(8,128)(2,1)S(1)} %get-tuple-element.87.taps_ref, bf16[640,512]{1,0:T(8,128)(2,1)S(1)} %lower_weight.1.w_ref), custom_call_target="tpu_custom_call" | custom-call | tf_op jit(solution)/shard_map/low/pallas_call | solution.py:496
  61.5 3.6 %all-to-all-start.2 = ((bf16[8,80,1024]{2,1,0:T(8,128)(2,1)}), bf16[8,80,1024]{2,1,0:T(8,128)(2,1)S(1)}, u32[]{:S(2)}, u32[]{:S(2)}) async-start(bf16[8,80,1024]{2,1,0:T(8,128)(2,1)} %low.1), calls=%async_computation.2 | async-start | bytes 2621440 | tf_op jit(solution)/shard_map/all_to_all | solution.py:506
  65.2 1.1 %core_sum.1 = (f32[4,48,512]{2,1,0:T(8,128)S(1)}, bf16[4,48,512]{2,1,0:T(8,128)(2,1)S(1)}, bf16[4,48,512]{2,1,0:T(8,128)(2,1)S(1)}, bf16[4,48,512]{2,1,0:T(8,128)(2,1)S(1)}) custom-call(f32[4,4,24,512]{3,2,1,0:T(8,128)S(1)} %get-tuple-element.55.keep_upper_ref, bf16[4,4,24,512]{3,2,1,0:T(8,128)(2,1)} %collective-permute-done.7.got_upper_hbm, ...), custom_call_target="tpu_custom_call" | custom-call | tf_op jit(solution)/shard_map/core_sum/pallas_call | solution.py:112
  66.3 1.5 %collective-permute-start.9 = (bf16[4,48,512]{2,1,0:T(8,128)(2,1)S(1)}, bf16[4,48,512]{2,1,0:T(8,128)(2,1)S(1)}, u32[]{:S(2)}, u32[]{:S(2)}) collective-permute-start(bf16[4,48,512]{2,1,0:T(8,128)(2,1)S(1)} %get-tuple-element.80), channel_id=1, source_target_pairs={{0,2},{2,4},{4,6},{6,0},{1,3},{3,5},{5,7},{7,1},{8,10},{10,12},{12... | collective-permute-start | bytes 589832 | tf_op jit(solution)/shard_map/ppermute | solution.py:32
  67.8 2.2 %collective-permute-start.10 = (bf16[4,48,512]{2,1,0:T(8,128)(2,1)S(1)}, bf16[4,48,512]{2,1,0:T(8,128)(2,1)S(1)}, u32[]{:S(2)}, u32[]{:S(2)}) collective-permute-start(bf16[4,48,512]{2,1,0:T(8,128)(2,1)S(1)} %get-tuple-element.81), channel_id=1, source_target_pairs={{0,4},{2,6},{4,0},{6,2},{1,5},{3,7},{5,1},{7,3},{8,12},{10,14},{12... | collective-permute-start | bytes 589832 | tf_op jit(solution)/shard_map/ppermute | solution.py:32
  70.0 1.4 %collective-permute-start.11 = (bf16[4,48,512]{2,1,0:T(8,128)(2,1)S(1)}, bf16[4,48,512]{2,1,0:T(8,128)(2,1)S(1)}, u32[]{:S(2)}, u32[]{:S(2)}) collective-permute-start(bf16[4,48,512]{2,1,0:T(8,128)(2,1)S(1)} %get-tuple-element.82), channel_id=1, source_target_pairs={{0,6},{2,0},{4,2},{6,4},{1,7},{3,1},{5,3},{7,5},{8,14},{10,8},{12,... | collective-permute-start | bytes 589832 | tf_op jit(solution)/shard_map/ppermute | solution.py:32
  71.4 2.9 %collective-permute-done.9.refs_0_ = bf16[4,48,512]{2,1,0:T(8,128)(2,1)S(1)} collective-permute-done((bf16[4,48,512]{2,1,0:T(8,128)(2,1)S(1)}, bf16[4,48,512]{2,1,0:T(8,128)(2,1)S(1)}, u32[]{:S(2)}, u32[]{:S(2)}) %collective-permute-start.9) | collective-permute-done | bytes 196640 | tf_op jit(solution)/shard_map/ppermute | solution.py:32
  74.2 2.8 %collective-permute-done.10.refs_1_ = bf16[4,48,512]{2,1,0:T(8,128)(2,1)S(1)} collective-permute-done((bf16[4,48,512]{2,1,0:T(8,128)(2,1)S(1)}, bf16[4,48,512]{2,1,0:T(8,128)(2,1)S(1)}, u32[]{:S(2)}, u32[]{:S(2)}) %collective-permute-start.10) | collective-permute-done | bytes 196640 | tf_op jit(solution)/shard_map/ppermute | solution.py:32
  77.1 3.5 %collective-permute-done.11.refs_2_ = bf16[4,48,512]{2,1,0:T(8,128)(2,1)S(1)} collective-permute-done((bf16[4,48,512]{2,1,0:T(8,128)(2,1)S(1)}, bf16[4,48,512]{2,1,0:T(8,128)(2,1)S(1)}, u32[]{:S(2)}, u32[]{:S(2)}) %collective-permute-start.11) | collective-permute-done | bytes 196640 | tf_op jit(solution)/shard_map/ppermute | solution.py:32
  80.5 0.1 y_sum.1
  80.6 1.3 %collective-permute-start.12 = (bf16[48,512]{1,0:T(8,128)(2,1)S(1)}, bf16[48,512]{1,0:T(8,128)(2,1)S(1)}, u32[]{:S(2)}, u32[]{:S(2)}) collective-permute-start(bf16[48,512]{1,0:T(8,128)(2,1)S(1)} %get-tuple-element.83), channel_id=1, source_target_pairs={{0,8},{8,16},{16,24},{24,0},{1,9},{9,17},{17,25},{25,1},{2,10},{10... | collective-permute-start | bytes 147464 | tf_op jit(solution)/shard_map/ppermute | solution.py:32
  81.9 2.8 %collective-permute-start.13 = (bf16[48,512]{1,0:T(8,128)(2,1)S(1)}, bf16[48,512]{1,0:T(8,128)(2,1)S(1)}, u32[]{:S(2)}, u32[]{:S(2)}) collective-permute-start(bf16[48,512]{1,0:T(8,128)(2,1)S(1)} %get-tuple-element.84), channel_id=1, source_target_pairs={{0,16},{8,24},{16,0},{24,8},{1,17},{9,25},{17,1},{25,9},{2,18},{10... | collective-permute-start | bytes 147464 | tf_op jit(solution)/shard_map/ppermute | solution.py:32
  84.7 1.8 %collective-permute-start.14 = (bf16[48,512]{1,0:T(8,128)(2,1)S(1)}, bf16[48,512]{1,0:T(8,128)(2,1)S(1)}, u32[]{:S(2)}, u32[]{:S(2)}) collective-permute-start(bf16[48,512]{1,0:T(8,128)(2,1)S(1)} %get-tuple-element.85), channel_id=1, source_target_pairs={{0,24},{8,0},{16,8},{24,16},{1,25},{9,1},{17,9},{25,17},{2,26},{10... | collective-permute-start | bytes 147464 | tf_op jit(solution)/shard_map/ppermute | solution.py:32
  86.5 0.8 low_total.1
  87.3 0.4 collective-permute-done.12.refs_0_
  87.7 2.1 %collective-permute-done.13.refs_1_ = bf16[48,512]{1,0:T(8,128)(2,1)S(1)} collective-permute-done((bf16[48,512]{1,0:T(8,128)(2,1)S(1)}, bf16[48,512]{1,0:T(8,128)(2,1)S(1)}, u32[]{:S(2)}, u32[]{:S(2)}) %collective-permute-start.13) | collective-permute-done | bytes 49184 | tf_op jit(solution)/shard_map/ppermute | solution.py:32
  89.9 2.4 %collective-permute-done.14.refs_2_ = bf16[48,512]{1,0:T(8,128)(2,1)S(1)} collective-permute-done((bf16[48,512]{1,0:T(8,128)(2,1)S(1)}, bf16[48,512]{1,0:T(8,128)(2,1)S(1)}, u32[]{:S(2)}, u32[]{:S(2)}) %collective-permute-start.14) | collective-permute-done | bytes 49184 | tf_op jit(solution)/shard_map/ppermute | solution.py:32
  92.2 0.9 %z_sum.1 = (f32[5,22,96]{2,1,0:T(8,128)}, f32[5,20,88]{2,1,0:T(8,128)}) custom-call(f32[48,512]{1,0:T(8,128)S(1)} %get-tuple-element.91.own_ref, bf16[48,512]{1,0:T(8,128)(2,1)S(1)} %collective-permute-done.12.refs_0_, bf16[48,512]{1,0:T(8,128)(2,1)S(1)} %collective-permute-done.13.refs_1_, bf16[48,512]{1,0:T(8,128)(2,1)S(1)} %collective-permute-done.14.refs_2_), custom_call_target="tpu_custom_call" | custom-call | tf_op jit(solution)/shard_map/z_sum/pallas_call | solution.py:98
  (16 shorter events, 0.1 us)
Async XLA Ops:
  0.6 23.4 %copy-start.2 = (bf16[1024,88]{0,1:T(8,128)(2,1)S(1)}, bf16[1024,88]{0,1:T(8,128)(2,1)}, u32[]{:S(2)}) copy-start(bf16[1024,88]{0,1:T(8,128)(2,1)} %param.11) | copy-start | bytes 540676
  0.6 24.4 %copy-start.3 = (bf16[512,96]{0,1:T(8,128)(2,1)S(1)}, bf16[512,96]{0,1:T(8,128)(2,1)}, u32[]{:S(2)}) copy-start(bf16[512,96]{0,1:T(8,128)(2,1)} %param.9) | copy-start | bytes 294916
  2.8 22.4 %copy-start.1 = (bf16[1024,640]{1,0:T(8,128)(2,1)S(1)}, bf16[1024,640]{1,0:T(8,128)(2,1)}, u32[]{:S(2)}) copy-start(bf16[1024,640]{1,0:T(8,128)(2,1)} %param.10) | copy-start | bytes 3932164
  2.8 30.0 %all-to-all-start = ((bf16[16,32,512]{2,1,0:T(8,128)(2,1)}), bf16[16,32,512]{2,1,0:T(8,128)(2,1)S(1)}, u32[]{:S(2)}, u32[]{:S(2)}) async-start(bf16[16,32,512]{2,1,0:T(8,128)(2,1)} %get-tuple-element.50), calls=%async_computation | async-start | bytes 1048576 | tf_op jit(solution)/shard_map/all_to_all | solution.py:426
  14.5 15.0 %collective-permute-start = (bf16[24,512]{1,0:T(8,128)(2,1)S(1)}, bf16[24,512]{1,0:T(8,128)(2,1)S(1)}, u32[]{:S(2)}, u32[]{:S(2)}) collective-permute-start(bf16[24,512]{1,0:T(8,128)(2,1)S(1)} %get-tuple-element.61), channel_id=1, source_target_pairs={{0,8},{8,16},{16,24},{24,0},{1,9},{9,17},{17,25},{25,1},{2,10},{10... | collective-permute-start | bytes 73736 | tf_op jit(solution)/shard_map/ppermute | solution.py:32
  16.9 16.0 %collective-permute-start.1 = (bf16[24,512]{1,0:T(8,128)(2,1)S(1)}, bf16[24,512]{1,0:T(8,128)(2,1)S(1)}, u32[]{:S(2)}, u32[]{:S(2)}) collective-permute-start(bf16[24,512]{1,0:T(8,128)(2,1)S(1)} %get-tuple-element.61), channel_id=1, source_target_pairs={{0,16},{8,24},{16,0},{24,8},{1,17},{9,25},{17,1},{25,9},{2,18},{10... | collective-permute-start | bytes 73736 | tf_op jit(solution)/shard_map/ppermute | solution.py:32
  20.5 12.4 %collective-permute-start.2 = (bf16[24,512]{1,0:T(8,128)(2,1)S(1)}, bf16[24,512]{1,0:T(8,128)(2,1)S(1)}, u32[]{:S(2)}, u32[]{:S(2)}) collective-permute-start(bf16[24,512]{1,0:T(8,128)(2,1)S(1)} %get-tuple-element.61), channel_id=1, source_target_pairs={{0,24},{8,0},{16,8},{24,16},{1,25},{9,1},{17,9},{25,17},{2,26},{10... | collective-permute-start | bytes 73736 | tf_op jit(solution)/shard_map/ppermute | solution.py:32
  32.9 1.9 %collective-permute-start.3 = (bf16[16,32,512]{2,1,0:T(8,128)(2,1)S(1)}, bf16[16,32,512]{2,1,0:T(8,128)(2,1)S(1)}, u32[]{:S(2)}, u32[]{:S(2)}) collective-permute-start(bf16[16,32,512]{2,1,0:T(8,128)(2,1)S(1)} %all-to-all-done.own_ref), channel_id=1, source_target_pairs={{0,1},{1,0},{2,3},{3,2},{4,5},{5,4},{6,7},{7,6},{8,9},{9,8},{10,11... | collective-permute-start | bytes 1572872 | tf_op jit(solution)/shard_map/ppermute | solution.py:32
  37.5 17.7 %all-to-all-start.1 = ((bf16[8,96,512]{2,1,0:T(8,128)(2,1)}), bf16[8,96,512]{2,1,0:T(8,128)(2,1)S(1)}, u32[]{:S(2)}, u32[]{:S(2)}) async-start(bf16[8,96,512]{2,1,0:T(8,128)(2,1)} %get-tuple-element.56), calls=%async_computation.1 | async-start | bytes 1572864 | tf_op jit(solution)/shard_map/all_to_all | solution.py:450
  42.0 13.2 %copy-start = (f32[96,256]{1,0:T(8,128)S(1)}, f32[96,256]{1,0:T(8,128)}, u32[]{:S(2)}) copy-start(f32[96,256]{1,0:T(8,128)} %get-tuple-element.75.edge_ref) | copy-start | bytes 294916
  42.1 7.2 %collective-permute-start.4 = (bf16[4,24,512]{2,1,0:T(8,128)(2,1)S(1)}, bf16[4,24,512]{2,1,0:T(8,128)(2,1)S(1)}, u32[]{:S(2)}, u32[]{:S(2)}) collective-permute-start(bf16[4,24,512]{2,1,0:T(8,128)(2,1)S(1)} %pad_maximum_fusion.refs_0_), channel_id=1, source_target_pairs={{0,2},{2,4},{4,6},{6,0},{1,3},{3,5},{5,7},{7,1},{8,10},{10,12},{12... | collective-permute-start | bytes 294920 | tf_op jit(solution)/shard_map/ppermute | solution.py:32
  43.5 6.9 %collective-permute-start.5 = (bf16[4,24,512]{2,1,0:T(8,128)(2,1)S(1)}, bf16[4,24,512]{2,1,0:T(8,128)(2,1)S(1)}, u32[]{:S(2)}, u32[]{:S(2)}) collective-permute-start(bf16[4,24,512]{2,1,0:T(8,128)(2,1)S(1)} %pad_maximum_fusion.refs_0_), channel_id=1, source_target_pairs={{0,4},{2,6},{4,0},{6,2},{1,5},{3,7},{5,1},{7,3},{8,12},{10,14},{12... | collective-permute-start | bytes 294920 | tf_op jit(solution)/shard_map/ppermute | solution.py:32
  45.7 5.7 %collective-permute-start.6 = (bf16[4,24,512]{2,1,0:T(8,128)(2,1)S(1)}, bf16[4,24,512]{2,1,0:T(8,128)(2,1)S(1)}, u32[]{:S(2)}, u32[]{:S(2)}) collective-permute-start(bf16[4,24,512]{2,1,0:T(8,128)(2,1)S(1)} %pad_maximum_fusion.refs_0_), channel_id=1, source_target_pairs={{0,6},{2,0},{4,2},{6,4},{1,7},{3,1},{5,3},{7,5},{8,14},{10,8},{12,... | collective-permute-start | bytes 294920 | tf_op jit(solution)/shard_map/ppermute | solution.py:32
  51.4 1.9 %collective-permute-start.7 = (bf16[4,4,24,512]{3,2,1,0:T(8,128)(2,1)S(1)}, bf16[4,4,24,512]{3,2,1,0:T(8,128)(2,1)}, u32[]{:S(2)}, u32[]{:S(2)}) collective-permute-start(bf16[4,4,24,512]{3,2,1,0:T(8,128)(2,1)S(1)} %get-tuple-element.71), channel_id=1, source_target_pairs={{0,1},{1,0},{2,3},{3,2},{4,5},{5,4},{6,7},{7,6},{8,9},{9,8},{10,11... | collective-permute-start | bytes 1179656 | tf_op jit(solution)/shard_map/ppermute | solution.py:32
  51.5 6.9 %collective-permute-start.15 = (bf16[16,24,512]{2,1,0:T(8,128)(2,1)S(1)}, bf16[16,24,512]{2,1,0:T(8,128)(2,1)}, u32[]{:S(2)}, u32[]{:S(2)}) collective-permute-start(bf16[16,24,512]{2,1,0:T(8,128)(2,1)S(1)} %join.1.own_ref), channel_id=1, source_target_pairs={{0,1},{1,0},{2,3},{3,2},{4,5},{5,4},{6,7},{7,6},{8,9},{9,8},{10,11... | collective-permute-start | bytes 1179656 | tf_op jit(solution)/shard_map/ppermute | solution.py:32
  58.3 3.2 %collective-permute-start.8 = (bf16[4,4,24,512]{3,2,1,0:T(8,128)(2,1)S(1)}, bf16[4,4,24,512]{3,2,1,0:T(8,128)(2,1)S(1)}, u32[]{:S(2)}, u32[]{:S(2)}) collective-permute-start(bf16[4,4,24,512]{3,2,1,0:T(8,128)(2,1)S(1)} %get-tuple-element.78), channel_id=1, source_target_pairs={{0,1},{1,0},{2,3},{3,2},{4,5},{5,4},{6,7},{7,6},{8,9},{9,8},{10,11... | collective-permute-start | bytes 1179656 | tf_op jit(solution)/shard_map/ppermute | solution.py:32
  61.5 25.0 %all-to-all-start.2 = ((bf16[8,80,1024]{2,1,0:T(8,128)(2,1)}), bf16[8,80,1024]{2,1,0:T(8,128)(2,1)S(1)}, u32[]{:S(2)}, u32[]{:S(2)}) async-start(bf16[8,80,1024]{2,1,0:T(8,128)(2,1)} %low.1), calls=%async_computation.2 | async-start | bytes 2621440 | tf_op jit(solution)/shard_map/all_to_all | solution.py:506
  66.3 8.0 %collective-permute-start.9 = (bf16[4,48,512]{2,1,0:T(8,128)(2,1)S(1)}, bf16[4,48,512]{2,1,0:T(8,128)(2,1)S(1)}, u32[]{:S(2)}, u32[]{:S(2)}) collective-permute-start(bf16[4,48,512]{2,1,0:T(8,128)(2,1)S(1)} %get-tuple-element.80), channel_id=1, source_target_pairs={{0,2},{2,4},{4,6},{6,0},{1,3},{3,5},{5,7},{7,1},{8,10},{10,12},{12... | collective-permute-start | bytes 589832 | tf_op jit(solution)/shard_map/ppermute | solution.py:32
  67.8 9.3 %collective-permute-start.10 = (bf16[4,48,512]{2,1,0:T(8,128)(2,1)S(1)}, bf16[4,48,512]{2,1,0:T(8,128)(2,1)S(1)}, u32[]{:S(2)}, u32[]{:S(2)}) collective-permute-start(bf16[4,48,512]{2,1,0:T(8,128)(2,1)S(1)} %get-tuple-element.81), channel_id=1, source_target_pairs={{0,4},{2,6},{4,0},{6,2},{1,5},{3,7},{5,1},{7,3},{8,12},{10,14},{12... | collective-permute-start | bytes 589832 | tf_op jit(solution)/shard_map/ppermute | solution.py:32
  70.0 10.5 %collective-permute-start.11 = (bf16[4,48,512]{2,1,0:T(8,128)(2,1)S(1)}, bf16[4,48,512]{2,1,0:T(8,128)(2,1)S(1)}, u32[]{:S(2)}, u32[]{:S(2)}) collective-permute-start(bf16[4,48,512]{2,1,0:T(8,128)(2,1)S(1)} %get-tuple-element.82), channel_id=1, source_target_pairs={{0,6},{2,0},{4,2},{6,4},{1,7},{3,1},{5,3},{7,5},{8,14},{10,8},{12,... | collective-permute-start | bytes 589832 | tf_op jit(solution)/shard_map/ppermute | solution.py:32
  80.6 7.1 %collective-permute-start.12 = (bf16[48,512]{1,0:T(8,128)(2,1)S(1)}, bf16[48,512]{1,0:T(8,128)(2,1)S(1)}, u32[]{:S(2)}, u32[]{:S(2)}) collective-permute-start(bf16[48,512]{1,0:T(8,128)(2,1)S(1)} %get-tuple-element.83), channel_id=1, source_target_pairs={{0,8},{8,16},{16,24},{24,0},{1,9},{9,17},{17,25},{25,1},{2,10},{10... | collective-permute-start | bytes 147464 | tf_op jit(solution)/shard_map/ppermute | solution.py:32
  81.9 8.0 %collective-permute-start.13 = (bf16[48,512]{1,0:T(8,128)(2,1)S(1)}, bf16[48,512]{1,0:T(8,128)(2,1)S(1)}, u32[]{:S(2)}, u32[]{:S(2)}) collective-permute-start(bf16[48,512]{1,0:T(8,128)(2,1)S(1)} %get-tuple-element.84), channel_id=1, source_target_pairs={{0,16},{8,24},{16,0},{24,8},{1,17},{9,25},{17,1},{25,9},{2,18},{10... | collective-permute-start | bytes 147464 | tf_op jit(solution)/shard_map/ppermute | solution.py:32
  84.7 7.6 %collective-permute-start.14 = (bf16[48,512]{1,0:T(8,128)(2,1)S(1)}, bf16[48,512]{1,0:T(8,128)(2,1)S(1)}, u32[]{:S(2)}, u32[]{:S(2)}) collective-permute-start(bf16[48,512]{1,0:T(8,128)(2,1)S(1)} %get-tuple-element.85), channel_id=1, source_target_pairs={{0,24},{8,0},{16,8},{24,16},{1,25},{9,1},{17,9},{25,17},{2,26},{10... | collective-permute-start | bytes 147464 | tf_op jit(solution)/shard_map/ppermute | solution.py:32

commit v7 on v5

--- a/solution.py
+++ b/solution.py
@@ -476,7 +476,7 @@
     )(lower_taps, lower_full)
     low_part, _ = lax.optimization_barrier((low_part, lower_got))
     low_parts = lax.all_to_all(low_part, DP, split_axis=0, concat_axis=0, tiled=True)
-    got = [shifted(send, "y", NY, s + 1) for s, send in enumerate(sends)]
+    got = [shifted(sends[s], "y", NY, s + 1) for s in (1, 0, 2)]
     low_grad = pl.pallas_call(
         total_kernel,
         out_shape=jax.ShapeDtypeStruct((80, 1024), BF),

time: 93.1 us -> 93.1 us (level); the launches traced: 92.6 us -> 91.6 us
  no operation moved by 1% of the time
where the time goes in v7:
time: 93.1 us; the launch traced here: 91.6 us
  starting transfers between devices  45 us (48%)
  waiting for transfers between devices  26.7 us (29%)
  Pallas kernels  16.1 us (17%)
  local copies, waits for them, and re-layouts  2.58 us (3%)
    ppermute x16, starting transfers between devices, shifted(): lax.ppermute(block, axis, [(i, (i + step) % count) for i in range(count)])  25.1 us
    ppermute x16, waiting for transfers between devices, shifted(): lax.ppermute(block, axis, [(i, (i + step) % count) for i in range(count)])  24.8 us
    all_to_all x1, starting transfers between devices, local(): lax.all_to_all(packed, ('zh', 'y'), split_axis=0, concat_axis=0, tiled=True)  11.6 us
    all_to_all x1, starting transfers between devices, local(): lax.all_to_all(mid_part, DP, split_axis=0, concat_axis=0, tiled=True)  4.55 us
    pallas_call x2, Pallas kernels, weight_grad(): pl.pallas_call(fetched_weight_grad_kernel if fetch else weight_grad_kerne...  4.09 us
    all_to_all x1, starting transfers between devices, local(): lax.all_to_all(low_part, DP, split_axis=0, concat_axis=0, tiled=True)  3.71 us
    pallas_call x1, Pallas kernels, local(): pl.pallas_call(upper_kernel, out_shape=(pltpu.HBM((8, 96, 512), BF), pltp...  2.67 us
    unnamed x15, local copies, waits for them, and re-layouts  2.51 us
  transfers between devices with their start and end apart: 19, of which 13 were waited for; matrix products, arithmetic and copies ran while one was open for 2% of the time, Pallas kernels for 11%

profile of v7, /device:TPU:8, one launch (start us, length us, event | category | flops | bytes accessed | tf_op | source)
XLA Modules:
  0.0 91.6 jit_solution(5228409460616186160)
XLA Ops:
  0.7 2.1 %pack.1 = (bf16[16,32,512]{2,1,0:T(8,128)(2,1)}, bf16[24,512]{1,0:T(8,128)(2,1)S(1)}) custom-call(bf16[3,8192]{1,0:T(4,128)(2,1)} %bitcast.24, bf16[5,22,96]{2,1,0:T(8,128)(2,1)} %upper_hbm.1, bf16[5,20,88]{2,1,0:T(8,128)(2,1)} %lower_hbm.1, bf16[96,512]{1,0:T(8,128)(2,1)} %bitcast.22, bf16[88,1024]{1,0:T(8,128)(2,1)} %bitcast.20), custom_call_target="tpu_custom_call" | custom-call | tf_op jit(solution)/shard_map/pack/pallas_call | solution.py:385
  2.8 11.6 %all-to-all-start = ((bf16[16,32,512]{2,1,0:T(8,128)(2,1)}), bf16[16,32,512]{2,1,0:T(8,128)(2,1)S(1)}, u32[]{:S(2)}, u32[]{:S(2)}) async-start(bf16[16,32,512]{2,1,0:T(8,128)(2,1)} %get-tuple-element.49), calls=%async_computation | async-start | bytes 1048576 | tf_op jit(solution)/shard_map/all_to_all | solution.py:410
  14.3 2.4 %collective-permute-start = (bf16[24,512]{1,0:T(8,128)(2,1)S(1)}, bf16[24,512]{1,0:T(8,128)(2,1)S(1)}, u32[]{:S(2)}, u32[]{:S(2)}) collective-permute-start(bf16[24,512]{1,0:T(8,128)(2,1)S(1)} %get-tuple-element.60), channel_id=1, source_target_pairs={{0,8},{8,16},{16,24},{24,0},{1,9},{9,17},{17,25},{25,1},{2,10},{10... | collective-permute-start | bytes 73736 | tf_op jit(solution)/shard_map/ppermute | solution.py:32
  16.7 3.6 %collective-permute-start.1 = (bf16[24,512]{1,0:T(8,128)(2,1)S(1)}, bf16[24,512]{1,0:T(8,128)(2,1)S(1)}, u32[]{:S(2)}, u32[]{:S(2)}) collective-permute-start(bf16[24,512]{1,0:T(8,128)(2,1)S(1)} %get-tuple-element.60), channel_id=1, source_target_pairs={{0,16},{8,24},{16,0},{24,8},{1,17},{9,25},{17,1},{25,9},{2,18},{10... | collective-permute-start | bytes 73736 | tf_op jit(solution)/shard_map/ppermute | solution.py:32
  20.3 3.6 %collective-permute-start.2 = (bf16[24,512]{1,0:T(8,128)(2,1)S(1)}, bf16[24,512]{1,0:T(8,128)(2,1)S(1)}, u32[]{:S(2)}, u32[]{:S(2)}) collective-permute-start(bf16[24,512]{1,0:T(8,128)(2,1)S(1)} %get-tuple-element.60), channel_id=1, source_target_pairs={{0,24},{8,0},{16,8},{24,16},{1,25},{9,1},{17,9},{25,17},{2,26},{10... | collective-permute-start | bytes 73736 | tf_op jit(solution)/shard_map/ppermute | solution.py:32
  23.9 0.1 reshape.12
  23.9 0.2 fusion.6.slope_ref
  24.1 0.1 fusion.13.slope_ref
  24.2 1.6 %copy.11 = bf16[1024,640]{0,1:T(8,128)(2,1)S(1)} copy(bf16[1024,640]{1,0:T(8,128)(2,1)} %param.10) | data formatting | bytes 2621440 | tf_op args[3]
  25.9 3.5 %collective-permute-done = bf16[24,512]{1,0:T(8,128)(2,1)S(1)} collective-permute-done((bf16[24,512]{1,0:T(8,128)(2,1)S(1)}, bf16[24,512]{1,0:T(8,128)(2,1)S(1)}, u32[]{:S(2)}, u32[]{:S(2)}) %collective-permute-start) | collective-permute-done | bytes 24608 | tf_op jit(solution)/shard_map/ppermute | solution.py:32
  29.3 3.3 %collective-permute-done.1 = bf16[24,512]{1,0:T(8,128)(2,1)S(1)} collective-permute-done((bf16[24,512]{1,0:T(8,128)(2,1)S(1)}, bf16[24,512]{1,0:T(8,128)(2,1)S(1)}, u32[]{:S(2)}, u32[]{:S(2)}) %collective-permute-start.1) | collective-permute-done | bytes 24608 | tf_op jit(solution)/shard_map/ppermute | solution.py:32
  32.7 0.1 pad_add_fusion.pos_ref
  32.8 1.8 %collective-permute-done.3.other_ref = bf16[16,32,512]{2,1,0:T(8,128)(2,1)S(1)} collective-permute-done((bf16[16,32,512]{2,1,0:T(8,128)(2,1)S(1)}, bf16[16,32,512]{2,1,0:T(8,128)(2,1)S(1)}, u32[]{:S(2)}, u32[]{:S(2)}) %collective-permute-start.3) | collective-permute-done | bytes 524320 | tf_op jit(solution)/shard_map/ppermute | solution.py:32
  34.6 2.7 %upper.1 = (bf16[8,96,512]{2,1,0:T(8,128)(2,1)}, bf16[512,512]{1,0:T(8,128)(2,1)}, f32[96,256]{1,0:T(8,128)}) custom-call(s32[3]{0:T(128)S(1)} %pad_add_fusion.pos_ref, f32[96,512]{1,0:T(8,128)S(1)} %fusion.13.slope_ref, bf16[16,32,512]{2,1,0:T(8,128)(2,1)S(1)} %all-to-all-done.own_ref, bf16[16,32,512]{2,1,0:T(8,128)(2,1)S(1)} %collective-permute-done.3.other_ref), custom_call_target="tpu_custom_call" | custom-call | tf_op jit(solution)/shard_map/upper/pallas_call | solution.py:416
  37.3 4.6 %all-to-all-start.1 = ((bf16[8,96,512]{2,1,0:T(8,128)(2,1)}), bf16[8,96,512]{2,1,0:T(8,128)(2,1)S(1)}, u32[]{:S(2)}, u32[]{:S(2)}) async-start(bf16[8,96,512]{2,1,0:T(8,128)(2,1)} %get-tuple-element.55), calls=%async_computation.1 | async-start | bytes 1572864 | tf_op jit(solution)/shard_map/all_to_all | solution.py:434
  41.9 1.4 %collective-permute-start.4 = (bf16[4,24,512]{2,1,0:T(8,128)(2,1)S(1)}, bf16[4,24,512]{2,1,0:T(8,128)(2,1)S(1)}, u32[]{:S(2)}, u32[]{:S(2)}) collective-permute-start(bf16[4,24,512]{2,1,0:T(8,128)(2,1)S(1)} %pad_maximum_fusion.refs_0_), channel_id=1, source_target_pairs={{0,2},{2,4},{4,6},{6,0},{1,3},{3,5},{5,7},{7,1},{8,10},{10,12},{12... | collective-permute-start | bytes 294920 | tf_op jit(solution)/shard_map/ppermute | solution.py:32
  43.2 2.2 %collective-permute-start.5 = (bf16[4,24,512]{2,1,0:T(8,128)(2,1)S(1)}, bf16[4,24,512]{2,1,0:T(8,128)(2,1)S(1)}, u32[]{:S(2)}, u32[]{:S(2)}) collective-permute-start(bf16[4,24,512]{2,1,0:T(8,128)(2,1)S(1)} %pad_maximum_fusion.refs_0_), channel_id=1, source_target_pairs={{0,4},{2,6},{4,0},{6,2},{1,5},{3,7},{5,1},{7,3},{8,12},{10,14},{12... | collective-permute-start | bytes 294920 | tf_op jit(solution)/shard_map/ppermute | solution.py:32
  45.5 1.0 %collective-permute-start.6 = (bf16[4,24,512]{2,1,0:T(8,128)(2,1)S(1)}, bf16[4,24,512]{2,1,0:T(8,128)(2,1)S(1)}, u32[]{:S(2)}, u32[]{:S(2)}) collective-permute-start(bf16[4,24,512]{2,1,0:T(8,128)(2,1)S(1)} %pad_maximum_fusion.refs_0_), channel_id=1, source_target_pairs={{0,6},{2,0},{4,2},{6,4},{1,7},{3,1},{5,3},{7,5},{8,14},{10,8},{12,... | collective-permute-start | bytes 294920 | tf_op jit(solution)/shard_map/ppermute | solution.py:32
  46.5 2.5 %weight_grad.2 = (f32[4,4,24,512]{3,2,1,0:T(8,128)S(1)}, bf16[4,4,24,512]{3,2,1,0:T(8,128)(2,1)S(1)}) custom-call(s32[3]{0:T(128)S(1)} %pad_add_fusion.pos_ref, bf16[704,512]{1,0:T(8,128)(2,1)} %bitcast.19, bf16[512,512]{1,0:T(8,128)(2,1)} %get-tuple-element.53.taps_hbm), custom_call_target="tpu_custom_call" | custom-call | tf_op jit(solution)/shard_map/weight_grad/pallas_call | solution.py:371
  49.0 0.9 copy-done
  49.9 0.2 collective-permute-done.5.refs_2_
  50.1 1.0 %collective-permute-done.6.refs_3_ = bf16[4,24,512]{2,1,0:T(8,128)(2,1)S(1)} collective-permute-done((bf16[4,24,512]{2,1,0:T(8,128)(2,1)S(1)}, bf16[4,24,512]{2,1,0:T(8,128)(2,1)S(1)}, u32[]{:S(2)}, u32[]{:S(2)}) %collective-permute-start.6) | collective-permute-done | bytes 98336 | tf_op jit(solution)/shard_map/ppermute | solution.py:32
  51.2 0.1 collective-permute-start.7
  51.3 0.5 collective-permute-start.15
  51.8 1.3 %collective-permute-done.7.got_upper_hbm = bf16[4,4,24,512]{3,2,1,0:T(8,128)(2,1)} collective-permute-done((bf16[4,4,24,512]{3,2,1,0:T(8,128)(2,1)S(1)}, bf16[4,4,24,512]{3,2,1,0:T(8,128)(2,1)}, u32[]{:S(2)}, u32[]{:S(2)}) %collective-permute-start.7) | collective-permute-done | bytes 393248 | tf_op jit(solution)/shard_map/ppermute | solution.py:32
  53.1 1.9 %all-to-all-done.1.mid_ref = bf16[8,96,512]{2,1,0:T(8,128)(2,1)S(1)} async-done(((bf16[8,96,512]{2,1,0:T(8,128)(2,1)}), bf16[8,96,512]{2,1,0:T(8,128)(2,1)S(1)}, u32[]{:S(2)}, u32[]{:S(2)}) %all-to-all-start.1) | async-done | bytes 786464 | tf_op jit(solution)/shard_map/all_to_all | solution.py:434
  55.0 1.0 %lower_taps.1.taps_ref = bf16[512,1024]{1,0:T(8,128)(2,1)S(1)} custom-call(s32[3]{0:T(128)S(1)} %pad_add_fusion.pos_ref, bf16[8,96,512]{2,1,0:T(8,128)(2,1)S(1)} %all-to-all-done.1.mid_ref, f32[96,1024]{1,0:T(8,128)S(1)} %fusion.6.slope_ref, f32[96,256]{1,0:T(8,128)S(1)} %copy-done.4), custom_call_target="tpu_custom_call" | custom-call | tf_op jit(solution)/shard_map/lower_taps/pallas_call | solution.py:456
  56.0 1.6 %weight_grad.3 = (f32[4,4,24,512]{3,2,1,0:T(8,128)S(1)}, bf16[4,4,24,512]{3,2,1,0:T(8,128)(2,1)S(1)}) custom-call(s32[3]{0:T(128)S(1)} %pad_add_fusion.pos_ref, bf16[640,1024]{1,0:T(8,128)(2,1)S(1)} %bitcast.17, bf16[512,1024]{1,0:T(8,128)(2,1)S(1)} %lower_taps.1.taps_ref), custom_call_target="tpu_custom_call" | custom-call | tf_op jit(solution)/shard_map/weight_grad/pallas_call | solution.py:371
  57.6 0.1 collective-permute-start.8
  57.7 1.4 %lower_weight.1.w_ref = bf16[640,512]{1,0:T(8,128)(2,1)S(1)} custom-call(s32[3]{0:T(128)S(1)} %pad_add_fusion.pos_ref, bf16[16,24,512]{2,1,0:T(8,128)(2,1)S(1)} %join.1.own_ref, bf16[16,24,512]{2,1,0:T(8,128)(2,1)} %collective-permute-done.15.other_ref), custom_call_target="tpu_custom_call" | custom-call | tf_op jit(solution)/shard_map/lower_weight/pallas_call | solution.py:445
  59.1 1.9 %low.1 = bf16[8,80,1024]{2,1,0:T(8,128)(2,1)} custom-call(bf16[512,1024]{1,0:T(8,128)(2,1)S(1)} %lower_taps.1.taps_ref, bf16[640,512]{1,0:T(8,128)(2,1)S(1)} %lower_weight.1.w_ref), custom_call_target="tpu_custom_call" | custom-call | tf_op jit(solution)/shard_map/low/pallas_call | solution.py:468
  61.0 3.7 %all-to-all-start.2 = ((bf16[8,80,1024]{2,1,0:T(8,128)(2,1)}), bf16[8,80,1024]{2,1,0:T(8,128)(2,1)S(1)}, u32[]{:S(2)}, u32[]{:S(2)}) async-start(bf16[8,80,1024]{2,1,0:T(8,128)(2,1)} %low.1), calls=%async_computation.2 | async-start | bytes 2621440 | tf_op jit(solution)/shard_map/all_to_all | solution.py:478
  64.8 1.1 %core_sum.1 = (f32[4,48,512]{2,1,0:T(8,128)S(1)}, bf16[4,48,512]{2,1,0:T(8,128)(2,1)S(1)}, bf16[4,48,512]{2,1,0:T(8,128)(2,1)S(1)}, bf16[4,48,512]{2,1,0:T(8,128)(2,1)S(1)}) custom-call(f32[4,4,24,512]{3,2,1,0:T(8,128)S(1)} %copy-done.1, bf16[4,4,24,512]{3,2,1,0:T(8,128)(2,1)} %collective-permute-done.7.got_upper_hbm, f32[4,4,24,512]{3,2,1,0:T(8,128)S(1)} %copy-done.3, ...), custom_call_target="tpu_custom_call" | custom-call | tf_op jit(solution)/shard_map/core_sum/pallas_call | solution.py:112
  65.8 2.4 %collective-permute-start.9 = (bf16[4,48,512]{2,1,0:T(8,128)(2,1)S(1)}, bf16[4,48,512]{2,1,0:T(8,128)(2,1)S(1)}, u32[]{:S(2)}, u32[]{:S(2)}) collective-permute-start(bf16[4,48,512]{2,1,0:T(8,128)(2,1)S(1)} %get-tuple-element.79), channel_id=1, source_target_pairs={{0,4},{2,6},{4,0},{6,2},{1,5},{3,7},{5,1},{7,3},{8,12},{10,14},{12... | collective-permute-start | bytes 589832 | tf_op jit(solution)/shard_map/ppermute | solution.py:32
  68.2 0.8 collective-permute-start.10
  69.0 1.2 %collective-permute-start.11 = (bf16[4,48,512]{2,1,0:T(8,128)(2,1)S(1)}, bf16[4,48,512]{2,1,0:T(8,128)(2,1)S(1)}, u32[]{:S(2)}, u32[]{:S(2)}) collective-permute-start(bf16[4,48,512]{2,1,0:T(8,128)(2,1)S(1)} %get-tuple-element.81), channel_id=1, source_target_pairs={{0,6},{2,0},{4,2},{6,4},{1,7},{3,1},{5,3},{7,5},{8,14},{10,8},{12,... | collective-permute-start | bytes 589832 | tf_op jit(solution)/shard_map/ppermute | solution.py:32
  70.3 5.1 %collective-permute-done.9.refs_0_ = bf16[4,48,512]{2,1,0:T(8,128)(2,1)S(1)} collective-permute-done((bf16[4,48,512]{2,1,0:T(8,128)(2,1)S(1)}, bf16[4,48,512]{2,1,0:T(8,128)(2,1)S(1)}, u32[]{:S(2)}, u32[]{:S(2)}) %collective-permute-start.9) | collective-permute-done | bytes 196640 | tf_op jit(solution)/shard_map/ppermute | solution.py:32
  75.4 3.5 %collective-permute-done.10.refs_1_ = bf16[4,48,512]{2,1,0:T(8,128)(2,1)S(1)} collective-permute-done((bf16[4,48,512]{2,1,0:T(8,128)(2,1)S(1)}, bf16[4,48,512]{2,1,0:T(8,128)(2,1)S(1)}, u32[]{:S(2)}, u32[]{:S(2)}) %collective-permute-start.10) | collective-permute-done | bytes 196640 | tf_op jit(solution)/shard_map/ppermute | solution.py:32
  78.8 0.1 collective-permute-done.11.refs_2_
  79.0 0.1 y_sum.1
  79.0 1.1 %collective-permute-start.12 = (bf16[48,512]{1,0:T(8,128)(2,1)S(1)}, bf16[48,512]{1,0:T(8,128)(2,1)S(1)}, u32[]{:S(2)}, u32[]{:S(2)}) collective-permute-start(bf16[48,512]{1,0:T(8,128)(2,1)S(1)} %get-tuple-element.82), channel_id=1, source_target_pairs={{0,8},{8,16},{16,24},{24,0},{1,9},{9,17},{17,25},{25,1},{2,10},{10... | collective-permute-start | bytes 147464 | tf_op jit(solution)/shard_map/ppermute | solution.py:32
  80.2 3.0 %collective-permute-start.13 = (bf16[48,512]{1,0:T(8,128)(2,1)S(1)}, bf16[48,512]{1,0:T(8,128)(2,1)S(1)}, u32[]{:S(2)}, u32[]{:S(2)}) collective-permute-start(bf16[48,512]{1,0:T(8,128)(2,1)S(1)} %get-tuple-element.83), channel_id=1, source_target_pairs={{0,16},{8,24},{16,0},{24,8},{1,17},{9,25},{17,1},{25,9},{2,18},{10... | collective-permute-start | bytes 147464 | tf_op jit(solution)/shard_map/ppermute | solution.py:32
  83.2 1.8 %collective-permute-start.14 = (bf16[48,512]{1,0:T(8,128)(2,1)S(1)}, bf16[48,512]{1,0:T(8,128)(2,1)S(1)}, u32[]{:S(2)}, u32[]{:S(2)}) collective-permute-start(bf16[48,512]{1,0:T(8,128)(2,1)S(1)} %get-tuple-element.84), channel_id=1, source_target_pairs={{0,24},{8,0},{16,8},{24,16},{1,25},{9,1},{17,9},{25,17},{2,26},{10... | collective-permute-start | bytes 147464 | tf_op jit(solution)/shard_map/ppermute | solution.py:32
  84.9 0.8 low_total.1
  85.8 0.4 collective-permute-done.12.refs_0_
  86.1 2.1 %collective-permute-done.13.refs_1_ = bf16[48,512]{1,0:T(8,128)(2,1)S(1)} collective-permute-done((bf16[48,512]{1,0:T(8,128)(2,1)S(1)}, bf16[48,512]{1,0:T(8,128)(2,1)S(1)}, u32[]{:S(2)}, u32[]{:S(2)}) %collective-permute-start.13) | collective-permute-done | bytes 49184 | tf_op jit(solution)/shard_map/ppermute | solution.py:32
  88.2 2.5 %collective-permute-done.14.refs_2_ = bf16[48,512]{1,0:T(8,128)(2,1)S(1)} collective-permute-done((bf16[48,512]{1,0:T(8,128)(2,1)S(1)}, bf16[48,512]{1,0:T(8,128)(2,1)S(1)}, u32[]{:S(2)}, u32[]{:S(2)}) %collective-permute-start.14) | collective-permute-done | bytes 49184 | tf_op jit(solution)/shard_map/ppermute | solution.py:32
  90.7 0.9 %z_sum.1 = (f32[5,22,96]{2,1,0:T(8,128)}, f32[5,20,88]{2,1,0:T(8,128)}) custom-call(f32[48,512]{1,0:T(8,128)S(1)} %get-tuple-element.89.own_ref, bf16[48,512]{1,0:T(8,128)(2,1)S(1)} %collective-permute-done.12.refs_0_, bf16[48,512]{1,0:T(8,128)(2,1)S(1)} %collective-permute-done.13.refs_1_, bf16[48,512]{1,0:T(8,128)(2,1)S(1)} %collective-permute-done.14.refs_2_), custom_call_target="tpu_custom_call" | custom-call | tf_op jit(solution)/shard_map/z_sum/pallas_call | solution.py:98
  (23 shorter events, 0.1 us)
Async XLA Ops:
  0.6 23.2 %copy-start.5 = (bf16[1024,88]{0,1:T(8,128)(2,1)S(1)}, bf16[1024,88]{0,1:T(8,128)(2,1)}, u32[]{:S(2)}) copy-start(bf16[1024,88]{0,1:T(8,128)(2,1)} %param.11) | copy-start | bytes 540676
  0.6 23.5 %copy-start.6 = (bf16[512,96]{0,1:T(8,128)(2,1)S(1)}, bf16[512,96]{0,1:T(8,128)(2,1)}, u32[]{:S(2)}) copy-start(bf16[512,96]{0,1:T(8,128)(2,1)} %param.9) | copy-start | bytes 294916
  2.8 29.9 %all-to-all-start = ((bf16[16,32,512]{2,1,0:T(8,128)(2,1)}), bf16[16,32,512]{2,1,0:T(8,128)(2,1)S(1)}, u32[]{:S(2)}, u32[]{:S(2)}) async-start(bf16[16,32,512]{2,1,0:T(8,128)(2,1)} %get-tuple-element.49), calls=%async_computation | async-start | bytes 1048576 | tf_op jit(solution)/shard_map/all_to_all | solution.py:410
  14.3 15.0 %collective-permute-start = (bf16[24,512]{1,0:T(8,128)(2,1)S(1)}, bf16[24,512]{1,0:T(8,128)(2,1)S(1)}, u32[]{:S(2)}, u32[]{:S(2)}) collective-permute-start(bf16[24,512]{1,0:T(8,128)(2,1)S(1)} %get-tuple-element.60), channel_id=1, source_target_pairs={{0,8},{8,16},{16,24},{24,0},{1,9},{9,17},{17,25},{25,1},{2,10},{10... | collective-permute-start | bytes 73736 | tf_op jit(solution)/shard_map/ppermute | solution.py:32
  16.7 16.0 %collective-permute-start.1 = (bf16[24,512]{1,0:T(8,128)(2,1)S(1)}, bf16[24,512]{1,0:T(8,128)(2,1)S(1)}, u32[]{:S(2)}, u32[]{:S(2)}) collective-permute-start(bf16[24,512]{1,0:T(8,128)(2,1)S(1)} %get-tuple-element.60), channel_id=1, source_target_pairs={{0,16},{8,24},{16,0},{24,8},{1,17},{9,25},{17,1},{25,9},{2,18},{10... | collective-permute-start | bytes 73736 | tf_op jit(solution)/shard_map/ppermute | solution.py:32
  20.3 12.4 %collective-permute-start.2 = (bf16[24,512]{1,0:T(8,128)(2,1)S(1)}, bf16[24,512]{1,0:T(8,128)(2,1)S(1)}, u32[]{:S(2)}, u32[]{:S(2)}) collective-permute-start(bf16[24,512]{1,0:T(8,128)(2,1)S(1)} %get-tuple-element.60), channel_id=1, source_target_pairs={{0,24},{8,0},{16,8},{24,16},{1,25},{9,1},{17,9},{25,17},{2,26},{10... | collective-permute-start | bytes 73736 | tf_op jit(solution)/shard_map/ppermute | solution.py:32
  32.7 1.9 %collective-permute-start.3 = (bf16[16,32,512]{2,1,0:T(8,128)(2,1)S(1)}, bf16[16,32,512]{2,1,0:T(8,128)(2,1)S(1)}, u32[]{:S(2)}, u32[]{:S(2)}) collective-permute-start(bf16[16,32,512]{2,1,0:T(8,128)(2,1)S(1)} %all-to-all-done.own_ref), channel_id=1, source_target_pairs={{0,1},{1,0},{2,3},{3,2},{4,5},{5,4},{6,7},{7,6},{8,9},{9,8},{10,11... | collective-permute-start | bytes 1572872 | tf_op jit(solution)/shard_map/ppermute | solution.py:32
  37.3 17.7 %all-to-all-start.1 = ((bf16[8,96,512]{2,1,0:T(8,128)(2,1)}), bf16[8,96,512]{2,1,0:T(8,128)(2,1)S(1)}, u32[]{:S(2)}, u32[]{:S(2)}) async-start(bf16[8,96,512]{2,1,0:T(8,128)(2,1)} %get-tuple-element.55), calls=%async_computation.1 | async-start | bytes 1572864 | tf_op jit(solution)/shard_map/all_to_all | solution.py:434
  41.8 13.2 %copy-start.4 = (f32[96,256]{1,0:T(8,128)S(1)}, f32[96,256]{1,0:T(8,128)}, u32[]{:S(2)}) copy-start(f32[96,256]{1,0:T(8,128)} %get-tuple-element.75.edge_ref) | copy-start | bytes 294916
  41.9 8.1 %collective-permute-start.4 = (bf16[4,24,512]{2,1,0:T(8,128)(2,1)S(1)}, bf16[4,24,512]{2,1,0:T(8,128)(2,1)S(1)}, u32[]{:S(2)}, u32[]{:S(2)}) collective-permute-start(bf16[4,24,512]{2,1,0:T(8,128)(2,1)S(1)} %pad_maximum_fusion.refs_0_), channel_id=1, source_target_pairs={{0,2},{2,4},{4,6},{6,0},{1,3},{3,5},{5,7},{7,1},{8,10},{10,12},{12... | collective-permute-start | bytes 294920 | tf_op jit(solution)/shard_map/ppermute | solution.py:32
  43.2 6.9 %collective-permute-start.5 = (bf16[4,24,512]{2,1,0:T(8,128)(2,1)S(1)}, bf16[4,24,512]{2,1,0:T(8,128)(2,1)S(1)}, u32[]{:S(2)}, u32[]{:S(2)}) collective-permute-start(bf16[4,24,512]{2,1,0:T(8,128)(2,1)S(1)} %pad_maximum_fusion.refs_0_), channel_id=1, source_target_pairs={{0,4},{2,6},{4,0},{6,2},{1,5},{3,7},{5,1},{7,3},{8,12},{10,14},{12... | collective-permute-start | bytes 294920 | tf_op jit(solution)/shard_map/ppermute | solution.py:32
  45.5 5.7 %collective-permute-start.6 = (bf16[4,24,512]{2,1,0:T(8,128)(2,1)S(1)}, bf16[4,24,512]{2,1,0:T(8,128)(2,1)S(1)}, u32[]{:S(2)}, u32[]{:S(2)}) collective-permute-start(bf16[4,24,512]{2,1,0:T(8,128)(2,1)S(1)} %pad_maximum_fusion.refs_0_), channel_id=1, source_target_pairs={{0,6},{2,0},{4,2},{6,4},{1,7},{3,1},{5,3},{7,5},{8,14},{10,8},{12,... | collective-permute-start | bytes 294920 | tf_op jit(solution)/shard_map/ppermute | solution.py:32
  49.0 0.9 copy-start
  51.2 1.9 %collective-permute-start.7 = (bf16[4,4,24,512]{3,2,1,0:T(8,128)(2,1)S(1)}, bf16[4,4,24,512]{3,2,1,0:T(8,128)(2,1)}, u32[]{:S(2)}, u32[]{:S(2)}) collective-permute-start(bf16[4,4,24,512]{3,2,1,0:T(8,128)(2,1)S(1)} %get-tuple-element.70), channel_id=1, source_target_pairs={{0,1},{1,0},{2,3},{3,2},{4,5},{5,4},{6,7},{7,6},{8,9},{9,8},{10,11... | collective-permute-start | bytes 1179656 | tf_op jit(solution)/shard_map/ppermute | solution.py:32
  51.3 6.4 %collective-permute-start.15 = (bf16[16,24,512]{2,1,0:T(8,128)(2,1)S(1)}, bf16[16,24,512]{2,1,0:T(8,128)(2,1)}, u32[]{:S(2)}, u32[]{:S(2)}) collective-permute-start(bf16[16,24,512]{2,1,0:T(8,128)(2,1)S(1)} %join.1.own_ref), channel_id=1, source_target_pairs={{0,1},{1,0},{2,3},{3,2},{4,5},{5,4},{6,7},{7,6},{8,9},{9,8},{10,11... | collective-permute-start | bytes 1179656 | tf_op jit(solution)/shard_map/ppermute | solution.py:32
  57.6 1.5 %copy-start.2 = (f32[4,4,24,512]{3,2,1,0:T(8,128)}, f32[4,4,24,512]{3,2,1,0:T(8,128)S(1)}, u32[]{:S(2)}) copy-start(f32[4,4,24,512]{3,2,1,0:T(8,128)S(1)} %get-tuple-element.76.keep_lower_ref) | copy-start | bytes 2359300
  57.6 3.4 %collective-permute-start.8 = (bf16[4,4,24,512]{3,2,1,0:T(8,128)(2,1)S(1)}, bf16[4,4,24,512]{3,2,1,0:T(8,128)(2,1)S(1)}, u32[]{:S(2)}, u32[]{:S(2)}) collective-permute-start(bf16[4,4,24,512]{3,2,1,0:T(8,128)(2,1)S(1)} %get-tuple-element.77), channel_id=1, source_target_pairs={{0,1},{1,0},{2,3},{3,2},{4,5},{5,4},{6,7},{7,6},{8,9},{9,8},{10,11... | collective-permute-start | bytes 1179656 | tf_op jit(solution)/shard_map/ppermute | solution.py:32
  61.0 3.8 %copy-start.1 = (f32[4,4,24,512]{3,2,1,0:T(8,128)S(1)}, f32[4,4,24,512]{3,2,1,0:T(8,128)}, u32[]{:S(2)}) copy-start(f32[4,4,24,512]{3,2,1,0:T(8,128)} %copy-done) | copy-start | bytes 2359300
  61.0 3.8 %copy-start.3 = (f32[4,4,24,512]{3,2,1,0:T(8,128)S(1)}, f32[4,4,24,512]{3,2,1,0:T(8,128)}, u32[]{:S(2)}) copy-start(f32[4,4,24,512]{3,2,1,0:T(8,128)} %copy-done.2) | copy-start | bytes 2359300
  61.0 23.9 %all-to-all-start.2 = ((bf16[8,80,1024]{2,1,0:T(8,128)(2,1)}), bf16[8,80,1024]{2,1,0:T(8,128)(2,1)S(1)}, u32[]{:S(2)}, u32[]{:S(2)}) async-start(bf16[8,80,1024]{2,1,0:T(8,128)(2,1)} %low.1), calls=%async_computation.2 | async-start | bytes 2621440 | tf_op jit(solution)/shard_map/all_to_all | solution.py:478
  65.8 9.5 %collective-permute-start.9 = (bf16[4,48,512]{2,1,0:T(8,128)(2,1)S(1)}, bf16[4,48,512]{2,1,0:T(8,128)(2,1)S(1)}, u32[]{:S(2)}, u32[]{:S(2)}) collective-permute-start(bf16[4,48,512]{2,1,0:T(8,128)(2,1)S(1)} %get-tuple-element.79), channel_id=1, source_target_pairs={{0,4},{2,6},{4,0},{6,2},{1,5},{3,7},{5,1},{7,3},{8,12},{10,14},{12... | collective-permute-start | bytes 589832 | tf_op jit(solution)/shard_map/ppermute | solution.py:32
  68.2 10.6 %collective-permute-start.10 = (bf16[4,48,512]{2,1,0:T(8,128)(2,1)S(1)}, bf16[4,48,512]{2,1,0:T(8,128)(2,1)S(1)}, u32[]{:S(2)}, u32[]{:S(2)}) collective-permute-start(bf16[4,48,512]{2,1,0:T(8,128)(2,1)S(1)} %get-tuple-element.80), channel_id=1, source_target_pairs={{0,2},{2,4},{4,6},{6,0},{1,3},{3,5},{5,7},{7,1},{8,10},{10,12},{12... | collective-permute-start | bytes 589832 | tf_op jit(solution)/shard_map/ppermute | solution.py:32
  69.0 9.9 %collective-permute-start.11 = (bf16[4,48,512]{2,1,0:T(8,128)(2,1)S(1)}, bf16[4,48,512]{2,1,0:T(8,128)(2,1)S(1)}, u32[]{:S(2)}, u32[]{:S(2)}) collective-permute-start(bf16[4,48,512]{2,1,0:T(8,128)(2,1)S(1)} %get-tuple-element.81), channel_id=1, source_target_pairs={{0,6},{2,0},{4,2},{6,4},{1,7},{3,1},{5,3},{7,5},{8,14},{10,8},{12,... | collective-permute-start | bytes 589832 | tf_op jit(solution)/shard_map/ppermute | solution.py:32
  79.0 7.1 %collective-permute-start.12 = (bf16[48,512]{1,0:T(8,128)(2,1)S(1)}, bf16[48,512]{1,0:T(8,128)(2,1)S(1)}, u32[]{:S(2)}, u32[]{:S(2)}) collective-permute-start(bf16[48,512]{1,0:T(8,128)(2,1)S(1)} %get-tuple-element.82), channel_id=1, source_target_pairs={{0,8},{8,16},{16,24},{24,0},{1,9},{9,17},{17,25},{25,1},{2,10},{10... | collective-permute-start | bytes 147464 | tf_op jit(solution)/shard_map/ppermute | solution.py:32
  80.2 8.0 %collective-permute-start.13 = (bf16[48,512]{1,0:T(8,128)(2,1)S(1)}, bf16[48,512]{1,0:T(8,128)(2,1)S(1)}, u32[]{:S(2)}, u32[]{:S(2)}) collective-permute-start(bf16[48,512]{1,0:T(8,128)(2,1)S(1)} %get-tuple-element.83), channel_id=1, source_target_pairs={{0,16},{8,24},{16,0},{24,8},{1,17},{9,25},{17,1},{25,9},{2,18},{10... | collective-permute-start | bytes 147464 | tf_op jit(solution)/shard_map/ppermute | solution.py:32
  83.2 7.5 %collective-permute-start.14 = (bf16[48,512]{1,0:T(8,128)(2,1)S(1)}, bf16[48,512]{1,0:T(8,128)(2,1)S(1)}, u32[]{:S(2)}, u32[]{:S(2)}) collective-permute-start(bf16[48,512]{1,0:T(8,128)(2,1)S(1)} %get-tuple-element.84), channel_id=1, source_target_pairs={{0,24},{8,0},{16,8},{24,16},{1,25},{9,1},{17,9},{25,17},{2,26},{10... | collective-permute-start | bytes 147464 | tf_op jit(solution)/shard_map/ppermute | solution.py:32
